TPU v7x, 512 devices: a whole 4x8x8 slice. The times are simulated.
512 devices in a mesh: pair: 16 (over x, y_lo), aux: 32 (over y_hi, z, core).
Axes of the slice: x: 4, y: 8 (y_hi: 2, y_lo: 4; y = y_hi * 4 + y_lo), z: 8, core: 2. Of those that a mesh axis runs over, the one named last changes fastest.
Arguments:
- amplitudes: bfloat16 [16, 512, 512], P('pair', 'aux'), may hold values from -6 to 6
- factors: bfloat16 [4096, 512, 512], P('aux', 'pair'), may hold values from -0.03125 to 0.03125
- hole_weights: float32 [16, 16], replicated, may hold values from -1.5 to 1.5
- driver: float32 [16, 6, 512], P('pair', None, 'aux'), may hold values from -6 to 6
- eps_vir: float32 [512], replicated, may hold values from 0.5 to 3
- pair_energy: float32 [16], P('pair'), may hold values from -3 to -0.5
Outputs:
- residual: float32 [16, 6, 512], P('pair', None, 'aux')
- new_amps: float32 [16, 6, 512], P('pair', None, 'aux')
All inputs are finite; a program needn't handle non-finite values.
Results may differ from a plain program's by a relative error of at most 0.0003.
Values may be sent and summed in bfloat16 or wider, within the bound.
No kernel may reach another device: no remote copies, remote signals or barrier semaphores. Data moves between devices by JAX's collectives and lax.ppermute only.
A program may use at most 64 MiB of HBM per device.

v0:
```python
import jax
import jax.numpy as jnp
from jax import lax
from jax.sharding import Mesh
from jax.sharding import PartitionSpec as P

PAIR = ("pair_0", "pair_1")


def sent_to_all(array, axis):
    count = lax.axis_size(axis)
    return lax.all_to_all(
        jnp.broadcast_to(array[None], (count, *array.shape)), axis, 0, 0, tiled=True
    )


def in_order(tiles, dim):
    tiles = jnp.moveaxis(tiles, 0, dim)
    shape = tiles.shape
    return tiles.reshape(*shape[:dim], shape[dim] * shape[dim + 1], *shape[dim + 2 :])


def collect(array, axis, dim):
    tiles = sent_to_all(array, axis)
    return in_order(tiles, dim)


def spread(array, axes, root):
    array = jnp.where(lax.axis_index(axes) == root, array, jnp.zeros_like(array))
    for axis in axes:
        array = lax.psum(array, axis)
    return array


def cut_along(array, dim, count):
    before, after = (array.shape[:dim], array.shape[dim + 1 :])
    return jnp.moveaxis(array.reshape(*before, count, -1, *after), dim, 0)


def sent_and_summed(array, axis, dim):
    count = lax.axis_size(axis)
    tiles = lax.all_to_all(cut_along(array, dim, count), axis, 0, 0, tiled=True)
    return jnp.sum(tiles, axis=0)


def half_of(window, amp_pair):
    return jnp.einsum("qac,cd->aqd", window, amp_pair, preferred_element_type=jnp.float32).astype(
        jnp.bfloat16
    )


def contract(halves, factors):
    return jnp.einsum("aqd,qbd->ab", halves, factors, preferred_element_type=jnp.float32)


def per_device(amplitudes, factors, hole_weights, driver, eps_vir, pair_energy):
    window_rows = driver.shape[1]
    columns = driver.shape[2]
    amp_full = collect(amplitudes, "aux", 1)
    window = spread(factors[:, :window_rows, :], PAIR, 0)
    amp_window = amp_full[:, :window_rows, :]
    slab = lax.all_to_all(amp_window, PAIR, split_axis=2, concat_axis=0, tiled=True)

    def ladder_pair(amp_pair):
        return contract(half_of(window, amp_pair), factors)

    particle = lax.map(ladder_pair, lax.all_gather(amp_full, PAIR, axis=0, tiled=True))
    hole_term = jnp.einsum(
        "pk,kab->pab", hole_weights, slab.astype(jnp.float32), precision=lax.Precision.HIGHEST
    )
    aux_index = lax.axis_index("aux")
    partial_value = particle + jnp.where(aux_index == 0, hole_term, 0.0)
    returned = lax.all_to_all(partial_value, PAIR, split_axis=0, concat_axis=2, tiled=True)
    summed = sent_and_summed(returned, "aux", 2)
    residual = driver + summed
    column_start = aux_index * columns
    amp_cols = lax.dynamic_slice_in_dim(amp_window, column_start, columns, 2).astype(jnp.float32)
    eps_cols = lax.dynamic_slice_in_dim(eps_vir, column_start, columns, 0)
    denominator = (
        eps_vir[:window_rows][None, :, None] + eps_cols[None, None, :] - pair_energy[:, None, None]
    )
    new_amps = amp_cols - residual / denominator
    return (residual, new_amps)


def solution(mesh):
    finer = Mesh(mesh.devices.reshape(4, 4, mesh.shape["aux"]), ("pair_0", "pair_1", "aux"))
    in_specs = (P(PAIR, "aux", None), P("aux", PAIR, None), P(), P(PAIR, None, "aux"), P(), P(PAIR))
    out_specs = (P(PAIR, None, "aux"), P(PAIR, None, "aux"))
    return jax.shard_map(
        per_device, mesh=finer, in_specs=in_specs, out_specs=out_specs, check_vma=False
    )
```

profile of v0, /device:TPU:6, one launch (start us, length us, event | category | flops | bytes accessed | tf_op | source)
XLA Modules:
  0.0 423.6 jit_solution(4023504486053572570)
XLA Ops:
  11.7 16.0 %all-to-all-start = ((bf16[32,1,16,512]{3,2,1,0:T(8,128)(2,1)}), bf16[32,1,16,512]{3,2,1,0:T(8,128)(2,1)S(1)}, u32[]{:S(2)}, u32[]{:S(2)}) async-start(bf16[32,1,16,512]{3,2,1,0:T(8,128)(2,1)} %broadcast_in_dim.25), calls=%async_computation | async-start | bytes 1048576 | tf_op jit(solution)/shard_map/all_to_all | solution.py:12
  27.7 42.2 %all-reduce.3.cloned.1.call-done = bf16[128,6,512]{2,0,1:T(8,128)(2,1)} async-done(((bf16[128,6,512]{2,0,1:T(8,128)(2,1)}), bf16[128,6,512]{2,0,1:T(8,128)(2,1)}) %all-reduce.3.cloned.1.call-update) | async-done | bytes 786448 | tf_op jit(solution)/shard_map/psum | solution.py:31
  72.4 8.2 %all-to-all-start.1 = ((bf16[1,6,512]{1,0,2:T(2,128)(2,1)}), bf16[1,6,512]{1,0,2:T(2,128)(2,1)S(1)}, u32[]{:S(2)}, u32[]{:S(2)}) async-start(bf16[1,6,512]{1,0,2:T(2,128)(2,1)} %copy.39), calls=%async_computation.1 | async-start | bytes 524288 | tf_op jit(solution)/shard_map/all_to_all | solution.py:62
  80.6 9.1 %copy.38 = bf16[128,32,512]{0,1,2:T(8,128)(2,1)} copy(bf16[128,32,512]{2,1,0:T(8,128)(2,1)} %param.9) | data formatting | bytes 8388608 | tf_op jit(solution)/shard_map/while | solution.py:67
  90.0 113.3 %all-reduce.5.cloned.1.call-done = bf16[128,6,512]{2,0,1:T(8,128)(2,1)} async-done(((bf16[128,6,512]{2,0,1:T(8,128)(2,1)}), bf16[128,6,512]{2,0,1:T(8,128)(2,1)}) %all-reduce.5.cloned.1.call-update) | async-done | bytes 786448 | tf_op jit(solution)/shard_map/psum | solution.py:31
  203.3 82.8 %all-gather.2.cloned.1.call-done = bf16[16,512,512]{2,1,0:T(8,128)(2,1)} async-done(((bf16[1,512,512]{2,1,0:T(8,128)(2,1)}), bf16[16,512,512]{2,1,0:T(8,128)(2,1)}) %all-gather.2.cloned.1.call-update) | async-done | bytes 8388624 | tf_op jit(solution)/shard_map/all_gather | solution.py:67
  286.1 89.0 %while.11 = (s32[]{:T(128)}, f32[16,6,32]{2,0,1:T(8,128)S(1)}, bf16[16,512,512]{2,1,0:T(8,128)(2,1)}, bf16[128,6,512]{2,0,1:T(8,128)(2,1)}, bf16[128,32,512]{0,1,2:T(8,128)(2,1)}) while((s32[]{:T(128)}, f32[16,6,32]{2,0,1:T(8,128)S(1)}, bf16[16,512,512]{2,1,0:T(8,128)(2,1)}, bf16[128,6,512]{2,0,1:T(8,128)(2,1)}, ...), condition=%wide.region_3.4_spmd.clone, body=%wide.region_2.3_spmd.sunk.clone | while | flops 428212224 | bytes 7081805 | solution.py:67
  286.1 1.9 fusion.24
  288.1 3.6 convolution_bitcast_fusion.3
  291.7 1.9 fusion.24
  293.6 3.6 convolution_bitcast_fusion.3
  297.3 1.9 fusion.24
  299.2 3.6 convolution_bitcast_fusion.3
  304.7 3.6 convolution_bitcast_fusion.3
  310.3 3.6 convolution_bitcast_fusion.3
  315.9 3.6 convolution_bitcast_fusion.3
  321.4 3.6 convolution_bitcast_fusion.3
  327.0 3.6 convolution_bitcast_fusion.3
  332.5 3.6 convolution_bitcast_fusion.3
  336.2 1.9 fusion.24
  338.1 3.6 convolution_bitcast_fusion.3
  343.6 3.6 convolution_bitcast_fusion.3
  349.2 3.6 convolution_bitcast_fusion.3
  352.8 1.9 fusion.24
  354.8 3.6 convolution_bitcast_fusion.3
  360.3 3.6 convolution_bitcast_fusion.3
  365.9 3.6 convolution_bitcast_fusion.3
  369.5 1.9 fusion.24
  371.4 3.6 convolution_bitcast_fusion.3
  375.4 11.8 %all_to_all.43 = f32[16,1,192]{2,1,0:T(1,128)S(1)} all-to-all(f32[16,1,192]{2,1,0:T(1,128)S(1)} %reshape.71), channel_id=1, replica_groups=mesh['pair_0'=4,'pair_1'=4,'aux'=32] {'pair_0','pair_1'}, dimensions={0} | all-to-all | bytes 24576 | tf_op jit(solution)/shard_map/all_to_all | solution.py:73
  389.3 12.8 %all-to-all-start.3 = ((f32[32,1,6,16]{3,1,2,0:T(1,128)}), f32[32,1,6,16]{3,1,2,0:T(1,128)S(1)}, u32[]{:S(2)}, u32[]{:S(2)}) async-start(f32[32,1,6,16]{3,1,2,0:T(1,128)} %copy.44), calls=%async_computation.3 | async-start | bytes 196608 | tf_op jit(solution)/shard_map/all_to_all | solution.py:42
  402.9 11.9 %all-to-all-done.3 = f32[32,1,6,16]{3,1,2,0:T(1,128)S(1)} async-done(((f32[32,1,6,16]{3,1,2,0:T(1,128)}), f32[32,1,6,16]{3,1,2,0:T(1,128)S(1)}, u32[]{:S(2)}, u32[]{:S(2)}) %all-to-all-start.3) | async-done | bytes 12320 | tf_op jit(solution)/shard_map/all_to_all | solution.py:42
  (84 shorter events, 30.2 us)
Async XLA Ops:
  8.0 367.1 %copy-start = (f32[16,16]{1,0:T(8,128)S(1)}, f32[16,16]{1,0:T(8,128)}, u32[]{:S(2)}) copy-start(f32[16,16]{1,0:T(8,128)} %param.10) | copy-start | bytes 3076
  8.0 2.8 copy-start.2
  8.0 61.9 %all-reduce.3.cloned.1.call-start = ((), (), s32[]{:S(2)}) async-start(), calls=%async_computation.5 | async-start | bytes 1572864 | tf_op jit(solution)/shard_map/psum | solution.py:31
  11.7 58.3 %all-to-all-start = ((bf16[32,1,16,512]{3,2,1,0:T(8,128)(2,1)}), bf16[32,1,16,512]{3,2,1,0:T(8,128)(2,1)S(1)}, u32[]{:S(2)}, u32[]{:S(2)}) async-start(bf16[32,1,16,512]{3,2,1,0:T(8,128)(2,1)} %broadcast_in_dim.25), calls=%async_computation | async-start | bytes 1048576 | tf_op jit(solution)/shard_map/all_to_all | solution.py:12
  27.7 175.6 %all-reduce.5.cloned.1.call-start = ((), (), s32[]{:S(2)}) async-start(), calls=%async_computation.6 | async-start | bytes 1572864 | tf_op jit(solution)/shard_map/psum | solution.py:31
  70.0 216.2 %all-gather.2.cloned.1.call-start = ((), (), s32[]{:S(2)}) async-start(), calls=%async_computation.4 | async-start | bytes 8912896 | tf_op jit(solution)/shard_map/all_gather | solution.py:67
  70.0 0.8 copy-start.1
  72.4 17.3 %all-to-all-start.1 = ((bf16[1,6,512]{1,0,2:T(2,128)(2,1)}), bf16[1,6,512]{1,0,2:T(2,128)(2,1)S(1)}, u32[]{:S(2)}, u32[]{:S(2)}) async-start(bf16[1,6,512]{1,0,2:T(2,128)(2,1)} %copy.39), calls=%async_computation.1 | async-start | bytes 524288 | tf_op jit(solution)/shard_map/all_to_all | solution.py:62
  286.1 116.7 %copy-start.4 = (f32[512]{0:T(512)S(1)}, f32[512]{0:T(512)}, u32[]{:S(2)}) copy-start(f32[512]{0:T(512)} %param.12) | copy-start | bytes 6148
  286.1 128.8 %copy-start.3 = (f32[1,6,16]{2,0,1:T(1,128)S(1)}, f32[1,6,16]{2,0,1:T(1,128)}, u32[]{:S(2)}) copy-start(f32[1,6,16]{2,0,1:T(1,128)} %param.11) | copy-start | bytes 1156
  286.1 128.8 %slice-start = ((f32[512]{0:T(512)}), f32[6]{0:T(128)S(1)}, s32[]{:S(2)}) async-start(f32[512]{0:T(512)} %param.12), calls=%async_computation.7 | async-start | bytes 1024 | tf_op jit(solution)/shard_map/slice | solution.py:80
  389.3 25.5 %all-to-all-start.3 = ((f32[32,1,6,16]{3,1,2,0:T(1,128)}), f32[32,1,6,16]{3,1,2,0:T(1,128)S(1)}, u32[]{:S(2)}, u32[]{:S(2)}) async-start(f32[32,1,6,16]{3,1,2,0:T(1,128)} %copy.44), calls=%async_computation.3 | async-start | bytes 196608 | tf_op jit(solution)/shard_map/all_to_all | solution.py:42
Sparse Core Ops, SparseCore 0:
  11.2 58.6 all-reduce.2
  72.9 130.3 all-reduce.4
Sparse Core Ops, SparseCore 1:
  72.5 213.5 all-gather.1
where the time goes:
time: 427 us; the launch traced here: 424 us
  waiting for transfers between devices  250 us (59%)
  matrix products  87.7 us (21%)
  starting transfers between devices  37.1 us (9%)
  local copies, waits for them, and re-layouts  17.7 us (4%)
  between operations  16.3 us (4%)
  blocking collectives  11.8 us (3%)
    psum x2, waiting for transfers between devices, spread(): array = lax.psum(array, axis)  156 us
    all_gather x1, waiting for transfers between devices, per_device(): lax.all_gather(amp_full, PAIR, axis=0, tiled=True)  82.8 us
    dot_general x16, matrix products, contract(): jnp.einsum('aqd,qbd->ab', halves, factors, preferred_element_type=jnp.flo...  56.9 us
    dot_general x16, matrix products, half_of(): jnp.einsum('qac,cd->aqd', window, amp_pair, preferred_element_type=jnp.fl...  30.7 us
    all_to_all x1, starting transfers between devices, sent_to_all(): lax.all_to_all(jnp.broadcast_to(array[None], (count, *array.shape)), axis...  16 us
    all_to_all x1, starting transfers between devices, sent_and_summed(): tiles = lax.all_to_all(cut_along(array, dim, count), axis, 0, 0, tiled=True)  12.8 us
    all_to_all x1, waiting for transfers between devices, sent_and_summed(): tiles = lax.all_to_all(cut_along(array, dim, count), axis, 0, 0, tiled=True)  11.9 us
    all_to_all x1, blocking collectives, per_device(): lax.all_to_all(partial_value, PAIR, split_axis=0, concat_axis=2, tiled=True)  11.8 us
  transfers between devices with their start and end apart: 6, of which 4 were waited for; matrix products, arithmetic and copies ran while one was open for 3% of the time, Pallas kernels for 0%

commit v1 on v0

v1 whole, which is shorter than its diff:
```python
import jax
import jax.numpy as jnp
from jax import lax
from jax.experimental import pallas as pl
from jax.experimental.pallas import tpu as pltpu
from jax.sharding import Mesh
from jax.sharding import PartitionSpec as P

AXES = ("x", "ylo", "yhi", "z", "core")
PAIR = ("x", "ylo")
AUX = ("yhi", "z", "core")
Y = ("ylo", "yhi")
BF16 = jnp.bfloat16
F32 = jnp.float32
BLOCK_Q = 8


def shifted(array, axis, by):
    if axis == "x":
        count = lax.axis_size("x")
        return lax.ppermute(array, "x", [(i, (i + by) % count) for i in range(count)])
    lows, highs = lax.axis_size("ylo"), lax.axis_size("yhi")

    def index(y):
        return (y % lows) * highs + y // lows

    full = lows * highs
    return lax.ppermute(array, Y, [(index(y), index((y + by) % full)) for y in range(full)])


def ring(array, axis):
    behind, ahead = shifted(array, axis, 1), shifted(array, axis, -1)
    half = array.shape[0] // 2
    return behind, ahead, shifted(behind[:half], axis, 1), shifted(ahead[half:], axis, -1)


def swapped(array):
    return lax.ppermute(array, "core", [(0, 1), (1, 0)])


def window_of(factors, rows):
    parts = lax.axis_size("x")
    lows = lax.axis_size("ylo")
    wide = jnp.transpose(factors[:, :rows, :], (1, 0, 2))
    quarter = wide.shape[1] // parts
    pieces = [wide[:, i * quarter : (i + 1) * quarter, :] for i in range(parts)]
    x, ylo = lax.axis_index("x"), lax.axis_index("ylo")
    mine = jnp.where((x == 0) & (ylo == 0), pieces[0], jnp.zeros_like(pieces[0]))
    for i in range(1, parts):
        mine = mine + lax.ppermute(pieces[i], PAIR, [(0, i * lows)])
    spread = jnp.where(ylo == 0, mine, jnp.zeros_like(mine))
    for k in range(1, lows):
        spread = spread + lax.ppermute(mine, PAIR, [(i * lows, i * lows + k) for i in range(parts)])
    return lax.all_to_all(
        jnp.broadcast_to(spread[None], (parts, *spread.shape)), "x", 0, 0, tiled=True
    )


def ladder_kernel(scalars, f_own, f_other, w_own, w_other, *refs):
    amps, (out, head, halves) = refs[:-3], refs[-3:]
    rows = w_own.shape[1]
    per_piece = w_own.shape[2] // BLOCK_Q
    pieces = w_own.shape[0]
    blocks = pieces * per_piece
    depth = w_own.shape[3]
    columns = f_own.shape[2]
    span = rows * BLOCK_Q

    local = 0
    for chunk in amps:
        for k in range(chunk.shape[0]):
            amp = chunk[k]
            head[pl.ds(scalars[local], 1)] = amp[None, : head.shape[1], :]
            for which, w in enumerate((w_own, w_other)):
                for piece in range(pieces):
                    got = jnp.dot(
                        w[piece].reshape(rows * per_piece * BLOCK_Q, depth),
                        amp,
                        preferred_element_type=F32,
                    ).reshape(rows, per_piece, BLOCK_Q, columns)
                    for b in range(per_piece):
                        at = (which * blocks + piece * per_piece + b) * columns
                        halves[local * span : (local + 1) * span, at : at + columns] = (
                            got[:, b].reshape(span, columns).astype(BF16)
                        )
            local += 1
    total = None
    group = 8
    for which, f in enumerate((f_own, f_other)):
        for start in range(0, blocks, group):
            right = jnp.concatenate(
                [
                    f[(start + b) * BLOCK_Q : (start + b + 1) * BLOCK_Q].reshape(-1, columns)
                    for b in range(group)
                ],
                axis=1,
            )
            at = (which * blocks + start) * columns
            term = lax.dot_general(
                halves[:, at : at + group * columns],
                right,
                (((1,), (1,)), ((), ())),
                preferred_element_type=F32,
            )
            total = term if total is None else total + term
    width = f_own.shape[1]
    lanes = BLOCK_Q * width
    total = total.reshape(local * rows, BLOCK_Q, lanes)
    q = lax.broadcasted_iota(jnp.int32, total.shape, 1)
    lane = lax.broadcasted_iota(jnp.int32, total.shape, 2)
    folded = jnp.sum(jnp.where(lane // width == q, total, 0.0), axis=1)
    folded = folded[:, : lanes // 2] + folded[:, lanes // 2 :]
    folded = folded + pltpu.roll(folded, 64, 1)
    folded = folded + pltpu.roll(folded, 32, 1)
    for i in range(local):
        out[pl.ds(scalars[i], 1)] = folded[i * rows : (i + 1) * rows][None]


def per_device(amplitudes, factors, hole_weights, driver, eps_vir, pair_energy):
    pairs = hole_weights.shape[0]
    rows, columns = driver.shape[1], driver.shape[2]
    depth = factors.shape[2]
    half = depth // 2
    width = factors.shape[1]
    x, ylo, yhi, z, core = (lax.axis_index(name) for name in AXES)
    aux_index = lax.axis_index(AUX)
    pair_index = lax.axis_index(PAIR)
    xs, lows = lax.axis_size("x"), lax.axis_size("ylo")

    own = amplitudes[0]
    split = jnp.stack([own[:, :half], own[:, half:]])
    sent = jnp.tile(split[None], (lax.axis_size("yhi") * lax.axis_size("z"), 1, 1, 1))
    amp = lax.all_to_all(sent.reshape(-1, *split.shape[1:]), AUX, 0, 0, tiled=True)
    amp = amp.reshape(-1, half)

    f_other = swapped(lax.dynamic_slice_in_dim(factors, (1 - core) * half, half, 2))
    window = window_of(factors, rows)
    window_other = swapped(window)

    start = (aux_index * columns) % half
    here = lax.dynamic_slice_in_dim(amp[:rows], start, columns, 1)
    there = lax.dynamic_slice_in_dim(amp[:rows], (start + columns * (1 - 2 * core)) % half, columns, 1)
    amp_cols = jnp.where(core == yhi, here, swapped(there)).astype(F32)

    behind, ahead, first, last = ring(amp, "y")
    chunk = jnp.stack([amp, behind, ahead, jnp.concatenate([first, last])])
    amps = (chunk, *ring(chunk, "x"))
    offsets = (0, 1, -1, 2)
    places = [(i, k) for i in range(3) for k in range(4)] + [(3, k) for k in range(4)]
    order = jnp.stack(
        [((x - offsets[i]) % xs) * lows + (ylo - offsets[k]) % lows for i, k in places]
    ).astype(jnp.int32)
    scalars = jnp.concatenate([order, core[None].astype(jnp.int32)])

    head_rows = 16
    blocks = factors.shape[0] // BLOCK_Q
    span = rows * BLOCK_Q
    whole = pl.BlockSpec(memory_space=pltpu.VMEM)
    quarters = window.shape
    particle, head = pl.pallas_call(
        ladder_kernel,
        grid_spec=pltpu.PrefetchScalarGridSpec(
            num_scalar_prefetch=1,
            grid=(1,),
            in_specs=[
                pl.BlockSpec((factors.shape[0], width, half), lambda i, s: (0, 0, s[pairs])),
            ]
            + [whole] * (3 + len(amps)),
            out_specs=[whole, whole],
            scratch_shapes=[pltpu.VMEM((pairs * span, 2 * blocks * half), BF16)],
        ),
        out_shape=[
            jax.ShapeDtypeStruct((pairs, rows, 128), F32),
            jax.ShapeDtypeStruct((pairs, head_rows, half), BF16),
        ],
        compiler_params=pltpu.CompilerParams(vmem_limit_bytes=56 * 1024 * 1024),
        cost_estimate=pl.CostEstimate(
            flops=9_700_000_000, bytes_accessed=12_000_000, transcendentals=0
        ),
    )(scalars, factors, f_other, window, window_other, *amps)
    particle = particle[:, :, :width]

    place = (pair_index * width) % half
    near = lax.dynamic_slice_in_dim(head[:, :rows, :], place, width, 2).astype(F32)
    hole_term = jnp.einsum("pk,kab->pab", hole_weights, near, precision=lax.Precision.HIGHEST)
    chosen = (yhi == 0) & (z == 0) & (core == (pair_index * width) // half)
    partial_value = particle + jnp.where(chosen, hole_term, 0.0)

    tiles = partial_value.reshape(pairs, rows, width // columns, columns)
    tiles = jnp.transpose(tiles, (0, 2, 1, 3)).reshape(-1, 1, rows * columns)
    summed = jnp.sum(lax.all_to_all(tiles, AUX, 0, 0, tiled=True), axis=0)
    count = lax.axis_size(AUX)
    halves = width // columns
    moves = []
    for g in range(pairs):
        for j in range(count):
            moves.append((g * count + j, (j // halves) * count + halves * g + j % halves))
    summed = lax.ppermute(summed, AXES, moves).reshape(1, rows, columns)

    residual = driver + summed
    eps_cols = lax.dynamic_slice_in_dim(eps_vir, aux_index * columns, columns, 0)
    denominator = (
        eps_vir[:rows][None, :, None] + eps_cols[None, None, :] - pair_energy[:, None, None]
    )
    new_amps = amp_cols[None] - residual / denominator
    return (residual, new_amps)


def solution(mesh):
    finer = Mesh(mesh.devices.reshape(4, 4, 2, 8, 2), AXES)
    in_specs = (P(PAIR, AUX, None), P(AUX, PAIR, None), P(), P(PAIR, None, AUX), P(), P(PAIR))
    out_specs = (P(PAIR, None, AUX), P(PAIR, None, AUX))
    return jax.shard_map(
        per_device, mesh=finer, in_specs=in_specs, out_specs=out_specs, check_vma=False
    )
```

time: 427 us -> 188 us (0.44)
  waiting for transfers between devices: 250 us -> 56.8 us
  matrix products: 87.7 us -> 0.14 us
  starting transfers between devices: 37.1 us -> 67 us
  blocking collectives: 11.8 us -> 27.4 us
  Pallas kernels: 0 us -> 15.3 us
  between operations: 16.3 us -> 1.86 us
    psum x2 -> x0, waiting for transfers between devices: 156 us -> none  [spread(): array = lax.psum(array, axis)]
    dot_general x33 -> x1, matrix products: 87.7 us -> 0.14 us  [per_device(): jnp.einsum('pk,kab->pab', hole_weights, near, precision=lax.Precision.HIG...]
    all_gather x1 -> x0, waiting for transfers between devices: 82.8 us -> none  [per_device(): lax.all_gather(amp_full, PAIR, axis=0, tiled=True)]
    ppermute x0 -> x18, starting transfers between devices: none -> 44 us  [the longest x4 13.1 us: shifted(): lax.ppermute(array, Y, [(index(y), index((y + by) % full)) for y in range...]
    ppermute x0 -> x18, waiting for transfers between devices: none -> 32.1 us  [the longest x4 13 us: shifted(): lax.ppermute(array, 'x', [(i, (i + by) % count) for i in range(count)])]
    all_to_all x1, blocking collectives: 11.8 us -> 27.4 us  [window_of(): lax.all_to_all(jnp.broadcast_to(spread[None], (parts, *spread.shape)), 'x...]
    pallas_call x0 -> x1, Pallas kernels: none -> 15.3 us  [per_device(): pl.pallas_call(ladder_kernel, grid_spec=pltpu.PrefetchScalarGridSpec(num_...]
    all_to_all x3 -> x2, starting transfers between devices: 37 us -> 22.9 us  [the longest x1 16 us: per_device(): lax.all_to_all(sent.reshape(-1, *split.shape[1:]), AUX, 0, 0, tiled=True)]
  transfers between devices with their start and end apart: 6 -> 20, of which waited for: 4 -> 7; matrix products, arithmetic and copies ran while one was open for 3% -> 7% of each run, Pallas kernels for 0% -> 0%
where the time goes in v1:
time: 188 us; the launch traced here: 187 us
  starting transfers between devices  67 us (36%)
  waiting for transfers between devices  56.8 us (30%)
  blocking collectives  27.4 us (15%)
  Pallas kernels  15.3 us (8%)
  local copies, waits for them, and re-layouts  14.1 us (8%)
  other arithmetic  4.11 us (2%)
    all_to_all x1, blocking collectives, window_of(): lax.all_to_all(jnp.broadcast_to(spread[None], (parts, *spread.shape)), 'x...  27.4 us
    all_to_all x1, starting transfers between devices, per_device(): lax.all_to_all(sent.reshape(-1, *split.shape[1:]), AUX, 0, 0, tiled=True)  16 us
    pallas_call x1, Pallas kernels, per_device(): pl.pallas_call(ladder_kernel, grid_spec=pltpu.PrefetchScalarGridSpec(num_...  15.3 us
    all_to_all x1, waiting for transfers between devices, per_device(): lax.all_to_all(sent.reshape(-1, *split.shape[1:]), AUX, 0, 0, tiled=True)  13.3 us
    ppermute x4, starting transfers between devices, shifted(): lax.ppermute(array, Y, [(index(y), index((y + by) % full)) for y in range...  13.1 us
    ppermute x4, waiting for transfers between devices, shifted(): lax.ppermute(array, 'x', [(i, (i + by) % count) for i in range(count)])  13 us
    ppermute x1, waiting for transfers between devices, per_device(): summed = lax.ppermute(summed, AXES, moves).reshape(1, rows, columns)  12.3 us
    ppermute x4, starting transfers between devices, shifted(): lax.ppermute(array, 'x', [(i, (i + by) % count) for i in range(count)])  12 us
  transfers between devices with their start and end apart: 20, of which 7 were waited for; matrix products, arithmetic and copies ran while one was open for 7% of the time, Pallas kernels for 0%

profile of v1, /device:TPU:6, one launch (start us, length us, event | category | flops | bytes accessed | tf_op | source)
XLA Modules:
  0.0 186.7 jit_solution(9212152848591449440)
XLA Ops:
  2.1 16.0 %all-to-all-start.1 = ((bf16[32,16,256]{2,1,0:T(8,128)(2,1)}), bf16[32,16,256]{2,1,0:T(8,128)(2,1)S(1)}, u32[]{:S(2)}, u32[]{:S(2)}) async-start(bf16[32,16,256]{2,1,0:T(8,128)(2,1)} %bitcast.21), calls=%async_computation.1 | async-start | bytes 524288 | tf_op jit(solution)/shard_map/all_to_all | solution.py:133
  18.1 1.3 slice_bitcast_fusion
  19.4 13.3 %all-to-all-done.1 = bf16[32,16,256]{2,1,0:T(8,128)(2,1)S(1)} async-done(((bf16[32,16,256]{2,1,0:T(8,128)(2,1)}), bf16[32,16,256]{2,1,0:T(8,128)(2,1)S(1)}, u32[]{:S(2)}, u32[]{:S(2)}) %all-to-all-start.1) | async-done | bytes 262176 | tf_op jit(solution)/shard_map/all_to_all | solution.py:133
  32.7 1.9 %collective-permute-start.9 = (bf16[512,256]{1,0:T(8,128)(2,1)S(1)}, bf16[512,256]{1,0:T(8,128)(2,1)}, u32[]{:S(2)}, u32[]{:S(2)}) collective-permute-start(bf16[512,256]{1,0:T(8,128)(2,1)S(1)} %bitcast.46), channel_id=1, source_target_pairs={{0,112},{32,0},{64,32},{96,64},{16,96},{48,16},{80,48},{112,80},{1... | collective-permute-start | bytes 786440 | tf_op jit(solution)/shard_map/ppermute | solution.py:28
  34.6 5.3 %collective-permute-start.8 = (bf16[512,256]{1,0:T(8,128)(2,1)S(1)}, bf16[512,256]{1,0:T(8,128)(2,1)}, u32[]{:S(2)}, u32[]{:S(2)}) collective-permute-start(bf16[512,256]{1,0:T(8,128)(2,1)S(1)} %bitcast.47), channel_id=1, source_target_pairs={{0,32},{32,64},{64,96},{96,16},{16,48},{48,80},{80,112},{112,0},{1... | collective-permute-start | bytes 786440 | tf_op jit(solution)/shard_map/ppermute | solution.py:28
  40.8 1.3 collective-permute-start.3
  42.1 1.4 collective-permute-start.2
  43.5 1.4 collective-permute-start.1
  44.8 1.8 constant_dynamic-slice_fusion.2
  46.6 1.9 %collective-permute-start = (bf16[128,32,256]{2,1,0:T(8,128)(2,1)S(1)}, bf16[128,32,256]{2,1,0:T(8,128)(2,1)}, u32[]{:S(2)}, u32[]{:S(2)}) collective-permute-start(bf16[128,32,256]{2,1,0:T(8,128)(2,1)S(1)} %constant_dynamic-slice_fusion.2), channel_id=1, source_target_pairs={{0,1},{1,0},{2,3},{3,2},{4,5},{5,4},{6,7},{7,6},{8,9},{9,8},{10,11... | collective-permute-start | bytes 6291464 | tf_op jit(solution)/shard_map/ppermute | solution.py:38
  49.5 1.9 %collective-permute-start.11 = (bf16[256,256]{1,0:T(8,128)(2,1)S(1)}, bf16[256,256]{1,0:T(8,128)(2,1)S(1)}, u32[]{:S(2)}, u32[]{:S(2)}) collective-permute-start(bf16[256,256]{1,0:T(8,128)(2,1)S(1)} %slice.68), channel_id=1, source_target_pairs={{0,112},{32,0},{64,32},{96,64},{16,96},{48,16},{80,48},{112,80},{1... | collective-permute-start | bytes 393224 | tf_op jit(solution)/shard_map/ppermute | solution.py:28
  52.3 4.0 %collective-permute-start.10 = (bf16[256,256]{1,0:T(8,128)(2,1)S(1)}, bf16[256,256]{1,0:T(8,128)(2,1)S(1)}, u32[]{:S(2)}, u32[]{:S(2)}) collective-permute-start(bf16[256,256]{1,0:T(8,128)(2,1)S(1)} %slice.67), channel_id=1, source_target_pairs={{0,32},{32,64},{64,96},{96,16},{16,48},{48,80},{80,112},{112,0},{1... | collective-permute-start | bytes 393224 | tf_op jit(solution)/shard_map/ppermute | solution.py:28
  56.3 1.2 fusion.2
  57.5 4.7 %collective-permute-start.6 = (bf16[6,32,512]{2,0,1:T(8,128)(2,1)S(1)}, bf16[6,32,512]{2,0,1:T(8,128)(2,1)S(1)}, u32[]{:S(2)}, u32[]{:S(2)}) collective-permute-start(bf16[6,32,512]{2,0,1:T(8,128)(2,1)S(1)} %fusion.2), channel_id=1, source_target_pairs={{0,96},{128,224},{256,352},{384,480},{1,97},{129,225},{257,353},{3... | collective-permute-start | bytes 589832 | tf_op jit(solution)/shard_map/ppermute | solution.py:53
  62.2 1.3 collective-permute-start.5
  63.5 1.3 collective-permute-start.4
  66.0 4.3 %collective-permute-start.12 = (bf16[4,512,256]{2,1,0:T(8,128)(2,1)S(1)}, bf16[4,512,256]{2,1,0:T(8,128)(2,1)S(1)}, u32[]{:S(2)}, u32[]{:S(2)}) collective-permute-start(bf16[4,512,256]{2,1,0:T(8,128)(2,1)S(1)} %pad_maximum_fusion.refs_0_), channel_id=1, source_target_pairs={{0,128},{128,256},{256,384},{384,0},{1,129},{129,257},{257,385},{3... | collective-permute-start | bytes 3145736 | tf_op jit(solution)/shard_map/ppermute | solution.py:21
  70.4 1.9 %collective-permute-start.13 = (bf16[4,512,256]{2,1,0:T(8,128)(2,1)S(1)}, bf16[4,512,256]{2,1,0:T(8,128)(2,1)S(1)}, u32[]{:S(2)}, u32[]{:S(2)}) collective-permute-start(bf16[4,512,256]{2,1,0:T(8,128)(2,1)S(1)} %pad_maximum_fusion.refs_0_), channel_id=1, source_target_pairs={{0,384},{128,0},{256,128},{384,256},{1,385},{129,1},{257,129},{385... | collective-permute-start | bytes 3145736 | tf_op jit(solution)/shard_map/ppermute | solution.py:21
  72.3 2.2 %collective-permute-done.5 = bf16[6,32,512]{2,0,1:T(8,128)(2,1)S(1)} collective-permute-done((bf16[6,32,512]{2,0,1:T(8,128)(2,1)S(1)}, bf16[6,32,512]{2,0,1:T(8,128)(2,1)S(1)}, u32[]{:S(2)}, u32[]{:S(2)}) %collective-permute-start.5) | collective-permute-done | bytes 196640 | tf_op jit(solution)/shard_map/ppermute | solution.py:53
  74.5 4.6 %collective-permute-done.4 = bf16[6,32,512]{2,0,1:T(8,128)(2,1)S(1)} collective-permute-done((bf16[6,32,512]{2,0,1:T(8,128)(2,1)S(1)}, bf16[6,32,512]{2,0,1:T(8,128)(2,1)S(1)}, u32[]{:S(2)}, u32[]{:S(2)}) %collective-permute-start.4) | collective-permute-done | bytes 196640 | tf_op jit(solution)/shard_map/ppermute | solution.py:53
  79.3 27.4 %all_to_all.15.w_own = bf16[4,6,32,512]{3,2,1,0:T(8,128)(2,1)} all-to-all(bf16[4,6,32,512]{3,2,1,0:T(8,128)(2,1)S(1)} %broadcast_in_dim.23), channel_id=1, replica_groups=mesh['x'=4,'ylo'=4,'yhi'=2,'z'=8,'core'=2] {'x'}, dimensions={0} | all-to-all | bytes 1572864 | tf_op jit(solution)/shard_map/all_to_all | solution.py:54
  106.7 1.9 %collective-permute-start.7 = (bf16[4,6,32,512]{3,2,1,0:T(8,128)(2,1)}, bf16[4,6,32,512]{3,2,1,0:T(8,128)(2,1)}, u32[]{:S(2)}, u32[]{:S(2)}) collective-permute-start(bf16[4,6,32,512]{3,2,1,0:T(8,128)(2,1)} %all_to_all.15.w_own), channel_id=1, source_target_pairs={{0,1},{1,0},{2,3},{3,2},{4,5},{5,4},{6,7},{7,6},{8,9},{9,8},{10,11... | collective-permute-start | bytes 2359304 | tf_op jit(solution)/shard_map/ppermute | solution.py:38
  109.6 1.9 %collective-permute-start.14 = (bf16[2,512,256]{2,1,0:T(8,128)(2,1)}, bf16[2,512,256]{2,1,0:T(8,128)(2,1)}, u32[]{:S(2)}, u32[]{:S(2)}) collective-permute-start(bf16[2,512,256]{2,1,0:T(8,128)(2,1)} %slice.69), channel_id=1, source_target_pairs={{0,128},{128,256},{256,384},{384,0},{1,129},{129,257},{257,385},{3... | collective-permute-start | bytes 1572872 | tf_op jit(solution)/shard_map/ppermute | solution.py:21
  112.8 3.9 %collective-permute-start.15 = (bf16[2,512,256]{2,1,0:T(8,128)(2,1)}, bf16[2,512,256]{2,1,0:T(8,128)(2,1)}, u32[]{:S(2)}, u32[]{:S(2)}) collective-permute-start(bf16[2,512,256]{2,1,0:T(8,128)(2,1)} %slice.70), channel_id=1, source_target_pairs={{0,384},{128,0},{256,128},{384,256},{1,385},{129,1},{257,129},{385... | collective-permute-start | bytes 1572872 | tf_op jit(solution)/shard_map/ppermute | solution.py:21
  117.6 8.5 %collective-permute-done.14.refs_3_ = bf16[2,512,256]{2,1,0:T(8,128)(2,1)} collective-permute-done((bf16[2,512,256]{2,1,0:T(8,128)(2,1)}, bf16[2,512,256]{2,1,0:T(8,128)(2,1)}, u32[]{:S(2)}, u32[]{:S(2)}) %collective-permute-start.14) | collective-permute-done | bytes 524320 | tf_op jit(solution)/shard_map/ppermute | solution.py:21
  126.1 4.4 %collective-permute-done.15.refs_4_ = bf16[2,512,256]{2,1,0:T(8,128)(2,1)} collective-permute-done((bf16[2,512,256]{2,1,0:T(8,128)(2,1)}, bf16[2,512,256]{2,1,0:T(8,128)(2,1)}, u32[]{:S(2)}, u32[]{:S(2)}) %collective-permute-start.15) | collective-permute-done | bytes 524320 | tf_op jit(solution)/shard_map/ppermute | solution.py:21
  130.6 15.3 %shard_map.77 = (f32[16,6,128]{2,1,0:T(8,128)}, bf16[16,16,256]{2,1,0:T(8,128)(2,1)}) custom-call(s32[17]{0:T(128)} %concatenate.6.scalars, bf16[128,32,512]{2,1,0:T(8,128)(2,1)} %f_own.1, bf16[128,32,256]{2,1,0:T(8,128)(2,1)} %collective-permute-done.f_other, bf16[4,6,32,512]{3,2,1,0:T(8,128)(2,1)} %all_to_all.15.w_own, ...), custom_call_target="tpu_custom_call" | custom-call | flops 9699999744 | bytes 12000000 | tf_op jit(solution)/shard_map/pallas_call | solution.py:160
  148.7 7.0 %all-to-all-start.2 = ((f32[32,1,96]{2,1,0:T(1,128)}), f32[32,1,96]{2,1,0:T(1,128)S(1)}, u32[]{:S(2)}, u32[]{:S(2)}) async-start(f32[32,1,96]{2,1,0:T(1,128)} %bitcast.30), calls=%async_computation.2 | async-start | bytes 32768 | tf_op jit(solution)/shard_map/all_to_all | solution.py:191
  156.4 11.4 %all-to-all-done.2 = f32[32,1,96]{2,1,0:T(1,128)S(1)} async-done(((f32[32,1,96]{2,1,0:T(1,128)}), f32[32,1,96]{2,1,0:T(1,128)S(1)}, u32[]{:S(2)}, u32[]{:S(2)}) %all-to-all-start.2) | async-done | bytes 12320 | tf_op jit(solution)/shard_map/all_to_all | solution.py:191
  167.9 1.9 %collective-permute-start.16 = (f32[1,96]{1,0:T(1,128)S(1)}, f32[1,96]{1,0:T(1,128)S(1)}, u32[]{:S(2)}, u32[]{:S(2)}) collective-permute-start(f32[1,96]{1,0:T(1,128)S(1)} %bitcast.52), channel_id=1, source_target_pairs={{0,0},{1,1},{2,32},{3,33},{4,64},{5,65},{6,96},{7,97},{8,128},{9,1... | collective-permute-start | bytes 1160 | tf_op jit(solution)/shard_map/ppermute | solution.py:198
  169.9 1.9 %collective-permute-start.17 = (bf16[6,16]{1,0:T(8,128)(2,1)S(1)}, bf16[6,16]{1,0:T(8,128)(2,1)S(1)}, u32[]{:S(2)}, u32[]{:S(2)}) collective-permute-start(bf16[6,16]{1,0:T(8,128)(2,1)S(1)} %constant_dynamic-slice_fusion), channel_id=1, source_target_pairs={{0,1},{1,0},{2,3},{3,2},{4,5},{5,4},{6,7},{7,6},{8,9},{9,8},{10,11... | collective-permute-start | bytes 584 | tf_op jit(solution)/shard_map/ppermute | solution.py:38
  171.9 12.3 %collective-permute-done.16 = f32[1,96]{1,0:T(1,128)S(1)} collective-permute-done((f32[1,96]{1,0:T(1,128)S(1)}, f32[1,96]{1,0:T(1,128)S(1)}, u32[]{:S(2)}, u32[]{:S(2)}) %collective-permute-start.16) | collective-permute-done | bytes 416 | tf_op jit(solution)/shard_map/ppermute | solution.py:198
  (59 shorter events, 14.1 us)
Async XLA Ops:
  0.6 146.1 %copy-start = (f32[16,16]{1,0:T(8,128)S(1)}, f32[16,16]{1,0:T(8,128)}, u32[]{:S(2)}) copy-start(f32[16,16]{1,0:T(8,128)} %param.8) | copy-start | bytes 3076
  2.1 30.6 %all-to-all-start.1 = ((bf16[32,16,256]{2,1,0:T(8,128)(2,1)}), bf16[32,16,256]{2,1,0:T(8,128)(2,1)S(1)}, u32[]{:S(2)}, u32[]{:S(2)}) async-start(bf16[32,16,256]{2,1,0:T(8,128)(2,1)} %bitcast.21), calls=%async_computation.1 | async-start | bytes 524288 | tf_op jit(solution)/shard_map/all_to_all | solution.py:133
  32.7 13.9 %collective-permute-start.9 = (bf16[512,256]{1,0:T(8,128)(2,1)S(1)}, bf16[512,256]{1,0:T(8,128)(2,1)}, u32[]{:S(2)}, u32[]{:S(2)}) collective-permute-start(bf16[512,256]{1,0:T(8,128)(2,1)S(1)} %bitcast.46), channel_id=1, source_target_pairs={{0,112},{32,0},{64,32},{96,64},{16,96},{48,16},{80,48},{112,80},{1... | collective-permute-start | bytes 786440 | tf_op jit(solution)/shard_map/ppermute | solution.py:28
  34.6 14.9 %collective-permute-start.8 = (bf16[512,256]{1,0:T(8,128)(2,1)S(1)}, bf16[512,256]{1,0:T(8,128)(2,1)}, u32[]{:S(2)}, u32[]{:S(2)}) collective-permute-start(bf16[512,256]{1,0:T(8,128)(2,1)S(1)} %bitcast.47), channel_id=1, source_target_pairs={{0,32},{32,64},{64,96},{96,16},{16,48},{48,80},{80,112},{112,0},{1... | collective-permute-start | bytes 786440 | tf_op jit(solution)/shard_map/ppermute | solution.py:28
  40.8 11.5 %collective-permute-start.3 = (bf16[6,32,512]{2,0,1:T(8,128)(2,1)}, bf16[6,32,512]{2,0,1:T(8,128)(2,1)}, u32[]{:S(2)}, u32[]{:S(2)}) collective-permute-start(bf16[6,32,512]{2,0,1:T(8,128)(2,1)} %get-tuple-element.15), channel_id=1, source_target_pairs={{0,384},{1,385},{2,386},{3,387},{4,388},{5,389},{6,390},{7,391},{8... | collective-permute-start | bytes 589832 | tf_op jit(solution)/shard_map/ppermute | solution.py:50
  42.1 14.2 %collective-permute-start.2 = (bf16[6,32,512]{2,0,1:T(8,128)(2,1)}, bf16[6,32,512]{2,0,1:T(8,128)(2,1)}, u32[]{:S(2)}, u32[]{:S(2)}) collective-permute-start(bf16[6,32,512]{2,0,1:T(8,128)(2,1)} %get-tuple-element.16), channel_id=1, source_target_pairs={{0,256},{1,257},{2,258},{3,259},{4,260},{5,261},{6,262},{7,263},{8... | collective-permute-start | bytes 589832 | tf_op jit(solution)/shard_map/ppermute | solution.py:50
  43.5 12.9 %collective-permute-start.1 = (bf16[6,32,512]{2,0,1:T(8,128)(2,1)}, bf16[6,32,512]{2,0,1:T(8,128)(2,1)}, u32[]{:S(2)}, u32[]{:S(2)}) collective-permute-start(bf16[6,32,512]{2,0,1:T(8,128)(2,1)} %get-tuple-element.14), channel_id=1, source_target_pairs={{0,128},{1,129},{2,130},{3,131},{4,132},{5,133},{6,134},{7,135},{8... | collective-permute-start | bytes 589832 | tf_op jit(solution)/shard_map/ppermute | solution.py:50
  46.6 71.0 %collective-permute-start = (bf16[128,32,256]{2,1,0:T(8,128)(2,1)S(1)}, bf16[128,32,256]{2,1,0:T(8,128)(2,1)}, u32[]{:S(2)}, u32[]{:S(2)}) collective-permute-start(bf16[128,32,256]{2,1,0:T(8,128)(2,1)S(1)} %constant_dynamic-slice_fusion.2), channel_id=1, source_target_pairs={{0,1},{1,0},{2,3},{3,2},{4,5},{5,4},{6,7},{7,6},{8,9},{9,8},{10,11... | collective-permute-start | bytes 6291464 | tf_op jit(solution)/shard_map/ppermute | solution.py:38
  49.5 14.1 %collective-permute-start.11 = (bf16[256,256]{1,0:T(8,128)(2,1)S(1)}, bf16[256,256]{1,0:T(8,128)(2,1)S(1)}, u32[]{:S(2)}, u32[]{:S(2)}) collective-permute-start(bf16[256,256]{1,0:T(8,128)(2,1)S(1)} %slice.68), channel_id=1, source_target_pairs={{0,112},{32,0},{64,32},{96,64},{16,96},{48,16},{80,48},{112,80},{1... | collective-permute-start | bytes 393224 | tf_op jit(solution)/shard_map/ppermute | solution.py:28
  52.3 12.5 %collective-permute-start.10 = (bf16[256,256]{1,0:T(8,128)(2,1)S(1)}, bf16[256,256]{1,0:T(8,128)(2,1)S(1)}, u32[]{:S(2)}, u32[]{:S(2)}) collective-permute-start(bf16[256,256]{1,0:T(8,128)(2,1)S(1)} %slice.67), channel_id=1, source_target_pairs={{0,32},{32,64},{64,96},{96,16},{16,48},{48,80},{80,112},{112,0},{1... | collective-permute-start | bytes 393224 | tf_op jit(solution)/shard_map/ppermute | solution.py:28
  57.5 12.8 %collective-permute-start.6 = (bf16[6,32,512]{2,0,1:T(8,128)(2,1)S(1)}, bf16[6,32,512]{2,0,1:T(8,128)(2,1)S(1)}, u32[]{:S(2)}, u32[]{:S(2)}) collective-permute-start(bf16[6,32,512]{2,0,1:T(8,128)(2,1)S(1)} %fusion.2), channel_id=1, source_target_pairs={{0,96},{128,224},{256,352},{384,480},{1,97},{129,225},{257,353},{3... | collective-permute-start | bytes 589832 | tf_op jit(solution)/shard_map/ppermute | solution.py:53
  62.2 12.3 %collective-permute-start.5 = (bf16[6,32,512]{2,0,1:T(8,128)(2,1)S(1)}, bf16[6,32,512]{2,0,1:T(8,128)(2,1)S(1)}, u32[]{:S(2)}, u32[]{:S(2)}) collective-permute-start(bf16[6,32,512]{2,0,1:T(8,128)(2,1)S(1)} %fusion.2), channel_id=1, source_target_pairs={{0,64},{128,192},{256,320},{384,448},{1,65},{129,193},{257,321},{3... | collective-permute-start | bytes 589832 | tf_op jit(solution)/shard_map/ppermute | solution.py:53
  63.5 15.5 %collective-permute-start.4 = (bf16[6,32,512]{2,0,1:T(8,128)(2,1)S(1)}, bf16[6,32,512]{2,0,1:T(8,128)(2,1)S(1)}, u32[]{:S(2)}, u32[]{:S(2)}) collective-permute-start(bf16[6,32,512]{2,0,1:T(8,128)(2,1)S(1)} %fusion.2), channel_id=1, source_target_pairs={{0,32},{128,160},{256,288},{384,416},{1,33},{129,161},{257,289},{3... | collective-permute-start | bytes 589832 | tf_op jit(solution)/shard_map/ppermute | solution.py:53
  66.0 64.5 %copy-start.1 = (bf16[4,512,256]{2,1,0:T(8,128)(2,1)}, bf16[4,512,256]{2,1,0:T(8,128)(2,1)S(1)}, u32[]{:S(2)}) copy-start(bf16[4,512,256]{2,1,0:T(8,128)(2,1)S(1)} %pad_maximum_fusion.refs_0_) | copy-start | bytes 3145732
  66.0 42.6 %collective-permute-start.12 = (bf16[4,512,256]{2,1,0:T(8,128)(2,1)S(1)}, bf16[4,512,256]{2,1,0:T(8,128)(2,1)S(1)}, u32[]{:S(2)}, u32[]{:S(2)}) collective-permute-start(bf16[4,512,256]{2,1,0:T(8,128)(2,1)S(1)} %pad_maximum_fusion.refs_0_), channel_id=1, source_target_pairs={{0,128},{128,256},{256,384},{384,0},{1,129},{129,257},{257,385},{3... | collective-permute-start | bytes 3145736 | tf_op jit(solution)/shard_map/ppermute | solution.py:21
  70.4 41.2 %collective-permute-start.13 = (bf16[4,512,256]{2,1,0:T(8,128)(2,1)S(1)}, bf16[4,512,256]{2,1,0:T(8,128)(2,1)S(1)}, u32[]{:S(2)}, u32[]{:S(2)}) collective-permute-start(bf16[4,512,256]{2,1,0:T(8,128)(2,1)S(1)} %pad_maximum_fusion.refs_0_), channel_id=1, source_target_pairs={{0,384},{128,0},{256,128},{384,256},{1,385},{129,1},{257,129},{385... | collective-permute-start | bytes 3145736 | tf_op jit(solution)/shard_map/ppermute | solution.py:21
  106.7 10.8 %collective-permute-start.7 = (bf16[4,6,32,512]{3,2,1,0:T(8,128)(2,1)}, bf16[4,6,32,512]{3,2,1,0:T(8,128)(2,1)}, u32[]{:S(2)}, u32[]{:S(2)}) collective-permute-start(bf16[4,6,32,512]{3,2,1,0:T(8,128)(2,1)} %all_to_all.15.w_own), channel_id=1, source_target_pairs={{0,1},{1,0},{2,3},{3,2},{4,5},{5,4},{6,7},{7,6},{8,9},{9,8},{10,11... | collective-permute-start | bytes 2359304 | tf_op jit(solution)/shard_map/ppermute | solution.py:38
  108.7 2.9 %copy-start.2 = (bf16[4,512,256]{2,1,0:T(8,128)(2,1)}, bf16[4,512,256]{2,1,0:T(8,128)(2,1)S(1)}, u32[]{:S(2)}) copy-start(bf16[4,512,256]{2,1,0:T(8,128)(2,1)S(1)} %collective-permute-done.12.refs_1_) | copy-start | bytes 3145732
  109.6 16.5 %collective-permute-start.14 = (bf16[2,512,256]{2,1,0:T(8,128)(2,1)}, bf16[2,512,256]{2,1,0:T(8,128)(2,1)}, u32[]{:S(2)}, u32[]{:S(2)}) collective-permute-start(bf16[2,512,256]{2,1,0:T(8,128)(2,1)} %slice.69), channel_id=1, source_target_pairs={{0,128},{128,256},{256,384},{384,0},{1,129},{129,257},{257,385},{3... | collective-permute-start | bytes 1572872 | tf_op jit(solution)/shard_map/ppermute | solution.py:21
  111.5 1.3 copy-start.3
  112.8 17.7 %collective-permute-start.15 = (bf16[2,512,256]{2,1,0:T(8,128)(2,1)}, bf16[2,512,256]{2,1,0:T(8,128)(2,1)}, u32[]{:S(2)}, u32[]{:S(2)}) collective-permute-start(bf16[2,512,256]{2,1,0:T(8,128)(2,1)} %slice.70), channel_id=1, source_target_pairs={{0,384},{128,0},{256,128},{384,256},{1,385},{129,1},{257,129},{385... | collective-permute-start | bytes 1572872 | tf_op jit(solution)/shard_map/ppermute | solution.py:21
  117.6 38.8 %copy-start.5 = (f32[512]{0:T(512)S(1)}, f32[512]{0:T(512)}, u32[]{:S(2)}) copy-start(f32[512]{0:T(512)} %param.10) | copy-start | bytes 6148
  117.6 67.9 %copy-start.4 = (f32[1,6,16]{2,0,1:T(1,128)S(1)}, f32[1,6,16]{2,0,1:T(1,128)}, u32[]{:S(2)}) copy-start(f32[1,6,16]{2,0,1:T(1,128)} %param.9) | copy-start | bytes 1156
  117.6 67.9 %slice-start = ((f32[512]{0:T(512)}), f32[6]{0:T(128)S(1)}, s32[]{:S(2)}) async-start(f32[512]{0:T(512)} %param.10), calls=%async_computation.3 | async-start | bytes 1024 | tf_op jit(solution)/shard_map/slice | solution.py:203
  148.7 19.2 %all-to-all-start.2 = ((f32[32,1,96]{2,1,0:T(1,128)}), f32[32,1,96]{2,1,0:T(1,128)S(1)}, u32[]{:S(2)}, u32[]{:S(2)}) async-start(f32[32,1,96]{2,1,0:T(1,128)} %bitcast.30), calls=%async_computation.2 | async-start | bytes 32768 | tf_op jit(solution)/shard_map/all_to_all | solution.py:191
  167.9 16.2 %collective-permute-start.16 = (f32[1,96]{1,0:T(1,128)S(1)}, f32[1,96]{1,0:T(1,128)S(1)}, u32[]{:S(2)}, u32[]{:S(2)}) collective-permute-start(f32[1,96]{1,0:T(1,128)S(1)} %bitcast.52), channel_id=1, source_target_pairs={{0,0},{1,1},{2,32},{3,33},{4,64},{5,65},{6,96},{7,97},{8,128},{9,1... | collective-permute-start | bytes 1160 | tf_op jit(solution)/shard_map/ppermute | solution.py:198
  169.9 15.5 %collective-permute-start.17 = (bf16[6,16]{1,0:T(8,128)(2,1)S(1)}, bf16[6,16]{1,0:T(8,128)(2,1)S(1)}, u32[]{:S(2)}, u32[]{:S(2)}) collective-permute-start(bf16[6,16]{1,0:T(8,128)(2,1)S(1)} %constant_dynamic-slice_fusion), channel_id=1, source_target_pairs={{0,1},{1,0},{2,3},{3,2},{4,5},{5,4},{6,7},{7,6},{8,9},{9,8},{10,11... | collective-permute-start | bytes 584 | tf_op jit(solution)/shard_map/ppermute | solution.py:38

commit v2 on v1

v2 whole, which is shorter than its diff:
```python
import jax
import jax.numpy as jnp
from jax import lax
from jax.experimental import pallas as pl
from jax.experimental.pallas import tpu as pltpu
from jax.sharding import Mesh
from jax.sharding import PartitionSpec as P

AXES = ("x", "ylo", "yhi", "z", "core")
PAIR = ("x", "ylo")
AUX = ("yhi", "z", "core")
Y = ("ylo", "yhi")
BF16 = jnp.bfloat16
F32 = jnp.float32
BLOCK_Q = 8


def shifted(array, axis, by):
    if axis == "x":
        count = lax.axis_size("x")
        return lax.ppermute(array, "x", [(i, (i + by) % count) for i in range(count)])
    lows, highs = lax.axis_size("ylo"), lax.axis_size("yhi")

    def index(y):
        return (y % lows) * highs + y // lows

    full = lows * highs
    return lax.ppermute(array, Y, [(index(y), index((y + by) % full)) for y in range(full)])


def swapped(array):
    return lax.ppermute(array, "core", [(0, 1), (1, 0)])


def window_scattered(factors, rows):
    parts, lows = lax.axis_size("x"), lax.axis_size("ylo")
    wide = jnp.transpose(factors[:, :rows, :], (1, 0, 2))
    quarter = wide.shape[1] // parts
    pieces = [wide[:, i * quarter : (i + 1) * quarter, :] for i in range(parts)]
    first = (lax.axis_index("x") == 0) & (lax.axis_index("ylo") == 0)
    mine = jnp.where(first, pieces[0], jnp.zeros_like(pieces[0]))
    for i in range(1, parts):
        mine = mine + lax.ppermute(pieces[i], PAIR, [(0, i * lows)])
    return mine


def window_spread(mine):
    parts, lows = lax.axis_size("x"), lax.axis_size("ylo")
    spread = jnp.where(lax.axis_index("ylo") == 0, mine, jnp.zeros_like(mine))
    for k in range(1, lows):
        spread = spread + lax.ppermute(mine, PAIR, [(i * lows, i * lows + k) for i in range(parts)])
    return spread


def window_collected(quarter):
    parts = lax.axis_size("x")
    return lax.all_to_all(
        jnp.broadcast_to(quarter[None], (parts, *quarter.shape)), "x", 0, 0, tiled=True
    )


def half_sums(f_own, f_other, w_own, w_other, chunks, halves):
    pieces, rows, per_piece, depth = w_own.shape
    per_piece = per_piece // BLOCK_Q
    blocks = pieces * per_piece
    columns = f_own.shape[2]
    span = rows * BLOCK_Q
    count = 0
    for chunk in chunks:
        for k in range(chunk.shape[0]):
            amp = chunk[k]
            for which, w in enumerate((w_own, w_other)):
                got = jnp.dot(
                    w[...].reshape(blocks * span, depth), amp, preferred_element_type=F32
                ).reshape(pieces, rows, per_piece, BLOCK_Q, columns)
                for piece in range(pieces):
                    for b in range(per_piece):
                        at = (which * blocks + piece * per_piece + b) * columns
                        halves[count * span : (count + 1) * span, at : at + columns] = (
                            got[piece, :, b].reshape(span, columns).astype(BF16)
                        )
            count += 1
    total = None
    group = 8
    for which, f in enumerate((f_own, f_other)):
        for start in range(0, blocks, group):
            right = jnp.concatenate(
                [
                    f[(start + b) * BLOCK_Q : (start + b + 1) * BLOCK_Q].reshape(-1, columns)
                    for b in range(group)
                ],
                axis=1,
            )
            at = (which * blocks + start) * columns
            term = lax.dot_general(
                halves[:, at : at + group * columns],
                right,
                (((1,), (1,)), ((), ())),
                preferred_element_type=F32,
            )
            total = term if total is None else total + term
    width = f_own.shape[1]
    total = total.reshape(count * rows, BLOCK_Q, BLOCK_Q * width)
    q = lax.broadcasted_iota(jnp.int32, total.shape, 1)
    lane = lax.broadcasted_iota(jnp.int32, total.shape, 2)
    return jnp.sum(jnp.where(lane // width == q, total, 0.0), axis=1)


def early_kernel(scalars, f_own, f_other, w_own, w_other, *refs):
    chunks, (sums, heads, halves) = refs[:-3], refs[-3:]
    sums[...] = half_sums(f_own, f_other, w_own, w_other, chunks, halves)
    count = 0
    for chunk in chunks:
        for k in range(chunk.shape[0]):
            heads[count] = chunk[k, : heads.shape[1], :].astype(F32)
            count += 1


def late_kernel(chunk_count, scalars, f_own, f_other, w_own, w_other, hole_weights, *refs):
    chunks, refs = refs[:chunk_count], refs[chunk_count:]
    early, (out, halves, head, hole) = refs[:-4], refs[-4:]
    rows = w_own.shape[1]
    width = f_own.shape[1]
    pairs = hole_weights.shape[0]
    sums = [s[...] for s in early[0::2]]
    sums.append(half_sums(f_own, f_other, w_own, w_other, chunks, halves))
    sums = jnp.concatenate(sums, axis=0)

    local = 0
    for heads in early[1::2]:
        for k in range(heads.shape[0]):
            head[pl.ds(scalars[local], 1)] = heads[k][None]
            local += 1
    for chunk in chunks:
        for k in range(chunk.shape[0]):
            head[pl.ds(scalars[local], 1)] = chunk[k, : head.shape[1], :].astype(F32)[None]
            local += 1
    for a in range(rows):
        hole[:, a, :] = jnp.dot(
            hole_weights[...], head[:, a, :], precision=lax.Precision.HIGHEST,
            preferred_element_type=F32,
        )
    place, chosen = scalars[pairs + 1], scalars[pairs + 2]
    lanes = sums.shape[1]
    for i in range(local):
        term = hole[pl.ds(scalars[i], 1)][0, :rows, :]
        lane = lax.broadcasted_iota(jnp.int32, term.shape, 1)
        mask = (lane >= place) & (lane < place + width) & (chosen == 1)
        both = sums[i * rows : (i + 1) * rows] + jnp.where(mask, term, 0.0)
        both = both[:, : lanes // 2] + both[:, lanes // 2 :]
        both = both + pltpu.roll(both, 64, 1)
        both = both + pltpu.roll(both, 32, 1)
        other = pltpu.roll(both, 16, 1)
        row = lax.broadcasted_iota(jnp.int32, both.shape, 0)
        group = lax.broadcasted_iota(jnp.int32, both.shape, 1) // 16
        for h in range(2):
            tile = jnp.where(row % 2 == h, both, other)
            tile = jnp.sum(jnp.where(group == row, tile, 0.0), axis=0, keepdims=True)
            out[pl.ds(scalars[i] * 2 + h, 1)] = tile[None]


def per_device(amplitudes, factors, hole_weights, driver, eps_vir, pair_energy):
    pairs = hole_weights.shape[0]
    rows, columns = driver.shape[1], driver.shape[2]
    half = factors.shape[2] // 2
    width = factors.shape[1]
    x, ylo, yhi, z, core = (lax.axis_index(name) for name in AXES)
    aux_index = lax.axis_index(AUX)
    pair_index = lax.axis_index(PAIR)
    xs, lows = lax.axis_size("x"), lax.axis_size("ylo")

    own = amplitudes[0]
    split = jnp.stack([own[:, :half], own[:, half:]])
    sent = jnp.tile(split[None], (lax.axis_size("yhi") * lax.axis_size("z"), 1, 1, 1))
    amp = lax.all_to_all(sent.reshape(-1, *split.shape[1:]), AUX, 0, 0, tiled=True)
    amp = amp.reshape(-1, half)

    scattered = window_scattered(factors, rows)
    f_other = swapped(lax.dynamic_slice_in_dim(factors, (1 - core) * half, half, 2))
    amp, scattered = lax.optimization_barrier((amp, scattered))

    behind, ahead = shifted(amp, "y", 1), shifted(amp, "y", -1)
    window = window_collected(window_spread(scattered))
    opposite = shifted(behind, "y", 1)

    start = (aux_index * columns) % half
    here = lax.dynamic_slice_in_dim(amp[:rows], start, columns, 1)
    there = lax.dynamic_slice_in_dim(amp[:rows], start + columns * (1 - 2 * core), columns, 1)
    amp_cols = jnp.where(core == yhi, here, swapped(there)).astype(F32)

    chunk = jnp.stack([amp, behind, ahead, opposite])
    chunk, window, amp_cols = lax.optimization_barrier((chunk, window, amp_cols))
    window_other = swapped(window)
    x_behind, x_ahead = shifted(chunk, "x", 1), shifted(chunk, "x", -1)
    offsets = (0, 1, -1, 2)
    order = jnp.stack(
        [((x - i) % xs) * lows + (ylo - k) % lows for i in offsets for k in offsets]
    ).astype(jnp.int32)
    place = (pair_index * width) % half
    chosen = (yhi == 0) & (z == 0) & (core == (pair_index * width) // half)
    scalars = jnp.concatenate(
        [order, jnp.stack([core, place, chosen.astype(jnp.int32)]).astype(jnp.int32)]
    )

    head_rows = 8
    blocks = factors.shape[0] // BLOCK_Q
    span = rows * BLOCK_Q
    whole = pl.BlockSpec(memory_space=pltpu.VMEM)
    own_half = pl.BlockSpec((factors.shape[0], width, half), lambda i, s: (0, 0, s[pairs]))
    params = pltpu.CompilerParams(vmem_limit_bytes=40 * 1024 * 1024)

    def scratch(count):
        return pltpu.VMEM((count * span, 2 * blocks * half), BF16)

    def cost(count):
        return pl.CostEstimate(
            flops=605_000_000 * count, bytes_accessed=8_000_000, transcendentals=0
        )

    def early(*chunks):
        count = sum(c.shape[0] for c in chunks)
        return pl.pallas_call(
            early_kernel,
            grid_spec=pltpu.PrefetchScalarGridSpec(
                num_scalar_prefetch=1,
                grid=(1,),
                in_specs=[own_half] + [whole] * (3 + len(chunks)),
                out_specs=[whole, whole],
                scratch_shapes=[scratch(count)],
            ),
            out_shape=[
                jax.ShapeDtypeStruct((count * rows, BLOCK_Q * width), F32),
                jax.ShapeDtypeStruct((count, head_rows, half), F32),
            ],
            compiler_params=params,
            cost_estimate=cost(count),
        )(scalars, factors, f_other, window, window_other, *chunks)

    first = early(chunk)
    x_behind, x_ahead, first = lax.optimization_barrier((x_behind, x_ahead, first))
    cut = lows // 2
    last = (shifted(x_behind[:cut], "x", 1), shifted(x_ahead[cut:], "x", -1))
    done = [*first, *early(x_behind, x_ahead)]
    tiles = pl.pallas_call(
        lambda *refs: late_kernel(len(last), *refs),
        grid_spec=pltpu.PrefetchScalarGridSpec(
            num_scalar_prefetch=1,
            grid=(1,),
            in_specs=[own_half] + [whole] * (4 + len(last) + len(done)),
            out_specs=whole,
            scratch_shapes=[
                scratch(lows),
                pltpu.VMEM((pairs, head_rows, half), F32),
                pltpu.VMEM((pairs, head_rows, half), F32),
            ],
        ),
        out_shape=jax.ShapeDtypeStruct((pairs * 2, 1, 128), F32),
        compiler_params=params,
        cost_estimate=cost(lows),
    )(scalars, factors, f_other, window, window_other, hole_weights, *last, *done)

    summed = jnp.sum(lax.all_to_all(tiles, AUX, 0, 0, tiled=True), axis=0)
    count = lax.axis_size(AUX)
    parts = width // columns
    moves = []
    for g in range(pairs):
        for j in range(count):
            moves.append((g * count + j, (j // parts) * count + parts * g + j % parts))
    summed = lax.ppermute(summed, AXES, moves)
    summed = summed[:, : rows * columns].reshape(1, rows, columns)

    residual = driver + summed
    eps_cols = lax.dynamic_slice_in_dim(eps_vir, aux_index * columns, columns, 0)
    denominator = (
        eps_vir[:rows][None, :, None] + eps_cols[None, None, :] - pair_energy[:, None, None]
    )
    new_amps = amp_cols[None] - residual / denominator
    return (residual, new_amps)


def solution(mesh):
    finer = Mesh(mesh.devices.reshape(4, 4, 2, 8, 2), AXES)
    in_specs = (P(PAIR, AUX, None), P(AUX, PAIR, None), P(), P(PAIR, None, AUX), P(), P(PAIR))
    out_specs = (P(PAIR, None, AUX), P(PAIR, None, AUX))
    return jax.shard_map(
        per_device, mesh=finer, in_specs=in_specs, out_specs=out_specs, check_vma=False
    )
```

time: 188 us -> 171 us (0.910)
  waiting for transfers between devices: 56.8 us -> 45.4 us
  blocking collectives: 27.4 us -> 19.5 us
  Pallas kernels: 15.3 us -> 21.3 us
  starting transfers between devices: 67 us -> 63.4 us
    all_to_all x1, waiting for transfers between devices: 13.3 us -> 0.01 us  [per_device(): lax.all_to_all(sent.reshape(-1, *split.shape[1:]), AUX, 0, 0, tiled=True)]
    ppermute x7, waiting for transfers between devices: 19.1 us -> 31.1 us  [the longest x3 13.5 us: window_spread(): lax.ppermute(mine, PAIR, [(i * lows, i * lows + k) for i in range(parts)])]
    all_to_all x1, waiting for transfers between devices: 11.4 us -> 0.01 us  [window_collected(): lax.all_to_all(jnp.broadcast_to(quarter[None], (parts, *quarter.shape)),...]
    all_to_all x1, blocking collectives: 27.4 us -> 19.5 us  [per_device(): summed = jnp.sum(lax.all_to_all(tiles, AUX, 0, 0, tiled=True), axis=0)]
    ppermute x4, waiting for transfers between devices: 13 us -> 6.55 us  [shifted(): lax.ppermute(array, 'x', [(i, (i + by) % count) for i in range(count)])]
    pallas_call x1 -> x3, Pallas kernels: 15.3 us -> 21.3 us  [the longest x2 14.9 us: early(): pl.pallas_call(early_kernel, grid_spec=pltpu.PrefetchScalarGridSpec(num_s...]
    ppermute x4 -> x3, waiting for transfers between devices: 0.01 us -> 4.46 us  [shifted(): lax.ppermute(array, Y, [(index(y), index((y + by) % full)) for y in range...]
    ppermute x3, waiting for transfers between devices: 0.01 us -> 3.25 us  [swapped(): return lax.ppermute(array, 'core', [(0, 1), (1, 0)])]
  transfers between devices with their start and end apart: 20 -> 19, of which waited for: 7 -> 10; matrix products, arithmetic and copies ran while one was open for 7% -> 6% of each run, Pallas kernels for 0% -> 9%
where the time goes in v2:
time: 171 us; the launch traced here: 170 us
  starting transfers between devices  63.4 us (37%)
  waiting for transfers between devices  45.4 us (27%)
  Pallas kernels  21.3 us (12%)
  blocking collectives  19.5 us (11%)
  local copies, waits for them, and re-layouts  14.9 us (9%)
  other arithmetic  3.48 us (2%)
  between operations  1.76 us (1%)
    all_to_all x1, blocking collectives, per_device(): summed = jnp.sum(lax.all_to_all(tiles, AUX, 0, 0, tiled=True), axis=0)  19.5 us
    all_to_all x1, starting transfers between devices, per_device(): lax.all_to_all(sent.reshape(-1, *split.shape[1:]), AUX, 0, 0, tiled=True)  16 us
    pallas_call x2, Pallas kernels, early(): pl.pallas_call(early_kernel, grid_spec=pltpu.PrefetchScalarGridSpec(num_s...  14.9 us
    ppermute x3, waiting for transfers between devices, window_spread(): lax.ppermute(mine, PAIR, [(i * lows, i * lows + k) for i in range(parts)])  13.5 us
    ppermute x3, starting transfers between devices, shifted(): lax.ppermute(array, Y, [(index(y), index((y + by) % full)) for y in range...  12.3 us
    ppermute x4, starting transfers between devices, shifted(): lax.ppermute(array, 'x', [(i, (i + by) % count) for i in range(count)])  11.9 us
    ppermute x1, waiting for transfers between devices, per_device(): summed = lax.ppermute(summed, AXES, moves)  11.8 us
    ppermute x4, waiting for transfers between devices, shifted(): lax.ppermute(array, 'x', [(i, (i + by) % count) for i in range(count)])  6.55 us
  transfers between devices with their start and end apart: 19, of which 10 were waited for; matrix products, arithmetic and copies ran while one was open for 6% of the time, Pallas kernels for 9%

profile of v2, /device:TPU:6, one launch (start us, length us, event | category | flops | bytes accessed | tf_op | source)
XLA Modules:
  0.0 169.8 jit_solution(17916191515011667826)
XLA Ops:
  2.1 16.0 %all-to-all-start = ((bf16[32,16,256]{2,1,0:T(8,128)(2,1)}), bf16[32,16,256]{2,1,0:T(8,128)(2,1)S(1)}, u32[]{:S(2)}, u32[]{:S(2)}) async-start(bf16[32,16,256]{2,1,0:T(8,128)(2,1)} %bitcast.22), calls=%async_computation | async-start | bytes 524288 | tf_op jit(solution)/shard_map/all_to_all | solution.py:175
  22.9 3.1 %constant_dynamic-slice_fusion.1 = bf16[128,32,256]{2,1,0:T(8,128)(2,1)} fusion(bf16[128,32,512]{2,1,0:T(8,128)(2,1)} %refs_1_.1, s32[]{:T(128)S(6)} %select_n.139), kind=kLoop, calls=%fused_computation.14 | loop fusion | bytes 4194308 | tf_op jit(solution)/shard_map/dynamic_slice | solution.py:179
  26.1 2.2 %collective-permute-start = (bf16[128,32,256]{2,1,0:T(8,128)(2,1)}, bf16[128,32,256]{2,1,0:T(8,128)(2,1)S(1)}, u32[]{:S(2)}, u32[]{:S(2)}) collective-permute-start(bf16[128,32,256]{2,1,0:T(8,128)(2,1)} %constant_dynamic-slice_fusion.1), channel_id=1, source_target_pairs={{0,1},{1,0},{2,3},{3,2},{4,5},{5,4},{6,7},{7,6},{8,9},{9,8},{10,11... | collective-permute-start | bytes 6291464 | tf_op jit(solution)/shard_map/ppermute | solution.py:32
  28.3 5.8 %collective-permute-done.3 = bf16[6,32,512]{2,0,1:T(8,128)(2,1)S(1)} collective-permute-done((bf16[6,32,512]{2,0,1:T(8,128)(2,1)S(1)}, bf16[6,32,512]{2,0,1:T(8,128)(2,1)S(1)}, u32[]{:S(2)}, u32[]{:S(2)}) %collective-permute-start.3) | collective-permute-done | bytes 196640 | tf_op jit(solution)/shard_map/ppermute | solution.py:43
  35.1 2.8 %collective-permute-start.7 = (bf16[6,32,512]{2,0,1:T(8,128)(2,1)S(1)}, bf16[6,32,512]{2,0,1:T(8,128)(2,1)S(1)}, u32[]{:S(2)}, u32[]{:S(2)}) collective-permute-start(bf16[6,32,512]{2,0,1:T(8,128)(2,1)S(1)} %fusion.2), channel_id=1, source_target_pairs={{0,32},{128,160},{256,288},{384,416},{1,33},{129,161},{257,289},{3... | collective-permute-start | bytes 589832 | tf_op jit(solution)/shard_map/ppermute | solution.py:51
  37.9 1.3 collective-permute-start.8
  39.2 1.3 collective-permute-start.9
  40.5 1.9 %collective-permute-start.4 = (bf16[512,256]{1,0:T(8,128)(2,1)S(1)}, bf16[512,256]{1,0:T(8,128)(2,1)S(1)}, u32[]{:S(2)}, u32[]{:S(2)}) collective-permute-start(bf16[512,256]{1,0:T(8,128)(2,1)S(1)} %bitcast.37), channel_id=1, source_target_pairs={{0,32},{32,64},{64,96},{96,16},{16,48},{48,80},{80,112},{112,0},{1... | collective-permute-start | bytes 786440 | tf_op jit(solution)/shard_map/ppermute | solution.py:28
  42.5 2.2 %collective-permute-done.7 = bf16[6,32,512]{2,0,1:T(8,128)(2,1)S(1)} collective-permute-done((bf16[6,32,512]{2,0,1:T(8,128)(2,1)S(1)}, bf16[6,32,512]{2,0,1:T(8,128)(2,1)S(1)}, u32[]{:S(2)}, u32[]{:S(2)}) %collective-permute-start.7) | collective-permute-done | bytes 196640 | tf_op jit(solution)/shard_map/ppermute | solution.py:51
  44.6 5.7 %collective-permute-done.8 = bf16[6,32,512]{2,0,1:T(8,128)(2,1)S(1)} collective-permute-done((bf16[6,32,512]{2,0,1:T(8,128)(2,1)S(1)}, bf16[6,32,512]{2,0,1:T(8,128)(2,1)S(1)}, u32[]{:S(2)}, u32[]{:S(2)}) %collective-permute-start.8) | collective-permute-done | bytes 196640 | tf_op jit(solution)/shard_map/ppermute | solution.py:51
  50.3 5.6 %collective-permute-done.9 = bf16[6,32,512]{2,0,1:T(8,128)(2,1)S(1)} collective-permute-done((bf16[6,32,512]{2,0,1:T(8,128)(2,1)S(1)}, bf16[6,32,512]{2,0,1:T(8,128)(2,1)S(1)}, u32[]{:S(2)}, u32[]{:S(2)}) %collective-permute-start.9) | collective-permute-done | bytes 196640 | tf_op jit(solution)/shard_map/ppermute | solution.py:51
  57.1 5.6 %all-to-all-start.1 = ((bf16[4,6,32,512]{3,2,1,0:T(8,128)(2,1)}), bf16[4,6,32,512]{3,2,1,0:T(8,128)(2,1)S(1)}, u32[]{:S(2)}, u32[]{:S(2)}) async-start(bf16[4,6,32,512]{3,2,1,0:T(8,128)(2,1)} %broadcast_in_dim.4), calls=%async_computation.1 | async-start | bytes 1572864 | tf_op jit(solution)/shard_map/all_to_all | solution.py:57
  62.7 8.5 %collective-permute-start.5 = (bf16[512,256]{1,0:T(8,128)(2,1)S(1)}, bf16[512,256]{1,0:T(8,128)(2,1)}, u32[]{:S(2)}, u32[]{:S(2)}) collective-permute-start(bf16[512,256]{1,0:T(8,128)(2,1)S(1)} %bitcast.39), channel_id=1, source_target_pairs={{0,112},{32,0},{64,32},{96,64},{16,96},{48,16},{80,48},{112,80},{1... | collective-permute-start | bytes 786440 | tf_op jit(solution)/shard_map/ppermute | solution.py:28
  71.2 1.9 %collective-permute-start.6 = (bf16[512,256]{1,0:T(8,128)(2,1)S(1)}, bf16[512,256]{1,0:T(8,128)(2,1)}, u32[]{:S(2)}, u32[]{:S(2)}) collective-permute-start(bf16[512,256]{1,0:T(8,128)(2,1)S(1)} %collective-permute-done.4), channel_id=1, source_target_pairs={{0,32},{32,64},{64,96},{96,16},{16,48},{48,80},{80,112},{112,0},{1... | collective-permute-start | bytes 786440 | tf_op jit(solution)/shard_map/ppermute | solution.py:28
  73.2 1.9 %collective-permute-start.10 = (bf16[6,16]{1,0:T(8,128)(2,1)S(1)}, bf16[6,16]{1,0:T(8,128)(2,1)S(1)}, u32[]{:S(2)}, u32[]{:S(2)}) collective-permute-start(bf16[6,16]{1,0:T(8,128)(2,1)S(1)} %constant_dynamic-slice_fusion), channel_id=1, source_target_pairs={{0,1},{1,0},{2,3},{3,2},{4,5},{5,4},{6,7},{7,6},{8,9},{9,8},{10,11... | collective-permute-start | bytes 584 | tf_op jit(solution)/shard_map/ppermute | solution.py:32
  76.3 4.5 %collective-permute-done.6 = bf16[512,256]{1,0:T(8,128)(2,1)} collective-permute-done((bf16[512,256]{1,0:T(8,128)(2,1)S(1)}, bf16[512,256]{1,0:T(8,128)(2,1)}, u32[]{:S(2)}, u32[]{:S(2)}) %collective-permute-start.6) | collective-permute-done | bytes 262176 | tf_op jit(solution)/shard_map/ppermute | solution.py:28
  80.7 2.1 %pad_maximum_fusion.refs_0_ = bf16[4,512,256]{2,1,0:T(8,128)(2,1)} fusion(bf16[1,512,256]{2,1,0:T(8,128)(2,1)} %bitcast.28, bf16[1,512,256]{2,1,0:T(8,128)(2,1)} %bitcast.27, bf16[1,512,256]{2,1,0:T(8,128)(2,1)S(1)} %bitcast.41, bf16[1,512,256]{2,1,0:T(8,128)(2,1)S(1)} %bitcast.40), kind=kLoop, calls=%fused_computation | loop fusion | flops 1572864 | bytes 2097152 | tf_op jit(solution)/shard_map/stack | solution.py:191
  82.9 1.9 %collective-permute-start.12 = (bf16[4,512,256]{2,1,0:T(8,128)(2,1)}, bf16[4,512,256]{2,1,0:T(8,128)(2,1)}, u32[]{:S(2)}, u32[]{:S(2)}) collective-permute-start(bf16[4,512,256]{2,1,0:T(8,128)(2,1)} %pad_maximum_fusion.refs_0_), channel_id=1, source_target_pairs={{0,128},{128,256},{256,384},{384,0},{1,129},{129,257},{257,385},{3... | collective-permute-start | bytes 3145736 | tf_op jit(solution)/shard_map/ppermute | solution.py:21
  84.8 3.9 %collective-permute-start.13 = (bf16[4,512,256]{2,1,0:T(8,128)(2,1)}, bf16[4,512,256]{2,1,0:T(8,128)(2,1)}, u32[]{:S(2)}, u32[]{:S(2)}) collective-permute-start(bf16[4,512,256]{2,1,0:T(8,128)(2,1)} %pad_maximum_fusion.refs_0_), channel_id=1, source_target_pairs={{0,384},{128,0},{256,128},{384,256},{1,385},{129,1},{257,129},{385... | collective-permute-start | bytes 3145736 | tf_op jit(solution)/shard_map/ppermute | solution.py:21
  88.8 1.9 %collective-permute-start.11 = (bf16[4,6,32,512]{3,2,1,0:T(8,128)(2,1)S(1)}, bf16[4,6,32,512]{3,2,1,0:T(8,128)(2,1)}, u32[]{:S(2)}, u32[]{:S(2)}) collective-permute-start(bf16[4,6,32,512]{3,2,1,0:T(8,128)(2,1)S(1)} %all-to-all-done.1.w_own.refs_3_), channel_id=1, source_target_pairs={{0,1},{1,0},{2,3},{3,2},{4,5},{5,4},{6,7},{7,6},{8,9},{9,8},{10,11... | collective-permute-start | bytes 2359304 | tf_op jit(solution)/shard_map/ppermute | solution.py:32
  90.9 2.1 %collective-permute-done.11.w_other.refs_4_ = bf16[4,6,32,512]{3,2,1,0:T(8,128)(2,1)} collective-permute-done((bf16[4,6,32,512]{3,2,1,0:T(8,128)(2,1)S(1)}, bf16[4,6,32,512]{3,2,1,0:T(8,128)(2,1)}, u32[]{:S(2)}, u32[]{:S(2)}) %collective-permute-start.11) | collective-permute-done | bytes 786464 | tf_op jit(solution)/shard_map/ppermute | solution.py:32
  93.1 2.2 %copy-done = bf16[128,32,512]{2,1,0:T(8,128)(2,1)S(1)} copy-done((bf16[128,32,512]{2,1,0:T(8,128)(2,1)S(1)}, bf16[128,32,512]{2,1,0:T(8,128)(2,1)}, u32[]{:S(2)}) %copy-start) | copy-done | bytes 4194328
  96.5 6.0 %shard_map.77 = (f32[24,256]{1,0:T(8,128)S(1)}, f32[4,8,256]{2,1,0:T(8,128)S(1)}) custom-call(s32[19]{0:T(128)S(1)} %concatenate.3.scalars.refs_0_, bf16[128,32,512]{2,1,0:T(8,128)(2,1)S(1)} %copy-done, bf16[128,32,256]{2,1,0:T(8,128)(2,1)S(1)} %collective-permute-done.f_other.refs_2_, bf16[4,6,32,512]{3,2,1,0:T(8,128)(2,1)S(1)} %all-to-all-done.1.w_own.refs_3_, ...), custom_call_target="tpu_custom_call" | custom-call | flops 2420000000 | bytes 8000000 | tf_op jit(solution)/shard_map/pallas_call | solution.py:222
  102.5 3.4 %collective-permute-done.12.refs_0_ = bf16[4,512,256]{2,1,0:T(8,128)(2,1)} collective-permute-done((bf16[4,512,256]{2,1,0:T(8,128)(2,1)}, bf16[4,512,256]{2,1,0:T(8,128)(2,1)}, u32[]{:S(2)}, u32[]{:S(2)}) %collective-permute-start.12) | collective-permute-done | bytes 1048608 | tf_op jit(solution)/shard_map/ppermute | solution.py:21
  105.9 3.1 %collective-permute-done.13.refs_1_ = bf16[4,512,256]{2,1,0:T(8,128)(2,1)} collective-permute-done((bf16[4,512,256]{2,1,0:T(8,128)(2,1)}, bf16[4,512,256]{2,1,0:T(8,128)(2,1)}, u32[]{:S(2)}, u32[]{:S(2)}) %collective-permute-start.13) | collective-permute-done | bytes 1048608 | tf_op jit(solution)/shard_map/ppermute | solution.py:21
  110.1 2.4 %collective-permute-start.14 = (bf16[2,512,256]{2,1,0:T(8,128)(2,1)S(1)}, bf16[2,512,256]{2,1,0:T(8,128)(2,1)S(1)}, u32[]{:S(2)}, u32[]{:S(2)}) collective-permute-start(bf16[2,512,256]{2,1,0:T(8,128)(2,1)S(1)} %slice.45), channel_id=1, source_target_pairs={{0,128},{128,256},{256,384},{384,0},{1,129},{129,257},{257,385},{3... | collective-permute-start | bytes 1572872 | tf_op jit(solution)/shard_map/ppermute | solution.py:21
  113.6 3.6 %collective-permute-start.15 = (bf16[2,512,256]{2,1,0:T(8,128)(2,1)S(1)}, bf16[2,512,256]{2,1,0:T(8,128)(2,1)S(1)}, u32[]{:S(2)}, u32[]{:S(2)}) collective-permute-start(bf16[2,512,256]{2,1,0:T(8,128)(2,1)S(1)} %slice.46), channel_id=1, source_target_pairs={{0,384},{128,0},{256,128},{384,256},{1,385},{129,1},{257,129},{385... | collective-permute-start | bytes 1572872 | tf_op jit(solution)/shard_map/ppermute | solution.py:21
  117.2 8.9 %shard_map.78 = (f32[48,256]{1,0:T(8,128)S(1)}, f32[8,8,256]{2,1,0:T(8,128)S(1)}) custom-call(s32[19]{0:T(128)S(1)} %concatenate.3.scalars.refs_0_, bf16[128,32,512]{2,1,0:T(8,128)(2,1)S(1)} %copy-done, bf16[128,32,256]{2,1,0:T(8,128)(2,1)S(1)} %collective-permute-done.f_other.refs_2_, bf16[4,6,32,512]{3,2,1,0:T(8,128)(2,1)S(1)} %all-to-all-done.1.w_own.refs_3_, ...), custom_call_target="tpu_custom_call" | custom-call | flops 4840000000 | bytes 8000000 | tf_op jit(solution)/shard_map/pallas_call | solution.py:222
  126.2 6.4 %shard_map.79 = f32[32,1,128]{2,1,0:T(1,128)S(1)} custom-call(s32[19]{0:T(128)S(1)} %concatenate.3.scalars.refs_0_, bf16[128,32,512]{2,1,0:T(8,128)(2,1)S(1)} %copy-done, bf16[128,32,256]{2,1,0:T(8,128)(2,1)S(1)} %collective-permute-done.f_other.refs_2_, bf16[4,6,32,512]{3,2,1,0:T(8,128)(2,1)S(1)} %all-to-all-done.1.w_own.refs_3_, ...), custom_call_target="tpu_custom_call" | custom-call | flops 2420000000 | bytes 8000000 | tf_op jit(solution)/shard_map/pallas_call | solution.py:244
  132.6 19.5 %all_to_all.15 = f32[32,1,128]{2,1,0:T(1,128)S(1)} all-to-all(f32[32,1,128]{2,1,0:T(1,128)S(1)} %shard_map.79), channel_id=1, replica_groups=mesh['x'=4,'ylo'=4,'yhi'=2,'z'=8,'core'=2] {'yhi','z','core'}, dimensions={0} | all-to-all | bytes 32768 | tf_op jit(solution)/shard_map/all_to_all | solution.py:262
  152.2 3.7 %collective-permute-start.16 = (f32[1,128]{1,0:T(1,128)S(1)}, f32[1,128]{1,0:T(1,128)S(1)}, u32[]{:S(2)}, u32[]{:S(2)}) collective-permute-start(f32[1,128]{1,0:T(1,128)S(1)} %bitcast.43), channel_id=1, source_target_pairs={{0,0},{1,1},{2,32},{3,33},{4,64},{5,65},{6,96},{7,97},{8,128},{9,1... | collective-permute-start | bytes 1544 | tf_op jit(solution)/shard_map/ppermute | solution.py:269
  156.6 11.8 %collective-permute-done.16 = f32[1,128]{1,0:T(1,128)S(1)} collective-permute-done((f32[1,128]{1,0:T(1,128)S(1)}, f32[1,128]{1,0:T(1,128)S(1)}, u32[]{:S(2)}, u32[]{:S(2)}) %collective-permute-start.16) | collective-permute-done | bytes 544 | tf_op jit(solution)/shard_map/ppermute | solution.py:269
  (48 shorter events, 14.7 us)
Async XLA Ops:
  2.1 33.0 %all-to-all-start = ((bf16[32,16,256]{2,1,0:T(8,128)(2,1)}), bf16[32,16,256]{2,1,0:T(8,128)(2,1)S(1)}, u32[]{:S(2)}, u32[]{:S(2)}) async-start(bf16[32,16,256]{2,1,0:T(8,128)(2,1)} %bitcast.22), calls=%async_computation | async-start | bytes 524288 | tf_op jit(solution)/shard_map/all_to_all | solution.py:175
  19.4 3.6 %copy-start.3 = (bf16[6,128,512]{2,0,1:T(8,128)(2,1)}, bf16[6,128,512]{2,0,1:T(8,128)(2,1)S(1)}, u32[]{:S(2)}) copy-start(bf16[6,128,512]{2,0,1:T(8,128)(2,1)S(1)} %slice_bitcast_fusion) | copy-start | bytes 2359300
  20.3 8.0 %collective-permute-start.1 = (bf16[6,32,512]{2,0,1:T(8,128)(2,1)}, bf16[6,32,512]{2,0,1:T(8,128)(2,1)S(1)}, u32[]{:S(2)}, u32[]{:S(2)}) collective-permute-start(bf16[6,32,512]{2,0,1:T(8,128)(2,1)} %get-tuple-element.34), channel_id=1, source_target_pairs={{0,128},{1,129},{2,130},{3,131},{4,132},{5,133},{6,134},{7,135},{8... | collective-permute-start | bytes 589832 | tf_op jit(solution)/shard_map/ppermute | solution.py:43
  20.9 7.3 %collective-permute-start.2 = (bf16[6,32,512]{2,0,1:T(8,128)(2,1)}, bf16[6,32,512]{2,0,1:T(8,128)(2,1)S(1)}, u32[]{:S(2)}, u32[]{:S(2)}) collective-permute-start(bf16[6,32,512]{2,0,1:T(8,128)(2,1)} %get-tuple-element.36), channel_id=1, source_target_pairs={{0,256},{1,257},{2,258},{3,259},{4,260},{5,261},{6,262},{7,263},{8... | collective-permute-start | bytes 589832 | tf_op jit(solution)/shard_map/ppermute | solution.py:43
  21.6 12.5 %collective-permute-start.3 = (bf16[6,32,512]{2,0,1:T(8,128)(2,1)S(1)}, bf16[6,32,512]{2,0,1:T(8,128)(2,1)S(1)}, u32[]{:S(2)}, u32[]{:S(2)}) collective-permute-start(bf16[6,32,512]{2,0,1:T(8,128)(2,1)S(1)} %get-tuple-element.35), channel_id=1, source_target_pairs={{0,384},{1,385},{2,386},{3,387},{4,388},{5,389},{6,390},{7,391},{8... | collective-permute-start | bytes 589832 | tf_op jit(solution)/shard_map/ppermute | solution.py:43
  26.1 67.0 %collective-permute-start = (bf16[128,32,256]{2,1,0:T(8,128)(2,1)}, bf16[128,32,256]{2,1,0:T(8,128)(2,1)S(1)}, u32[]{:S(2)}, u32[]{:S(2)}) collective-permute-start(bf16[128,32,256]{2,1,0:T(8,128)(2,1)} %constant_dynamic-slice_fusion.1), channel_id=1, source_target_pairs={{0,1},{1,0},{2,3},{3,2},{4,5},{5,4},{6,7},{7,6},{8,9},{9,8},{10,11... | collective-permute-start | bytes 6291464 | tf_op jit(solution)/shard_map/ppermute | solution.py:32
  35.1 9.5 %collective-permute-start.7 = (bf16[6,32,512]{2,0,1:T(8,128)(2,1)S(1)}, bf16[6,32,512]{2,0,1:T(8,128)(2,1)S(1)}, u32[]{:S(2)}, u32[]{:S(2)}) collective-permute-start(bf16[6,32,512]{2,0,1:T(8,128)(2,1)S(1)} %fusion.2), channel_id=1, source_target_pairs={{0,32},{128,160},{256,288},{384,416},{1,33},{129,161},{257,289},{3... | collective-permute-start | bytes 589832 | tf_op jit(solution)/shard_map/ppermute | solution.py:51
  37.9 12.4 %collective-permute-start.8 = (bf16[6,32,512]{2,0,1:T(8,128)(2,1)S(1)}, bf16[6,32,512]{2,0,1:T(8,128)(2,1)S(1)}, u32[]{:S(2)}, u32[]{:S(2)}) collective-permute-start(bf16[6,32,512]{2,0,1:T(8,128)(2,1)S(1)} %fusion.2), channel_id=1, source_target_pairs={{0,64},{128,192},{256,320},{384,448},{1,65},{129,193},{257,321},{3... | collective-permute-start | bytes 589832 | tf_op jit(solution)/shard_map/ppermute | solution.py:51
  39.2 16.7 %collective-permute-start.9 = (bf16[6,32,512]{2,0,1:T(8,128)(2,1)S(1)}, bf16[6,32,512]{2,0,1:T(8,128)(2,1)S(1)}, u32[]{:S(2)}, u32[]{:S(2)}) collective-permute-start(bf16[6,32,512]{2,0,1:T(8,128)(2,1)S(1)} %fusion.2), channel_id=1, source_target_pairs={{0,96},{128,224},{256,352},{384,480},{1,97},{129,225},{257,353},{3... | collective-permute-start | bytes 589832 | tf_op jit(solution)/shard_map/ppermute | solution.py:51
  40.5 30.6 %collective-permute-start.4 = (bf16[512,256]{1,0:T(8,128)(2,1)S(1)}, bf16[512,256]{1,0:T(8,128)(2,1)S(1)}, u32[]{:S(2)}, u32[]{:S(2)}) collective-permute-start(bf16[512,256]{1,0:T(8,128)(2,1)S(1)} %bitcast.37), channel_id=1, source_target_pairs={{0,32},{32,64},{64,96},{96,16},{16,48},{48,80},{80,112},{112,0},{1... | collective-permute-start | bytes 786440 | tf_op jit(solution)/shard_map/ppermute | solution.py:28
  57.1 25.8 %all-to-all-start.1 = ((bf16[4,6,32,512]{3,2,1,0:T(8,128)(2,1)}), bf16[4,6,32,512]{3,2,1,0:T(8,128)(2,1)S(1)}, u32[]{:S(2)}, u32[]{:S(2)}) async-start(bf16[4,6,32,512]{3,2,1,0:T(8,128)(2,1)} %broadcast_in_dim.4), calls=%async_computation.1 | async-start | bytes 1572864 | tf_op jit(solution)/shard_map/all_to_all | solution.py:57
  62.7 13.6 %collective-permute-start.5 = (bf16[512,256]{1,0:T(8,128)(2,1)S(1)}, bf16[512,256]{1,0:T(8,128)(2,1)}, u32[]{:S(2)}, u32[]{:S(2)}) collective-permute-start(bf16[512,256]{1,0:T(8,128)(2,1)S(1)} %bitcast.39), channel_id=1, source_target_pairs={{0,112},{32,0},{64,32},{96,64},{16,96},{48,16},{80,48},{112,80},{1... | collective-permute-start | bytes 786440 | tf_op jit(solution)/shard_map/ppermute | solution.py:28
  71.2 9.6 %collective-permute-start.6 = (bf16[512,256]{1,0:T(8,128)(2,1)S(1)}, bf16[512,256]{1,0:T(8,128)(2,1)}, u32[]{:S(2)}, u32[]{:S(2)}) collective-permute-start(bf16[512,256]{1,0:T(8,128)(2,1)S(1)} %collective-permute-done.4), channel_id=1, source_target_pairs={{0,32},{32,64},{64,96},{96,16},{16,48},{48,80},{80,112},{112,0},{1... | collective-permute-start | bytes 786440 | tf_op jit(solution)/shard_map/ppermute | solution.py:28
  73.2 3.0 %collective-permute-start.10 = (bf16[6,16]{1,0:T(8,128)(2,1)S(1)}, bf16[6,16]{1,0:T(8,128)(2,1)S(1)}, u32[]{:S(2)}, u32[]{:S(2)}) collective-permute-start(bf16[6,16]{1,0:T(8,128)(2,1)S(1)} %constant_dynamic-slice_fusion), channel_id=1, source_target_pairs={{0,1},{1,0},{2,3},{3,2},{4,5},{5,4},{6,7},{7,6},{8,9},{9,8},{10,11... | collective-permute-start | bytes 584 | tf_op jit(solution)/shard_map/ppermute | solution.py:32
  82.9 23.0 %collective-permute-start.12 = (bf16[4,512,256]{2,1,0:T(8,128)(2,1)}, bf16[4,512,256]{2,1,0:T(8,128)(2,1)}, u32[]{:S(2)}, u32[]{:S(2)}) collective-permute-start(bf16[4,512,256]{2,1,0:T(8,128)(2,1)} %pad_maximum_fusion.refs_0_), channel_id=1, source_target_pairs={{0,128},{128,256},{256,384},{384,0},{1,129},{129,257},{257,385},{3... | collective-permute-start | bytes 3145736 | tf_op jit(solution)/shard_map/ppermute | solution.py:21
  84.8 24.2 %collective-permute-start.13 = (bf16[4,512,256]{2,1,0:T(8,128)(2,1)}, bf16[4,512,256]{2,1,0:T(8,128)(2,1)}, u32[]{:S(2)}, u32[]{:S(2)}) collective-permute-start(bf16[4,512,256]{2,1,0:T(8,128)(2,1)} %pad_maximum_fusion.refs_0_), channel_id=1, source_target_pairs={{0,384},{128,0},{256,128},{384,256},{1,385},{129,1},{257,129},{385... | collective-permute-start | bytes 3145736 | tf_op jit(solution)/shard_map/ppermute | solution.py:21
  88.8 4.3 %collective-permute-start.11 = (bf16[4,6,32,512]{3,2,1,0:T(8,128)(2,1)S(1)}, bf16[4,6,32,512]{3,2,1,0:T(8,128)(2,1)}, u32[]{:S(2)}, u32[]{:S(2)}) collective-permute-start(bf16[4,6,32,512]{3,2,1,0:T(8,128)(2,1)S(1)} %all-to-all-done.1.w_own.refs_3_), channel_id=1, source_target_pairs={{0,1},{1,0},{2,3},{3,2},{4,5},{5,4},{6,7},{7,6},{8,9},{9,8},{10,11... | collective-permute-start | bytes 2359304 | tf_op jit(solution)/shard_map/ppermute | solution.py:32
  93.1 2.2 %copy-start = (bf16[128,32,512]{2,1,0:T(8,128)(2,1)S(1)}, bf16[128,32,512]{2,1,0:T(8,128)(2,1)}, u32[]{:S(2)}) copy-start(bf16[128,32,512]{2,1,0:T(8,128)(2,1)} %refs_1_.1) | copy-start | bytes 12582916
  95.3 1.2 copy-start.1
  110.1 16.0 %collective-permute-start.14 = (bf16[2,512,256]{2,1,0:T(8,128)(2,1)S(1)}, bf16[2,512,256]{2,1,0:T(8,128)(2,1)S(1)}, u32[]{:S(2)}, u32[]{:S(2)}) collective-permute-start(bf16[2,512,256]{2,1,0:T(8,128)(2,1)S(1)} %slice.45), channel_id=1, source_target_pairs={{0,128},{128,256},{256,384},{384,0},{1,129},{129,257},{257,385},{3... | collective-permute-start | bytes 1572872 | tf_op jit(solution)/shard_map/ppermute | solution.py:21
  113.6 12.5 %copy-start.2 = (f32[16,16]{1,0:T(8,128)S(1)}, f32[16,16]{1,0:T(8,128)}, u32[]{:S(2)}) copy-start(f32[16,16]{1,0:T(8,128)} %refs_5_.1) | copy-start | bytes 3076
  113.6 12.5 %collective-permute-start.15 = (bf16[2,512,256]{2,1,0:T(8,128)(2,1)S(1)}, bf16[2,512,256]{2,1,0:T(8,128)(2,1)S(1)}, u32[]{:S(2)}, u32[]{:S(2)}) collective-permute-start(bf16[2,512,256]{2,1,0:T(8,128)(2,1)S(1)} %slice.46), channel_id=1, source_target_pairs={{0,384},{128,0},{256,128},{384,256},{1,385},{129,1},{257,129},{385... | collective-permute-start | bytes 1572872 | tf_op jit(solution)/shard_map/ppermute | solution.py:21
  126.2 29.7 %copy-start.5 = (f32[512]{0:T(512)S(1)}, f32[512]{0:T(512)}, u32[]{:S(2)}) copy-start(f32[512]{0:T(512)} %param.10) | copy-start | bytes 6148
  126.2 42.4 %copy-start.4 = (f32[1,6,16]{2,0,1:T(1,128)S(1)}, f32[1,6,16]{2,0,1:T(1,128)}, u32[]{:S(2)}) copy-start(f32[1,6,16]{2,0,1:T(1,128)} %param.9) | copy-start | bytes 1156
  126.2 42.4 %slice-start = ((f32[512]{0:T(512)}), f32[6]{0:T(128)S(1)}, s32[]{:S(2)}) async-start(f32[512]{0:T(512)} %param.10), calls=%async_computation.3 | async-start | bytes 1024 | tf_op jit(solution)/shard_map/slice | solution.py:275
  152.2 16.2 %collective-permute-start.16 = (f32[1,128]{1,0:T(1,128)S(1)}, f32[1,128]{1,0:T(1,128)S(1)}, u32[]{:S(2)}, u32[]{:S(2)}) collective-permute-start(f32[1,128]{1,0:T(1,128)S(1)} %bitcast.43), channel_id=1, source_target_pairs={{0,0},{1,1},{2,32},{3,33},{4,64},{5,65},{6,96},{7,97},{8,128},{9,1... | collective-permute-start | bytes 1544 | tf_op jit(solution)/shard_map/ppermute | solution.py:269

commit v3 on v2

--- a/solution.py
+++ b/solution.py
@@ -46,24 +46,37 @@
 
 def window_spread(mine):
     parts, lows = lax.axis_size("x"), lax.axis_size("ylo")
-    spread = jnp.where(lax.axis_index("ylo") == 0, mine, jnp.zeros_like(mine))
-    for k in range(1, lows):
-        spread = spread + lax.ppermute(mine, PAIR, [(i * lows, i * lows + k) for i in range(parts)])
-    return spread
-
-
-def window_collected(quarter):
+    return [
+        lax.ppermute(mine, PAIR, [(i * lows, i * lows + k) for i in range(parts)])
+        for k in range(1, lows)
+    ]
+
+
+def window_collected(mine, spread):
+    quarter = jnp.where(lax.axis_index("ylo") == 0, mine, jnp.zeros_like(mine))
+    for piece in spread:
+        quarter = quarter + piece
+    return collected(quarter)
+
+
+def collected(array):
     parts = lax.axis_size("x")
     return lax.all_to_all(
-        jnp.broadcast_to(quarter[None], (parts, *quarter.shape)), "x", 0, 0, tiled=True
+        jnp.broadcast_to(array[None], (parts, *array.shape)), "x", 0, 0, tiled=True
     )
+
+
+def own_half(scalars, factors, f_other, pairs):
+    columns = f_other.shape[2]
+    start = pl.multiple_of(scalars[pairs] * columns, columns)
+    return factors.at[:, :, pl.ds(start, columns)]
 
 
 def half_sums(f_own, f_other, w_own, w_other, chunks, halves):
     pieces, rows, per_piece, depth = w_own.shape
     per_piece = per_piece // BLOCK_Q
     blocks = pieces * per_piece
-    columns = f_own.shape[2]
+    columns = f_other.shape[2]
     span = rows * BLOCK_Q
     count = 0
     for chunk in chunks:
@@ -99,15 +112,16 @@
                 preferred_element_type=F32,
             )
             total = term if total is None else total + term
-    width = f_own.shape[1]
+    width = f_other.shape[1]
     total = total.reshape(count * rows, BLOCK_Q, BLOCK_Q * width)
     q = lax.broadcasted_iota(jnp.int32, total.shape, 1)
     lane = lax.broadcasted_iota(jnp.int32, total.shape, 2)
     return jnp.sum(jnp.where(lane // width == q, total, 0.0), axis=1)
 
 
-def early_kernel(scalars, f_own, f_other, w_own, w_other, *refs):
+def early_kernel(pairs, scalars, factors, f_other, w_own, w_other, *refs):
     chunks, (sums, heads, halves) = refs[:-3], refs[-3:]
+    f_own = own_half(scalars, factors, f_other, pairs)
     sums[...] = half_sums(f_own, f_other, w_own, w_other, chunks, halves)
     count = 0
     for chunk in chunks:
@@ -116,12 +130,13 @@
             count += 1
 
 
-def late_kernel(chunk_count, scalars, f_own, f_other, w_own, w_other, hole_weights, *refs):
+def late_kernel(chunk_count, scalars, factors, f_other, w_own, w_other, hole_weights, *refs):
     chunks, refs = refs[:chunk_count], refs[chunk_count:]
     early, (out, halves, head, hole) = refs[:-4], refs[-4:]
     rows = w_own.shape[1]
-    width = f_own.shape[1]
+    width = f_other.shape[1]
     pairs = hole_weights.shape[0]
+    f_own = own_half(scalars, factors, f_other, pairs)
     sums = [s[...] for s in early[0::2]]
     sums.append(half_sums(f_own, f_other, w_own, w_other, chunks, halves))
     sums = jnp.concatenate(sums, axis=0)
@@ -176,25 +191,24 @@
     amp = amp.reshape(-1, half)
 
     scattered = window_scattered(factors, rows)
+    amp, scattered = lax.optimization_barrier((amp, scattered))
+
+    spread = window_spread(scattered)
+    chunk = collected(amp)
+    chunk, spread = lax.optimization_barrier((chunk, spread))
+    behind, ahead = shifted(chunk, "y", 1), shifted(chunk, "y", -1)
+    window = window_collected(scattered, spread)
+    window_other = swapped(window)
     f_other = swapped(lax.dynamic_slice_in_dim(factors, (1 - core) * half, half, 2))
-    amp, scattered = lax.optimization_barrier((amp, scattered))
-
-    behind, ahead = shifted(amp, "y", 1), shifted(amp, "y", -1)
-    window = window_collected(window_spread(scattered))
-    opposite = shifted(behind, "y", 1)
 
     start = (aux_index * columns) % half
     here = lax.dynamic_slice_in_dim(amp[:rows], start, columns, 1)
     there = lax.dynamic_slice_in_dim(amp[:rows], start + columns * (1 - 2 * core), columns, 1)
     amp_cols = jnp.where(core == yhi, here, swapped(there)).astype(F32)
-
-    chunk = jnp.stack([amp, behind, ahead, opposite])
-    chunk, window, amp_cols = lax.optimization_barrier((chunk, window, amp_cols))
-    window_other = swapped(window)
-    x_behind, x_ahead = shifted(chunk, "x", 1), shifted(chunk, "x", -1)
-    offsets = (0, 1, -1, 2)
+    window_other, amp_cols, f_other = lax.optimization_barrier((window_other, amp_cols, f_other))
+
     order = jnp.stack(
-        [((x - i) % xs) * lows + (ylo - k) % lows for i in offsets for k in offsets]
+        [i * lows + (ylo - k) % lows for k in (0, 1, -1, 2) for i in range(xs)]
     ).astype(jnp.int32)
     place = (pair_index * width) % half
     chosen = (yhi == 0) & (z == 0) & (core == (pair_index * width) // half)
@@ -206,8 +220,7 @@
     blocks = factors.shape[0] // BLOCK_Q
     span = rows * BLOCK_Q
     whole = pl.BlockSpec(memory_space=pltpu.VMEM)
-    own_half = pl.BlockSpec((factors.shape[0], width, half), lambda i, s: (0, 0, s[pairs]))
-    params = pltpu.CompilerParams(vmem_limit_bytes=40 * 1024 * 1024)
+    params = pltpu.CompilerParams(vmem_limit_bytes=44 * 1024 * 1024)
 
     def scratch(count):
         return pltpu.VMEM((count * span, 2 * blocks * half), BF16)
@@ -220,11 +233,11 @@
     def early(*chunks):
         count = sum(c.shape[0] for c in chunks)
         return pl.pallas_call(
-            early_kernel,
+            lambda *refs: early_kernel(pairs, *refs),
             grid_spec=pltpu.PrefetchScalarGridSpec(
                 num_scalar_prefetch=1,
                 grid=(1,),
-                in_specs=[own_half] + [whole] * (3 + len(chunks)),
+                in_specs=[whole] * (4 + len(chunks)),
                 out_specs=[whole, whole],
                 scratch_shapes=[scratch(count)],
             ),
@@ -237,16 +250,16 @@
         )(scalars, factors, f_other, window, window_other, *chunks)
 
     first = early(chunk)
-    x_behind, x_ahead, first = lax.optimization_barrier((x_behind, x_ahead, first))
-    cut = lows // 2
-    last = (shifted(x_behind[:cut], "x", 1), shifted(x_ahead[cut:], "x", -1))
-    done = [*first, *early(x_behind, x_ahead)]
+    behind, ahead, first = lax.optimization_barrier((behind, ahead, first))
+    cut = xs // 2
+    last = (shifted(behind[:cut], "y", 1), shifted(ahead[cut:], "y", -1))
+    done = [*first, *early(behind, ahead)]
     tiles = pl.pallas_call(
         lambda *refs: late_kernel(len(last), *refs),
         grid_spec=pltpu.PrefetchScalarGridSpec(
             num_scalar_prefetch=1,
             grid=(1,),
-            in_specs=[own_half] + [whole] * (4 + len(last) + len(done)),
+            in_specs=[whole] * (5 + len(last) + len(done)),
             out_specs=whole,
             scratch_shapes=[
                 scratch(lows),

time: 171 us -> 170 us (level)
  waiting for transfers between devices: 45.4 us -> 51.6 us
  other arithmetic: 3.48 us -> 0.33 us
  starting transfers between devices: 63.4 us -> 60.9 us
    ppermute x4 -> x0, starting transfers between devices: 11.9 us -> none  [shifted(): lax.ppermute(array, 'x', [(i, (i + by) % count) for i in range(count)])]
    ppermute x3 -> x4, waiting for transfers between devices: 4.46 us -> 11.5 us  [shifted(): lax.ppermute(array, Y, [(index(y), index((y + by) % full)) for y in range...]
    ppermute x4 -> x0, waiting for transfers between devices: 6.55 us -> none  [shifted(): lax.ppermute(array, 'x', [(i, (i + by) % count) for i in range(count)])]
    all_to_all x1 -> x2, starting transfers between devices: 5.6 us -> 11.7 us  [collected(): lax.all_to_all(jnp.broadcast_to(array[None], (parts, *array.shape)), 'x',...]
    ppermute x3, waiting for transfers between devices: 5.85 us -> 11.2 us  [window_scattered(): mine = mine + lax.ppermute(pieces[i], PAIR, [(0, i * lows)])]
    ppermute x3 -> x4, starting transfers between devices: 12.3 us -> 16.8 us  [shifted(): lax.ppermute(array, Y, [(index(y), index((y + by) % full)) for y in range...]
    ppermute x3, waiting for transfers between devices: 3.25 us -> 0.7 us  [swapped(): return lax.ppermute(array, 'core', [(0, 1), (1, 0)])]
    another operation x1 -> x0, other arithmetic: 2.15 us -> none  [per_device(): chunk = jnp.stack([amp, behind, ahead, opposite])]
  transfers between devices with their start and end apart: 19 -> 17, of which waited for: 10 -> 10; matrix products, arithmetic and copies ran while one was open for 6% -> 4% of each run, Pallas kernels for 9% -> 9%
where the time goes in v3:
time: 170 us; the launch traced here: 169 us
  starting transfers between devices  60.9 us (36%)
  waiting for transfers between devices  51.6 us (30%)
  Pallas kernels  21.3 us (13%)
  blocking collectives  19.1 us (11%)
  local copies, waits for them, and re-layouts  13.8 us (8%)
    all_to_all x1, blocking collectives, per_device(): summed = jnp.sum(lax.all_to_all(tiles, AUX, 0, 0, tiled=True), axis=0)  19.1 us
    ppermute x4, starting transfers between devices, shifted(): lax.ppermute(array, Y, [(index(y), index((y + by) % full)) for y in range...  16.8 us
    all_to_all x1, starting transfers between devices, per_device(): lax.all_to_all(sent.reshape(-1, *split.shape[1:]), AUX, 0, 0, tiled=True)  16 us
    pallas_call x2, Pallas kernels, early(): pl.pallas_call(lambda *refs: early_kernel(pairs, *refs), grid_spec=pltpu....  15 us
    ppermute x3, waiting for transfers between devices, window_spread(): lax.ppermute(mine, PAIR, [(i * lows, i * lows + k) for i in range(parts)])  14.8 us
    ppermute x1, waiting for transfers between devices, per_device(): summed = lax.ppermute(summed, AXES, moves)  13 us
    all_to_all x2, starting transfers between devices, collected(): lax.all_to_all(jnp.broadcast_to(array[None], (parts, *array.shape)), 'x',...  11.7 us
    ppermute x4, waiting for transfers between devices, shifted(): lax.ppermute(array, Y, [(index(y), index((y + by) % full)) for y in range...  11.5 us
  transfers between devices with their start and end apart: 17, of which 10 were waited for; matrix products, arithmetic and copies ran while one was open for 4% of the time, Pallas kernels for 9%

profile of v3, /device:TPU:6, one launch (start us, length us, event | category | flops | bytes accessed | tf_op | source)
XLA Modules:
  0.0 168.7 jit_solution(3134384486345570905)
XLA Ops:
  2.1 16.0 %all-to-all-start = ((bf16[32,16,256]{2,1,0:T(8,128)(2,1)}), bf16[32,16,256]{2,1,0:T(8,128)(2,1)S(1)}, u32[]{:S(2)}, u32[]{:S(2)}) async-start(bf16[32,16,256]{2,1,0:T(8,128)(2,1)} %bitcast.22), calls=%async_computation | async-start | bytes 524288 | tf_op jit(solution)/shard_map/all_to_all | solution.py:190
  18.1 1.3 slice_bitcast_fusion
  20.8 1.3 collective-permute-start.2
  22.1 11.1 %collective-permute-done.2 = bf16[6,32,512]{2,0,1:T(8,128)(2,1)S(1)} collective-permute-done((bf16[6,32,512]{2,0,1:T(8,128)(2,1)S(1)}, bf16[6,32,512]{2,0,1:T(8,128)(2,1)S(1)}, u32[]{:S(2)}, u32[]{:S(2)}) %collective-permute-start.2) | collective-permute-done | bytes 196640 | tf_op jit(solution)/shard_map/ppermute | solution.py:43
  33.3 1.0 broadcast_in_dim.6
  34.4 6.9 %all-to-all-start.1 = ((bf16[4,512,256]{2,1,0:T(8,128)(2,1)}), bf16[4,512,256]{2,1,0:T(8,128)(2,1)}, u32[]{:S(2)}, u32[]{:S(2)}) async-start(bf16[4,512,256]{2,1,0:T(8,128)(2,1)} %broadcast_in_dim.6), calls=%async_computation.1 | async-start | bytes 2097152 | tf_op jit(solution)/shard_map/all_to_all | solution.py:64
  41.3 3.1 %constant_dynamic-slice_fusion = bf16[128,32,256]{2,1,0:T(8,128)(2,1)} fusion(bf16[128,32,512]{2,1,0:T(8,128)(2,1)} %refs_1_.5, s32[]{:T(128)S(6)} %select_n.104), kind=kLoop, calls=%fused_computation.12 | loop fusion | bytes 4194308 | tf_op jit(solution)/shard_map/dynamic_slice | solution.py:202
  44.4 1.9 %collective-permute-start.8 = (bf16[128,32,256]{2,1,0:T(8,128)(2,1)}, bf16[128,32,256]{2,1,0:T(8,128)(2,1)S(1)}, u32[]{:S(2)}, u32[]{:S(2)}) collective-permute-start(bf16[128,32,256]{2,1,0:T(8,128)(2,1)} %constant_dynamic-slice_fusion), channel_id=1, source_target_pairs={{0,1},{1,0},{2,3},{3,2},{4,5},{5,4},{6,7},{7,6},{8,9},{9,8},{10,11... | collective-permute-start | bytes 6291464 | tf_op jit(solution)/shard_map/ppermute | solution.py:32
  46.3 2.4 %collective-permute-start.3 = (bf16[6,32,512]{2,0,1:T(8,128)(2,1)S(1)}, bf16[6,32,512]{2,0,1:T(8,128)(2,1)S(1)}, u32[]{:S(2)}, u32[]{:S(2)}) collective-permute-start(bf16[6,32,512]{2,0,1:T(8,128)(2,1)S(1)} %fusion.2), channel_id=1, source_target_pairs={{0,32},{128,160},{256,288},{384,416},{1,33},{129,161},{257,289},{3... | collective-permute-start | bytes 589832 | tf_op jit(solution)/shard_map/ppermute | solution.py:50
  48.7 1.3 collective-permute-start.4
  50.0 1.3 collective-permute-start.5
  51.4 4.0 %collective-permute-done.3 = bf16[6,32,512]{2,0,1:T(8,128)(2,1)S(1)} collective-permute-done((bf16[6,32,512]{2,0,1:T(8,128)(2,1)S(1)}, bf16[6,32,512]{2,0,1:T(8,128)(2,1)S(1)}, u32[]{:S(2)}, u32[]{:S(2)}) %collective-permute-start.3) | collective-permute-done | bytes 196640 | tf_op jit(solution)/shard_map/ppermute | solution.py:50
  55.3 5.6 %collective-permute-done.4 = bf16[6,32,512]{2,0,1:T(8,128)(2,1)S(1)} collective-permute-done((bf16[6,32,512]{2,0,1:T(8,128)(2,1)S(1)}, bf16[6,32,512]{2,0,1:T(8,128)(2,1)S(1)}, u32[]{:S(2)}, u32[]{:S(2)}) %collective-permute-start.4) | collective-permute-done | bytes 196640 | tf_op jit(solution)/shard_map/ppermute | solution.py:50
  60.9 5.2 %collective-permute-done.5 = bf16[6,32,512]{2,0,1:T(8,128)(2,1)S(1)} collective-permute-done((bf16[6,32,512]{2,0,1:T(8,128)(2,1)S(1)}, bf16[6,32,512]{2,0,1:T(8,128)(2,1)S(1)}, u32[]{:S(2)}, u32[]{:S(2)}) %collective-permute-start.5) | collective-permute-done | bytes 196640 | tf_op jit(solution)/shard_map/ppermute | solution.py:50
  67.3 4.8 %all-to-all-start.2 = ((bf16[4,6,32,512]{3,2,1,0:T(8,128)(2,1)}), bf16[4,6,32,512]{3,2,1,0:T(8,128)(2,1)S(1)}, u32[]{:S(2)}, u32[]{:S(2)}) async-start(bf16[4,6,32,512]{3,2,1,0:T(8,128)(2,1)} %broadcast_in_dim.7), calls=%async_computation.2 | async-start | bytes 1572864 | tf_op jit(solution)/shard_map/all_to_all | solution.py:64
  72.1 7.6 %collective-permute-start.10 = (bf16[4,512,256]{2,1,0:T(8,128)(2,1)}, bf16[4,512,256]{2,1,0:T(8,128)(2,1)}, u32[]{:S(2)}, u32[]{:S(2)}) collective-permute-start(bf16[4,512,256]{2,1,0:T(8,128)(2,1)} %all-to-all-done.1.refs_5_), channel_id=1, source_target_pairs={{0,112},{32,0},{64,32},{96,64},{16,96},{48,16},{80,48},{112,80},{1... | collective-permute-start | bytes 3145736 | tf_op jit(solution)/shard_map/ppermute | solution.py:28
  79.7 1.9 %collective-permute-start.9 = (bf16[4,512,256]{2,1,0:T(8,128)(2,1)}, bf16[4,512,256]{2,1,0:T(8,128)(2,1)}, u32[]{:S(2)}, u32[]{:S(2)}) collective-permute-start(bf16[4,512,256]{2,1,0:T(8,128)(2,1)} %all-to-all-done.1.refs_5_), channel_id=1, source_target_pairs={{0,32},{32,64},{64,96},{96,16},{16,48},{48,80},{80,112},{112,0},{1... | collective-permute-start | bytes 3145736 | tf_op jit(solution)/shard_map/ppermute | solution.py:28
  82.2 1.9 %collective-permute-start.6 = (bf16[4,6,32,512]{3,2,1,0:T(8,128)(2,1)S(1)}, bf16[4,6,32,512]{3,2,1,0:T(8,128)(2,1)}, u32[]{:S(2)}, u32[]{:S(2)}) collective-permute-start(bf16[4,6,32,512]{3,2,1,0:T(8,128)(2,1)S(1)} %all-to-all-done.2.refs_3_), channel_id=1, source_target_pairs={{0,1},{1,0},{2,3},{3,2},{4,5},{5,4},{6,7},{7,6},{8,9},{9,8},{10,11... | collective-permute-start | bytes 2359304 | tf_op jit(solution)/shard_map/ppermute | solution.py:32
  84.3 2.4 %collective-permute-start.7 = (bf16[6,16]{1,0:T(8,128)(2,1)S(1)}, bf16[6,16]{1,0:T(8,128)(2,1)S(1)}, u32[]{:S(2)}, u32[]{:S(2)}) collective-permute-start(bf16[6,16]{1,0:T(8,128)(2,1)S(1)} %constant_dynamic-slice_fusion.1), channel_id=1, source_target_pairs={{0,1},{1,0},{2,3},{3,2},{4,5},{5,4},{6,7},{7,6},{8,9},{9,8},{10,11... | collective-permute-start | bytes 584 | tf_op jit(solution)/shard_map/ppermute | solution.py:32
  87.6 2.2 %copy-done = bf16[128,32,512]{2,1,0:T(8,128)(2,1)S(1)} copy-done((bf16[128,32,512]{2,1,0:T(8,128)(2,1)S(1)}, bf16[128,32,512]{2,1,0:T(8,128)(2,1)}, u32[]{:S(2)}) %copy-start) | copy-done | bytes 4194328
  89.8 6.2 %shard_map.77 = (f32[24,256]{1,0:T(8,128)S(1)}, f32[4,8,256]{2,1,0:T(8,128)S(1)}) custom-call(s32[19]{0:T(128)S(1)} %concatenate.3.refs_0_, bf16[128,32,512]{2,1,0:T(8,128)(2,1)S(1)} %copy-done, bf16[128,32,256]{2,1,0:T(8,128)(2,1)S(1)} %collective-permute-done.8.refs_2_, bf16[4,6,32,512]{3,2,1,0:T(8,128)(2,1)S(1)} %all-to-all-done.2.refs_3_, ...), custom_call_target="tpu_custom_call" | custom-call | flops 2420000000 | bytes 8000000 | tf_op jit(solution)/shard_map/pallas_call | solution.py:235
  96.0 6.0 %collective-permute-done.10.refs_6_ = bf16[4,512,256]{2,1,0:T(8,128)(2,1)} collective-permute-done((bf16[4,512,256]{2,1,0:T(8,128)(2,1)}, bf16[4,512,256]{2,1,0:T(8,128)(2,1)}, u32[]{:S(2)}, u32[]{:S(2)}) %collective-permute-start.10) | collective-permute-done | bytes 1048608 | tf_op jit(solution)/shard_map/ppermute | solution.py:28
  101.9 5.3 %collective-permute-done.9.refs_5_ = bf16[4,512,256]{2,1,0:T(8,128)(2,1)} collective-permute-done((bf16[4,512,256]{2,1,0:T(8,128)(2,1)}, bf16[4,512,256]{2,1,0:T(8,128)(2,1)}, u32[]{:S(2)}, u32[]{:S(2)}) %collective-permute-start.9) | collective-permute-done | bytes 1048608 | tf_op jit(solution)/shard_map/ppermute | solution.py:28
  107.3 1.1 slice.45
  108.4 1.9 %collective-permute-start.11 = (bf16[2,512,256]{2,1,0:T(8,128)(2,1)S(1)}, bf16[2,512,256]{2,1,0:T(8,128)(2,1)S(1)}, u32[]{:S(2)}, u32[]{:S(2)}) collective-permute-start(bf16[2,512,256]{2,1,0:T(8,128)(2,1)S(1)} %slice.45), channel_id=1, source_target_pairs={{0,32},{32,64},{64,96},{96,16},{16,48},{48,80},{80,112},{112,0},{1... | collective-permute-start | bytes 1572872 | tf_op jit(solution)/shard_map/ppermute | solution.py:28
  110.3 1.1 slice.46
  111.4 5.3 %collective-permute-start.12 = (bf16[2,512,256]{2,1,0:T(8,128)(2,1)S(1)}, bf16[2,512,256]{2,1,0:T(8,128)(2,1)S(1)}, u32[]{:S(2)}, u32[]{:S(2)}) collective-permute-start(bf16[2,512,256]{2,1,0:T(8,128)(2,1)S(1)} %slice.46), channel_id=1, source_target_pairs={{0,112},{32,0},{64,32},{96,64},{16,96},{48,16},{80,48},{112,80},{1... | collective-permute-start | bytes 1572872 | tf_op jit(solution)/shard_map/ppermute | solution.py:28
  116.7 8.9 %shard_map.78 = (f32[48,256]{1,0:T(8,128)S(1)}, f32[8,8,256]{2,1,0:T(8,128)S(1)}) custom-call(s32[19]{0:T(128)S(1)} %concatenate.3.refs_0_, bf16[128,32,512]{2,1,0:T(8,128)(2,1)S(1)} %copy-done, bf16[128,32,256]{2,1,0:T(8,128)(2,1)S(1)} %collective-permute-done.8.refs_2_, bf16[4,6,32,512]{3,2,1,0:T(8,128)(2,1)S(1)} %all-to-all-done.2.refs_3_, ...), custom_call_target="tpu_custom_call" | custom-call | flops 4840000000 | bytes 8000000 | tf_op jit(solution)/shard_map/pallas_call | solution.py:235
  125.7 6.3 %shard_map.79 = f32[32,1,128]{2,1,0:T(1,128)S(1)} custom-call(s32[19]{0:T(128)S(1)} %concatenate.3.refs_0_, bf16[128,32,512]{2,1,0:T(8,128)(2,1)S(1)} %copy-done, bf16[128,32,256]{2,1,0:T(8,128)(2,1)S(1)} %collective-permute-done.8.refs_2_, bf16[4,6,32,512]{3,2,1,0:T(8,128)(2,1)S(1)} %all-to-all-done.2.refs_3_, ...), custom_call_target="tpu_custom_call" | custom-call | flops 2420000000 | bytes 8000000 | tf_op jit(solution)/shard_map/pallas_call | solution.py:257
  132.0 19.1 %all_to_all.20 = f32[32,1,128]{2,1,0:T(1,128)S(1)} all-to-all(f32[32,1,128]{2,1,0:T(1,128)S(1)} %shard_map.79), channel_id=1, replica_groups=mesh['x'=4,'ylo'=4,'yhi'=2,'z'=8,'core'=2] {'yhi','z','core'}, dimensions={0} | all-to-all | bytes 32768 | tf_op jit(solution)/shard_map/all_to_all | solution.py:275
  151.1 2.5 %collective-permute-start.13 = (f32[1,128]{1,0:T(1,128)S(1)}, f32[1,128]{1,0:T(1,128)S(1)}, u32[]{:S(2)}, u32[]{:S(2)}) collective-permute-start(f32[1,128]{1,0:T(1,128)S(1)} %bitcast.36), channel_id=1, source_target_pairs={{0,0},{1,1},{2,32},{3,33},{4,64},{5,65},{6,96},{7,97},{8,128},{9,1... | collective-permute-start | bytes 1544 | tf_op jit(solution)/shard_map/ppermute | solution.py:282
  154.4 13.0 %collective-permute-done.13 = f32[1,128]{1,0:T(1,128)S(1)} collective-permute-done((f32[1,128]{1,0:T(1,128)S(1)}, f32[1,128]{1,0:T(1,128)S(1)}, u32[]{:S(2)}, u32[]{:S(2)}) %collective-permute-start.13) | collective-permute-done | bytes 544 | tf_op jit(solution)/shard_map/ppermute | solution.py:282
  (40 shorter events, 7.2 us)
Async XLA Ops:
  2.1 31.3 %all-to-all-start = ((bf16[32,16,256]{2,1,0:T(8,128)(2,1)}), bf16[32,16,256]{2,1,0:T(8,128)(2,1)S(1)}, u32[]{:S(2)}, u32[]{:S(2)}) async-start(bf16[32,16,256]{2,1,0:T(8,128)(2,1)} %bitcast.22), calls=%async_computation | async-start | bytes 524288 | tf_op jit(solution)/shard_map/all_to_all | solution.py:190
  19.4 2.7 %collective-permute-start = (bf16[6,32,512]{2,0,1:T(8,128)(2,1)S(1)}, bf16[6,32,512]{2,0,1:T(8,128)(2,1)S(1)}, u32[]{:S(2)}, u32[]{:S(2)}) collective-permute-start(bf16[6,32,512]{2,0,1:T(8,128)(2,1)S(1)} %get-tuple-element.42), channel_id=1, source_target_pairs={{0,128},{1,129},{2,130},{3,131},{4,132},{5,133},{6,134},{7,135},{8... | collective-permute-start | bytes 589832 | tf_op jit(solution)/shard_map/ppermute | solution.py:43
  20.1 2.0 %collective-permute-start.1 = (bf16[6,32,512]{2,0,1:T(8,128)(2,1)S(1)}, bf16[6,32,512]{2,0,1:T(8,128)(2,1)S(1)}, u32[]{:S(2)}, u32[]{:S(2)}) collective-permute-start(bf16[6,32,512]{2,0,1:T(8,128)(2,1)S(1)} %get-tuple-element.44), channel_id=1, source_target_pairs={{0,256},{1,257},{2,258},{3,259},{4,260},{5,261},{6,262},{7,263},{8... | collective-permute-start | bytes 589832 | tf_op jit(solution)/shard_map/ppermute | solution.py:43
  20.8 12.5 %collective-permute-start.2 = (bf16[6,32,512]{2,0,1:T(8,128)(2,1)S(1)}, bf16[6,32,512]{2,0,1:T(8,128)(2,1)S(1)}, u32[]{:S(2)}, u32[]{:S(2)}) collective-permute-start(bf16[6,32,512]{2,0,1:T(8,128)(2,1)S(1)} %get-tuple-element.43), channel_id=1, source_target_pairs={{0,384},{1,385},{2,386},{3,387},{4,388},{5,389},{6,390},{7,391},{8... | collective-permute-start | bytes 589832 | tf_op jit(solution)/shard_map/ppermute | solution.py:43
  34.4 31.8 %all-to-all-start.1 = ((bf16[4,512,256]{2,1,0:T(8,128)(2,1)}), bf16[4,512,256]{2,1,0:T(8,128)(2,1)}, u32[]{:S(2)}, u32[]{:S(2)}) async-start(bf16[4,512,256]{2,1,0:T(8,128)(2,1)} %broadcast_in_dim.6), calls=%async_computation.1 | async-start | bytes 2097152 | tf_op jit(solution)/shard_map/all_to_all | solution.py:64
  44.4 43.2 %collective-permute-start.8 = (bf16[128,32,256]{2,1,0:T(8,128)(2,1)}, bf16[128,32,256]{2,1,0:T(8,128)(2,1)S(1)}, u32[]{:S(2)}, u32[]{:S(2)}) collective-permute-start(bf16[128,32,256]{2,1,0:T(8,128)(2,1)} %constant_dynamic-slice_fusion), channel_id=1, source_target_pairs={{0,1},{1,0},{2,3},{3,2},{4,5},{5,4},{6,7},{7,6},{8,9},{9,8},{10,11... | collective-permute-start | bytes 6291464 | tf_op jit(solution)/shard_map/ppermute | solution.py:32
  46.3 9.0 %collective-permute-start.3 = (bf16[6,32,512]{2,0,1:T(8,128)(2,1)S(1)}, bf16[6,32,512]{2,0,1:T(8,128)(2,1)S(1)}, u32[]{:S(2)}, u32[]{:S(2)}) collective-permute-start(bf16[6,32,512]{2,0,1:T(8,128)(2,1)S(1)} %fusion.2), channel_id=1, source_target_pairs={{0,32},{128,160},{256,288},{384,416},{1,33},{129,161},{257,289},{3... | collective-permute-start | bytes 589832 | tf_op jit(solution)/shard_map/ppermute | solution.py:50
  48.7 12.2 %collective-permute-start.4 = (bf16[6,32,512]{2,0,1:T(8,128)(2,1)S(1)}, bf16[6,32,512]{2,0,1:T(8,128)(2,1)S(1)}, u32[]{:S(2)}, u32[]{:S(2)}) collective-permute-start(bf16[6,32,512]{2,0,1:T(8,128)(2,1)S(1)} %fusion.2), channel_id=1, source_target_pairs={{0,64},{128,192},{256,320},{384,448},{1,65},{129,193},{257,321},{3... | collective-permute-start | bytes 589832 | tf_op jit(solution)/shard_map/ppermute | solution.py:50
  50.0 16.1 %collective-permute-start.5 = (bf16[6,32,512]{2,0,1:T(8,128)(2,1)S(1)}, bf16[6,32,512]{2,0,1:T(8,128)(2,1)S(1)}, u32[]{:S(2)}, u32[]{:S(2)}) collective-permute-start(bf16[6,32,512]{2,0,1:T(8,128)(2,1)S(1)} %fusion.2), channel_id=1, source_target_pairs={{0,96},{128,224},{256,352},{384,480},{1,97},{129,225},{257,353},{3... | collective-permute-start | bytes 589832 | tf_op jit(solution)/shard_map/ppermute | solution.py:50
  67.3 14.9 %all-to-all-start.2 = ((bf16[4,6,32,512]{3,2,1,0:T(8,128)(2,1)}), bf16[4,6,32,512]{3,2,1,0:T(8,128)(2,1)S(1)}, u32[]{:S(2)}, u32[]{:S(2)}) async-start(bf16[4,6,32,512]{3,2,1,0:T(8,128)(2,1)} %broadcast_in_dim.7), calls=%async_computation.2 | async-start | bytes 1572864 | tf_op jit(solution)/shard_map/all_to_all | solution.py:64
  72.1 29.9 %collective-permute-start.10 = (bf16[4,512,256]{2,1,0:T(8,128)(2,1)}, bf16[4,512,256]{2,1,0:T(8,128)(2,1)}, u32[]{:S(2)}, u32[]{:S(2)}) collective-permute-start(bf16[4,512,256]{2,1,0:T(8,128)(2,1)} %all-to-all-done.1.refs_5_), channel_id=1, source_target_pairs={{0,112},{32,0},{64,32},{96,64},{16,96},{48,16},{80,48},{112,80},{1... | collective-permute-start | bytes 3145736 | tf_op jit(solution)/shard_map/ppermute | solution.py:28
  79.7 27.6 %collective-permute-start.9 = (bf16[4,512,256]{2,1,0:T(8,128)(2,1)}, bf16[4,512,256]{2,1,0:T(8,128)(2,1)}, u32[]{:S(2)}, u32[]{:S(2)}) collective-permute-start(bf16[4,512,256]{2,1,0:T(8,128)(2,1)} %all-to-all-done.1.refs_5_), channel_id=1, source_target_pairs={{0,32},{32,64},{64,96},{96,16},{16,48},{48,80},{80,112},{112,0},{1... | collective-permute-start | bytes 3145736 | tf_op jit(solution)/shard_map/ppermute | solution.py:28
  82.2 5.4 %collective-permute-start.6 = (bf16[4,6,32,512]{3,2,1,0:T(8,128)(2,1)S(1)}, bf16[4,6,32,512]{3,2,1,0:T(8,128)(2,1)}, u32[]{:S(2)}, u32[]{:S(2)}) collective-permute-start(bf16[4,6,32,512]{3,2,1,0:T(8,128)(2,1)S(1)} %all-to-all-done.2.refs_3_), channel_id=1, source_target_pairs={{0,1},{1,0},{2,3},{3,2},{4,5},{5,4},{6,7},{7,6},{8,9},{9,8},{10,11... | collective-permute-start | bytes 2359304 | tf_op jit(solution)/shard_map/ppermute | solution.py:32
  84.3 3.2 %collective-permute-start.7 = (bf16[6,16]{1,0:T(8,128)(2,1)S(1)}, bf16[6,16]{1,0:T(8,128)(2,1)S(1)}, u32[]{:S(2)}, u32[]{:S(2)}) collective-permute-start(bf16[6,16]{1,0:T(8,128)(2,1)S(1)} %constant_dynamic-slice_fusion.1), channel_id=1, source_target_pairs={{0,1},{1,0},{2,3},{3,2},{4,5},{5,4},{6,7},{7,6},{8,9},{9,8},{10,11... | collective-permute-start | bytes 584 | tf_op jit(solution)/shard_map/ppermute | solution.py:32
  87.6 2.2 %copy-start = (bf16[128,32,512]{2,1,0:T(8,128)(2,1)S(1)}, bf16[128,32,512]{2,1,0:T(8,128)(2,1)}, u32[]{:S(2)}) copy-start(bf16[128,32,512]{2,1,0:T(8,128)(2,1)} %refs_1_.5) | copy-start | bytes 12582916
  108.4 17.2 %collective-permute-start.11 = (bf16[2,512,256]{2,1,0:T(8,128)(2,1)S(1)}, bf16[2,512,256]{2,1,0:T(8,128)(2,1)S(1)}, u32[]{:S(2)}, u32[]{:S(2)}) collective-permute-start(bf16[2,512,256]{2,1,0:T(8,128)(2,1)S(1)} %slice.45), channel_id=1, source_target_pairs={{0,32},{32,64},{64,96},{96,16},{16,48},{48,80},{80,112},{112,0},{1... | collective-permute-start | bytes 1572872 | tf_op jit(solution)/shard_map/ppermute | solution.py:28
  111.4 14.4 %copy-start.1 = (f32[16,16]{1,0:T(8,128)S(1)}, f32[16,16]{1,0:T(8,128)}, u32[]{:S(2)}) copy-start(f32[16,16]{1,0:T(8,128)} %refs_5_.1) | copy-start | bytes 3076
  111.4 14.3 %collective-permute-start.12 = (bf16[2,512,256]{2,1,0:T(8,128)(2,1)S(1)}, bf16[2,512,256]{2,1,0:T(8,128)(2,1)S(1)}, u32[]{:S(2)}, u32[]{:S(2)}) collective-permute-start(bf16[2,512,256]{2,1,0:T(8,128)(2,1)S(1)} %slice.46), channel_id=1, source_target_pairs={{0,112},{32,0},{64,32},{96,64},{16,96},{48,16},{80,48},{112,80},{1... | collective-permute-start | bytes 1572872 | tf_op jit(solution)/shard_map/ppermute | solution.py:28
  125.7 27.9 %copy-start.3 = (f32[512]{0:T(512)S(1)}, f32[512]{0:T(512)}, u32[]{:S(2)}) copy-start(f32[512]{0:T(512)} %param.10) | copy-start | bytes 6148
  125.7 41.8 %copy-start.2 = (f32[1,6,16]{2,0,1:T(1,128)S(1)}, f32[1,6,16]{2,0,1:T(1,128)}, u32[]{:S(2)}) copy-start(f32[1,6,16]{2,0,1:T(1,128)} %param.9) | copy-start | bytes 1156
  125.7 41.8 %slice-start = ((f32[512]{0:T(512)}), f32[6]{0:T(128)S(1)}, s32[]{:S(2)}) async-start(f32[512]{0:T(512)} %param.10), calls=%async_computation.4 | async-start | bytes 1024 | tf_op jit(solution)/shard_map/slice | solution.py:288
  151.1 16.2 %collective-permute-start.13 = (f32[1,128]{1,0:T(1,128)S(1)}, f32[1,128]{1,0:T(1,128)S(1)}, u32[]{:S(2)}, u32[]{:S(2)}) collective-permute-start(f32[1,128]{1,0:T(1,128)S(1)} %bitcast.36), channel_id=1, source_target_pairs={{0,0},{1,1},{2,32},{3,33},{4,64},{5,65},{6,96},{7,97},{8,128},{9,1... | collective-permute-start | bytes 1544 | tf_op jit(solution)/shard_map/ppermute | solution.py:282

commit v4 on v3

--- a/solution.py
+++ b/solution.py
@@ -52,11 +52,11 @@
     ]
 
 
-def window_collected(mine, spread):
+def window_quarter(mine, spread):
     quarter = jnp.where(lax.axis_index("ylo") == 0, mine, jnp.zeros_like(mine))
     for piece in spread:
         quarter = quarter + piece
-    return collected(quarter)
+    return quarter
 
 
 def collected(array):
@@ -66,22 +66,36 @@
     )
 
 
-def own_half(scalars, factors, f_other, pairs):
-    columns = f_other.shape[2]
+def fetched(scalars, pairs, factors, f_other, chunks, own, other, amps, arrived):
+    columns = other.shape[2]
     start = pl.multiple_of(scalars[pairs] * columns, columns)
-    return factors.at[:, :, pl.ds(start, columns)]
-
-
-def half_sums(f_own, f_other, w_own, w_other, chunks, halves):
+    taken, at = [], 0
+    for i, chunk in enumerate(chunks):
+        count = chunk.shape[0]
+        taken.append(
+            pltpu.make_async_copy(chunk, amps.at[at : at + count], arrived.at[2 + i])
+        )
+        at += count
+    copies = (
+        pltpu.make_async_copy(factors.at[:, :, pl.ds(start, columns)], own, arrived.at[0]),
+        pltpu.make_async_copy(f_other, other, arrived.at[1]),
+    )
+    for copy in (*taken, *copies):
+        copy.start()
+    return taken, copies
+
+
+def half_sums(taken, copies, f_own, f_other, w_own, w_other, chunks, amps, halves):
     pieces, rows, per_piece, depth = w_own.shape
     per_piece = per_piece // BLOCK_Q
     blocks = pieces * per_piece
     columns = f_other.shape[2]
     span = rows * BLOCK_Q
     count = 0
-    for chunk in chunks:
-        for k in range(chunk.shape[0]):
-            amp = chunk[k]
+    for copy, chunk in zip(taken, chunks):
+        copy.wait()
+        for _ in range(chunk.shape[0]):
+            amp = amps[count]
             for which, w in enumerate((w_own, w_other)):
                 got = jnp.dot(
                     w[...].reshape(blocks * span, depth), amp, preferred_element_type=F32
@@ -93,6 +107,8 @@
                             got[piece, :, b].reshape(span, columns).astype(BF16)
                         )
             count += 1
+    for copy in copies:
+        copy.wait()
     total = None
     group = 8
     for which, f in enumerate((f_own, f_other)):
@@ -120,25 +136,21 @@
 
 
 def early_kernel(pairs, scalars, factors, f_other, w_own, w_other, *refs):
-    chunks, (sums, heads, halves) = refs[:-3], refs[-3:]
-    f_own = own_half(scalars, factors, f_other, pairs)
-    sums[...] = half_sums(f_own, f_other, w_own, w_other, chunks, halves)
-    count = 0
-    for chunk in chunks:
-        for k in range(chunk.shape[0]):
-            heads[count] = chunk[k, : heads.shape[1], :].astype(F32)
-            count += 1
+    chunks, (sums, heads, halves, own, other, amps, arrived) = refs[:-7], refs[-7:]
+    taken, copies = fetched(scalars, pairs, factors, f_other, chunks, own, other, amps, arrived)
+    sums[...] = half_sums(taken, copies, own, other, w_own, w_other, chunks, amps, halves)
+    heads[...] = amps[:, : heads.shape[1], :].astype(F32)
 
 
 def late_kernel(chunk_count, scalars, factors, f_other, w_own, w_other, hole_weights, *refs):
     chunks, refs = refs[:chunk_count], refs[chunk_count:]
-    early, (out, halves, head, hole) = refs[:-4], refs[-4:]
+    early, (out, halves, own, other, amps, arrived, head, hole) = refs[:-8], refs[-8:]
     rows = w_own.shape[1]
     width = f_other.shape[1]
     pairs = hole_weights.shape[0]
-    f_own = own_half(scalars, factors, f_other, pairs)
+    taken, copies = fetched(scalars, pairs, factors, f_other, chunks, own, other, amps, arrived)
     sums = [s[...] for s in early[0::2]]
-    sums.append(half_sums(f_own, f_other, w_own, w_other, chunks, halves))
+    sums.append(half_sums(taken, copies, own, other, w_own, w_other, chunks, amps, halves))
     sums = jnp.concatenate(sums, axis=0)
 
     local = 0
@@ -146,10 +158,9 @@
         for k in range(heads.shape[0]):
             head[pl.ds(scalars[local], 1)] = heads[k][None]
             local += 1
-    for chunk in chunks:
-        for k in range(chunk.shape[0]):
-            head[pl.ds(scalars[local], 1)] = chunk[k, : head.shape[1], :].astype(F32)[None]
-            local += 1
+    for k in range(amps.shape[0]):
+        head[pl.ds(scalars[local], 1)] = amps[k, : head.shape[1], :].astype(F32)[None]
+        local += 1
     for a in range(rows):
         hole[:, a, :] = jnp.dot(
             hole_weights[...], head[:, a, :], precision=lax.Precision.HIGHEST,
@@ -191,15 +202,16 @@
     amp = amp.reshape(-1, half)
 
     scattered = window_scattered(factors, rows)
-    amp, scattered = lax.optimization_barrier((amp, scattered))
+    f_other = lax.dynamic_slice_in_dim(factors, (1 - core) * half, half, 2)
+    amp, scattered, f_other = lax.optimization_barrier((amp, scattered, f_other))
+    f_other = swapped(f_other)
 
     spread = window_spread(scattered)
     chunk = collected(amp)
-    chunk, spread = lax.optimization_barrier((chunk, spread))
+    chunk, spread[0] = lax.optimization_barrier((chunk, spread[0]))
     behind, ahead = shifted(chunk, "y", 1), shifted(chunk, "y", -1)
-    window = window_collected(scattered, spread)
+    window = collected(window_quarter(scattered, spread))
     window_other = swapped(window)
-    f_other = swapped(lax.dynamic_slice_in_dim(factors, (1 - core) * half, half, 2))
 
     start = (aux_index * columns) % half
     here = lax.dynamic_slice_in_dim(amp[:rows], start, columns, 1)
@@ -220,14 +232,18 @@
     blocks = factors.shape[0] // BLOCK_Q
     span = rows * BLOCK_Q
     whole = pl.BlockSpec(memory_space=pltpu.VMEM)
-    params = pltpu.CompilerParams(vmem_limit_bytes=44 * 1024 * 1024)
-
-    def scratch(count):
-        return pltpu.VMEM((count * span, 2 * blocks * half), BF16)
+    afar = pl.BlockSpec(memory_space=pltpu.HBM)
+    params = pltpu.CompilerParams(vmem_limit_bytes=56 * 1024 * 1024)
+
+    def scratch(count, arrays):
+        block = pltpu.VMEM((factors.shape[0], width, half), BF16)
+        kept = pltpu.VMEM((count * span, 2 * blocks * half), BF16)
+        amps = pltpu.VMEM((count, *amp.shape), BF16)
+        return [kept, block, block, amps, pltpu.SemaphoreType.DMA((2 + arrays,))]
 
     def cost(count):
         return pl.CostEstimate(
-            flops=605_000_000 * count, bytes_accessed=8_000_000, transcendentals=0
+            flops=1_000_000 * count, bytes_accessed=100_000, transcendentals=0
         )
 
     def early(*chunks):
@@ -237,9 +253,9 @@
             grid_spec=pltpu.PrefetchScalarGridSpec(
                 num_scalar_prefetch=1,
                 grid=(1,),
-                in_specs=[whole] * (4 + len(chunks)),
+                in_specs=[afar, afar, whole, whole] + [afar] * len(chunks),
                 out_specs=[whole, whole],
-                scratch_shapes=[scratch(count)],
+                scratch_shapes=scratch(count, len(chunks)),
             ),
             out_shape=[
                 jax.ShapeDtypeStruct((count * rows, BLOCK_Q * width), F32),
@@ -249,20 +265,20 @@
             cost_estimate=cost(count),
         )(scalars, factors, f_other, window, window_other, *chunks)
 
-    first = early(chunk)
-    behind, ahead, first = lax.optimization_barrier((behind, ahead, first))
     cut = xs // 2
     last = (shifted(behind[:cut], "y", 1), shifted(ahead[cut:], "y", -1))
-    done = [*first, *early(behind, ahead)]
+    done = early(chunk, behind, ahead)
     tiles = pl.pallas_call(
         lambda *refs: late_kernel(len(last), *refs),
         grid_spec=pltpu.PrefetchScalarGridSpec(
             num_scalar_prefetch=1,
             grid=(1,),
-            in_specs=[whole] * (5 + len(last) + len(done)),
+            in_specs=[afar, afar, whole, whole, whole]
+            + [afar] * len(last)
+            + [whole] * len(done),
             out_specs=whole,
             scratch_shapes=[
-                scratch(lows),
+                *scratch(lows, len(last)),
                 pltpu.VMEM((pairs, head_rows, half), F32),
                 pltpu.VMEM((pairs, head_rows, half), F32),
             ],

time: 170 us -> 169 us (level)
  blocking collectives: 19.1 us -> 35.5 us
  waiting for transfers between devices: 51.6 us -> 35.4 us
  starting transfers between devices: 60.9 us -> 54.3 us
  Pallas kernels: 21.3 us -> 26.4 us
    all_to_all x0 -> x1, blocking collectives: none -> 14.3 us  [collected(): lax.all_to_all(jnp.broadcast_to(array[None], (parts, *array.shape)), 'x',...]
    ppermute x3, waiting for transfers between devices: 14.8 us -> 6.88 us  [window_spread(): lax.ppermute(mine, PAIR, [(i * lows, i * lows + k) for i in range(parts)])]
    ppermute x4, waiting for transfers between devices: 11.5 us -> 4.8 us  [shifted(): lax.ppermute(array, Y, [(index(y), index((y + by) % full)) for y in range...]
    all_to_all x2 -> x1, starting transfers between devices: 11.7 us -> 6.89 us  [collected(): lax.all_to_all(jnp.broadcast_to(array[None], (parts, *array.shape)), 'x',...]
    pallas_call x1, Pallas kernels: 6.25 us -> 9.6 us  [per_device(): pl.pallas_call(lambda *refs: late_kernel(len(last), *refs), grid_spec=plt...]
    ppermute x3, waiting for transfers between devices: 11.2 us -> 8.06 us  [window_scattered(): mine = mine + lax.ppermute(pieces[i], PAIR, [(0, i * lows)])]
    all_to_all x1, blocking collectives: 19.1 us -> 21.2 us  [per_device(): summed = jnp.sum(lax.all_to_all(tiles, AUX, 0, 0, tiled=True), axis=0)]
    pallas_call x2 -> x1, Pallas kernels: 15 us -> 16.8 us  [early(): pl.pallas_call(lambda *refs: early_kernel(pairs, *refs), grid_spec=pltpu....]
  transfers between devices with their start and end apart: 17 -> 16, of which waited for: 10 -> 7; matrix products, arithmetic and copies ran while one was open for 4% -> 5% of each run, Pallas kernels for 9% -> 10%
where the time goes in v4:
time: 169 us; the launch traced here: 168 us
  starting transfers between devices  54.3 us (32%)
  blocking collectives  35.5 us (21%)
  waiting for transfers between devices  35.4 us (21%)
  Pallas kernels  26.4 us (16%)
  local copies, waits for them, and re-layouts  13.4 us (8%)
  between operations  1.69 us (1%)
    all_to_all x1, blocking collectives, per_device(): summed = jnp.sum(lax.all_to_all(tiles, AUX, 0, 0, tiled=True), axis=0)  21.2 us
    pallas_call x1, Pallas kernels, early(): pl.pallas_call(lambda *refs: early_kernel(pairs, *refs), grid_spec=pltpu....  16.8 us
    all_to_all x1, starting transfers between devices, per_device(): lax.all_to_all(sent.reshape(-1, *split.shape[1:]), AUX, 0, 0, tiled=True)  16 us
    ppermute x4, starting transfers between devices, shifted(): lax.ppermute(array, Y, [(index(y), index((y + by) % full)) for y in range...  15.1 us
    all_to_all x1, blocking collectives, collected(): lax.all_to_all(jnp.broadcast_to(array[None], (parts, *array.shape)), 'x',...  14.3 us
    ppermute x1, waiting for transfers between devices, per_device(): summed = lax.ppermute(summed, AXES, moves)  13.6 us
    pallas_call x1, Pallas kernels, per_device(): pl.pallas_call(lambda *refs: late_kernel(len(last), *refs), grid_spec=plt...  9.6 us
    ppermute x3, waiting for transfers between devices, window_scattered(): mine = mine + lax.ppermute(pieces[i], PAIR, [(0, i * lows)])  8.06 us
  transfers between devices with their start and end apart: 16, of which 7 were waited for; matrix products, arithmetic and copies ran while one was open for 5% of the time, Pallas kernels for 10%

profile of v4, /device:TPU:6, one launch (start us, length us, event | category | flops | bytes accessed | tf_op | source)
XLA Modules:
  0.0 167.9 jit_solution(11236540905897057926)
XLA Ops:
  2.1 16.0 %all-to-all-start = ((bf16[32,16,256]{2,1,0:T(8,128)(2,1)}), bf16[32,16,256]{2,1,0:T(8,128)(2,1)S(1)}, u32[]{:S(2)}, u32[]{:S(2)}) async-start(bf16[32,16,256]{2,1,0:T(8,128)(2,1)} %bitcast.22), calls=%async_computation | async-start | bytes 524288 | tf_op jit(solution)/shard_map/all_to_all | solution.py:201
  18.1 1.3 slice_bitcast_fusion
  20.8 1.3 collective-permute-start.2
  22.1 3.1 %constant_dynamic-slice_fusion.1 = bf16[128,32,256]{2,1,0:T(8,128)(2,1)} fusion(bf16[128,32,512]{2,1,0:T(8,128)(2,1)} %refs_1_.3, s32[]{:T(128)S(6)} %select_n.98), kind=kLoop, calls=%fused_computation.13 | loop fusion | bytes 4194308 | tf_op jit(solution)/shard_map/dynamic_slice | solution.py:205
  25.2 8.1 %collective-permute-done.2 = bf16[6,32,512]{2,0,1:T(8,128)(2,1)S(1)} collective-permute-done((bf16[6,32,512]{2,0,1:T(8,128)(2,1)S(1)}, bf16[6,32,512]{2,0,1:T(8,128)(2,1)S(1)}, u32[]{:S(2)}, u32[]{:S(2)}) %collective-permute-start.2) | collective-permute-done | bytes 196640 | tf_op jit(solution)/shard_map/ppermute | solution.py:43
  33.3 1.0 broadcast_in_dim.6
  34.4 6.9 %all-to-all-start.1 = ((bf16[4,512,256]{2,1,0:T(8,128)(2,1)}), bf16[4,512,256]{2,1,0:T(8,128)(2,1)}, u32[]{:S(2)}, u32[]{:S(2)}) async-start(bf16[4,512,256]{2,1,0:T(8,128)(2,1)} %broadcast_in_dim.6), calls=%async_computation.1 | async-start | bytes 2097152 | tf_op jit(solution)/shard_map/all_to_all | solution.py:64
  41.3 1.9 %collective-permute-start.8 = (bf16[128,32,256]{2,1,0:T(8,128)(2,1)}, bf16[128,32,256]{2,1,0:T(8,128)(2,1)S(1)}, u32[]{:S(2)}, u32[]{:S(2)}) collective-permute-start(bf16[128,32,256]{2,1,0:T(8,128)(2,1)} %constant_dynamic-slice_fusion.1), channel_id=1, source_target_pairs={{0,1},{1,0},{2,3},{3,2},{4,5},{5,4},{6,7},{7,6},{8,9},{9,8},{10,11... | collective-permute-start | bytes 6291464 | tf_op jit(solution)/shard_map/ppermute | solution.py:32
  43.2 2.4 %collective-permute-start.3 = (bf16[6,32,512]{2,0,1:T(8,128)(2,1)S(1)}, bf16[6,32,512]{2,0,1:T(8,128)(2,1)S(1)}, u32[]{:S(2)}, u32[]{:S(2)}) collective-permute-start(bf16[6,32,512]{2,0,1:T(8,128)(2,1)S(1)} %fusion.2), channel_id=1, source_target_pairs={{0,32},{128,160},{256,288},{384,416},{1,33},{129,161},{257,289},{3... | collective-permute-start | bytes 589832 | tf_op jit(solution)/shard_map/ppermute | solution.py:50
  45.6 1.3 collective-permute-start.4
  47.0 2.0 %collective-permute-start.5 = (bf16[6,32,512]{2,0,1:T(8,128)(2,1)S(1)}, bf16[6,32,512]{2,0,1:T(8,128)(2,1)}, u32[]{:S(2)}, u32[]{:S(2)}) collective-permute-start(bf16[6,32,512]{2,0,1:T(8,128)(2,1)S(1)} %fusion.2), channel_id=1, source_target_pairs={{0,96},{128,224},{256,352},{384,480},{1,97},{129,225},{257,353},{3... | collective-permute-start | bytes 589832 | tf_op jit(solution)/shard_map/ppermute | solution.py:50
  49.0 3.3 %collective-permute-done.3 = bf16[6,32,512]{2,0,1:T(8,128)(2,1)S(1)} collective-permute-done((bf16[6,32,512]{2,0,1:T(8,128)(2,1)S(1)}, bf16[6,32,512]{2,0,1:T(8,128)(2,1)S(1)}, u32[]{:S(2)}, u32[]{:S(2)}) %collective-permute-start.3) | collective-permute-done | bytes 196640 | tf_op jit(solution)/shard_map/ppermute | solution.py:50
  52.2 1.8 %all-to-all-done.1.refs_5_ = bf16[4,512,256]{2,1,0:T(8,128)(2,1)} async-done(((bf16[4,512,256]{2,1,0:T(8,128)(2,1)}), bf16[4,512,256]{2,1,0:T(8,128)(2,1)}, u32[]{:S(2)}, u32[]{:S(2)}) %all-to-all-start.1) | async-done | bytes 1048608 | tf_op jit(solution)/shard_map/all_to_all | solution.py:64
  54.0 1.9 %collective-permute-start.11 = (bf16[4,512,256]{2,1,0:T(8,128)(2,1)}, bf16[4,512,256]{2,1,0:T(8,128)(2,1)S(1)}, u32[]{:S(2)}, u32[]{:S(2)}) collective-permute-start(bf16[4,512,256]{2,1,0:T(8,128)(2,1)} %all-to-all-done.1.refs_5_), channel_id=1, source_target_pairs={{0,112},{32,0},{64,32},{96,64},{16,96},{48,16},{80,48},{112,80},{1... | collective-permute-start | bytes 3145736 | tf_op jit(solution)/shard_map/ppermute | solution.py:28
  56.0 3.9 %collective-permute-start.9 = (bf16[4,512,256]{2,1,0:T(8,128)(2,1)}, bf16[4,512,256]{2,1,0:T(8,128)(2,1)S(1)}, u32[]{:S(2)}, u32[]{:S(2)}) collective-permute-start(bf16[4,512,256]{2,1,0:T(8,128)(2,1)} %all-to-all-done.1.refs_5_), channel_id=1, source_target_pairs={{0,32},{32,64},{64,96},{96,16},{16,48},{48,80},{80,112},{112,0},{1... | collective-permute-start | bytes 3145736 | tf_op jit(solution)/shard_map/ppermute | solution.py:28
  59.9 3.6 %collective-permute-done.5 = bf16[6,32,512]{2,0,1:T(8,128)(2,1)} collective-permute-done((bf16[6,32,512]{2,0,1:T(8,128)(2,1)S(1)}, bf16[6,32,512]{2,0,1:T(8,128)(2,1)}, u32[]{:S(2)}, u32[]{:S(2)}) %collective-permute-start.5) | collective-permute-done | bytes 196640 | tf_op jit(solution)/shard_map/ppermute | solution.py:50
  63.5 1.0 add_add_fusion
  64.7 14.3 %all_to_all.20.refs_3_ = bf16[4,6,32,512]{3,2,1,0:T(8,128)(2,1)S(1)} all-to-all(bf16[4,6,32,512]{3,2,1,0:T(8,128)(2,1)S(1)} %broadcast_in_dim.7), channel_id=1, replica_groups=mesh['x'=4,'ylo'=4,'yhi'=2,'z'=8,'core'=2] {'x'}, dimensions={0} | all-to-all | bytes 1572864 | tf_op jit(solution)/shard_map/all_to_all | solution.py:64
  79.0 1.9 %collective-permute-start.6 = (bf16[4,6,32,512]{3,2,1,0:T(8,128)(2,1)S(1)}, bf16[4,6,32,512]{3,2,1,0:T(8,128)(2,1)}, u32[]{:S(2)}, u32[]{:S(2)}) collective-permute-start(bf16[4,6,32,512]{3,2,1,0:T(8,128)(2,1)S(1)} %all_to_all.20.refs_3_), channel_id=1, source_target_pairs={{0,1},{1,0},{2,3},{3,2},{4,5},{5,4},{6,7},{7,6},{8,9},{9,8},{10,11... | collective-permute-start | bytes 2359304 | tf_op jit(solution)/shard_map/ppermute | solution.py:32
  80.9 4.8 %collective-permute-done.9.refs_6_ = bf16[4,512,256]{2,1,0:T(8,128)(2,1)S(1)} collective-permute-done((bf16[4,512,256]{2,1,0:T(8,128)(2,1)}, bf16[4,512,256]{2,1,0:T(8,128)(2,1)S(1)}, u32[]{:S(2)}, u32[]{:S(2)}) %collective-permute-start.9) | collective-permute-done | bytes 1048608 | tf_op jit(solution)/shard_map/ppermute | solution.py:28
  85.7 0.9 slice.55
  86.6 4.3 %collective-permute-start.10 = (bf16[2,512,256]{2,1,0:T(8,128)(2,1)}, bf16[2,512,256]{2,1,0:T(8,128)(2,1)}, u32[]{:S(2)}, u32[]{:S(2)}) collective-permute-start(bf16[2,512,256]{2,1,0:T(8,128)(2,1)} %slice.55), channel_id=1, source_target_pairs={{0,32},{32,64},{64,96},{96,16},{16,48},{48,80},{80,112},{112,0},{1... | collective-permute-start | bytes 1572872 | tf_op jit(solution)/shard_map/ppermute | solution.py:28
  90.9 1.0 copy-done.2
  91.9 0.9 slice.56
  92.8 5.0 %collective-permute-start.12 = (bf16[2,512,256]{2,1,0:T(8,128)(2,1)}, bf16[2,512,256]{2,1,0:T(8,128)(2,1)}, u32[]{:S(2)}, u32[]{:S(2)}) collective-permute-start(bf16[2,512,256]{2,1,0:T(8,128)(2,1)} %slice.56), channel_id=1, source_target_pairs={{0,112},{32,0},{64,32},{96,64},{16,96},{48,16},{80,48},{112,80},{1... | collective-permute-start | bytes 1572872 | tf_op jit(solution)/shard_map/ppermute | solution.py:28
  98.1 2.1 %collective-permute-start.7 = (bf16[6,16]{1,0:T(8,128)(2,1)S(1)}, bf16[6,16]{1,0:T(8,128)(2,1)S(1)}, u32[]{:S(2)}, u32[]{:S(2)}) collective-permute-start(bf16[6,16]{1,0:T(8,128)(2,1)S(1)} %constant_dynamic-slice_fusion), channel_id=1, source_target_pairs={{0,1},{1,0},{2,3},{3,2},{4,5},{5,4},{6,7},{7,6},{8,9},{9,8},{10,11... | collective-permute-start | bytes 584 | tf_op jit(solution)/shard_map/ppermute | solution.py:32
  101.2 1.3 copy-done
  102.5 16.8 %shard_map.77 = (f32[72,256]{1,0:T(8,128)}, f32[12,8,256]{2,1,0:T(8,128)}) custom-call(s32[19]{0:T(128)} %concatenate.3.refs_0_, bf16[128,32,512]{2,1,0:T(8,128)(2,1)} %refs_1_.3, bf16[128,32,256]{2,1,0:T(8,128)(2,1)} %copy-done, bf16[4,6,32,512]{3,2,1,0:T(8,128)(2,1)} %copy-done.1, bf16[4,6,32,512]{3,2,1,0:T(8,128)(2,1)} %collective-permute-done.6.refs_4_, ...), custom_call_target="tpu_custom_call" | custom-call | flops 12000000 | bytes 100000 | tf_op jit(solution)/shard_map/pallas_call | solution.py:251
  119.4 9.6 %shard_map.78 = f32[32,1,128]{2,1,0:T(1,128)} custom-call(s32[19]{0:T(128)} %concatenate.3.refs_0_, bf16[128,32,512]{2,1,0:T(8,128)(2,1)} %refs_1_.3, bf16[128,32,256]{2,1,0:T(8,128)(2,1)} %copy-done, bf16[4,6,32,512]{3,2,1,0:T(8,128)(2,1)} %copy-done.1, bf16[4,6,32,512]{3,2,1,0:T(8,128)(2,1)} %collective-permute-done.6.refs_4_, f32[16,16]{1,0:T(8,128)} %refs_5_.1, ...), custom_call_target="tpu_custom_call" | custom-call | flops 4000000 | bytes 100000 | tf_op jit(solution)/shard_map/pallas_call | solution.py:271
  129.0 21.2 %all_to_all.21 = f32[32,1,128]{2,1,0:T(1,128)S(1)} all-to-all(f32[32,1,128]{2,1,0:T(1,128)} %shard_map.78), channel_id=1, replica_groups=mesh['x'=4,'ylo'=4,'yhi'=2,'z'=8,'core'=2] {'yhi','z','core'}, dimensions={0} | all-to-all | bytes 32768 | tf_op jit(solution)/shard_map/all_to_all | solution.py:291
  150.3 1.9 %collective-permute-start.13 = (f32[1,128]{1,0:T(1,128)S(1)}, f32[1,128]{1,0:T(1,128)S(1)}, u32[]{:S(2)}, u32[]{:S(2)}) collective-permute-start(f32[1,128]{1,0:T(1,128)S(1)} %bitcast.36), channel_id=1, source_target_pairs={{0,0},{1,1},{2,32},{3,33},{4,64},{5,65},{6,96},{7,97},{8,128},{9,1... | collective-permute-start | bytes 1544 | tf_op jit(solution)/shard_map/ppermute | solution.py:298
  153.0 13.6 %collective-permute-done.13 = f32[1,128]{1,0:T(1,128)S(1)} collective-permute-done((f32[1,128]{1,0:T(1,128)S(1)}, f32[1,128]{1,0:T(1,128)S(1)}, u32[]{:S(2)}, u32[]{:S(2)}) %collective-permute-start.13) | collective-permute-done | bytes 544 | tf_op jit(solution)/shard_map/ppermute | solution.py:298
  (42 shorter events, 5.7 us)
Async XLA Ops:
  2.1 31.3 %all-to-all-start = ((bf16[32,16,256]{2,1,0:T(8,128)(2,1)}), bf16[32,16,256]{2,1,0:T(8,128)(2,1)S(1)}, u32[]{:S(2)}, u32[]{:S(2)}) async-start(bf16[32,16,256]{2,1,0:T(8,128)(2,1)} %bitcast.22), calls=%async_computation | async-start | bytes 524288 | tf_op jit(solution)/shard_map/all_to_all | solution.py:201
  19.4 5.8 %collective-permute-start = (bf16[6,32,512]{2,0,1:T(8,128)(2,1)S(1)}, bf16[6,32,512]{2,0,1:T(8,128)(2,1)S(1)}, u32[]{:S(2)}, u32[]{:S(2)}) collective-permute-start(bf16[6,32,512]{2,0,1:T(8,128)(2,1)S(1)} %get-tuple-element.28), channel_id=1, source_target_pairs={{0,128},{1,129},{2,130},{3,131},{4,132},{5,133},{6,134},{7,135},{8... | collective-permute-start | bytes 589832 | tf_op jit(solution)/shard_map/ppermute | solution.py:43
  20.1 5.1 %collective-permute-start.1 = (bf16[6,32,512]{2,0,1:T(8,128)(2,1)S(1)}, bf16[6,32,512]{2,0,1:T(8,128)(2,1)S(1)}, u32[]{:S(2)}, u32[]{:S(2)}) collective-permute-start(bf16[6,32,512]{2,0,1:T(8,128)(2,1)S(1)} %get-tuple-element.30), channel_id=1, source_target_pairs={{0,256},{1,257},{2,258},{3,259},{4,260},{5,261},{6,262},{7,263},{8... | collective-permute-start | bytes 589832 | tf_op jit(solution)/shard_map/ppermute | solution.py:43
  20.8 12.5 %collective-permute-start.2 = (bf16[6,32,512]{2,0,1:T(8,128)(2,1)S(1)}, bf16[6,32,512]{2,0,1:T(8,128)(2,1)S(1)}, u32[]{:S(2)}, u32[]{:S(2)}) collective-permute-start(bf16[6,32,512]{2,0,1:T(8,128)(2,1)S(1)} %get-tuple-element.29), channel_id=1, source_target_pairs={{0,384},{1,385},{2,386},{3,387},{4,388},{5,389},{6,390},{7,391},{8... | collective-permute-start | bytes 589832 | tf_op jit(solution)/shard_map/ppermute | solution.py:43
  34.4 19.6 %all-to-all-start.1 = ((bf16[4,512,256]{2,1,0:T(8,128)(2,1)}), bf16[4,512,256]{2,1,0:T(8,128)(2,1)}, u32[]{:S(2)}, u32[]{:S(2)}) async-start(bf16[4,512,256]{2,1,0:T(8,128)(2,1)} %broadcast_in_dim.6), calls=%async_computation.1 | async-start | bytes 2097152 | tf_op jit(solution)/shard_map/all_to_all | solution.py:64
  41.3 59.9 %collective-permute-start.8 = (bf16[128,32,256]{2,1,0:T(8,128)(2,1)}, bf16[128,32,256]{2,1,0:T(8,128)(2,1)S(1)}, u32[]{:S(2)}, u32[]{:S(2)}) collective-permute-start(bf16[128,32,256]{2,1,0:T(8,128)(2,1)} %constant_dynamic-slice_fusion.1), channel_id=1, source_target_pairs={{0,1},{1,0},{2,3},{3,2},{4,5},{5,4},{6,7},{7,6},{8,9},{9,8},{10,11... | collective-permute-start | bytes 6291464 | tf_op jit(solution)/shard_map/ppermute | solution.py:32
  43.2 9.0 %collective-permute-start.3 = (bf16[6,32,512]{2,0,1:T(8,128)(2,1)S(1)}, bf16[6,32,512]{2,0,1:T(8,128)(2,1)S(1)}, u32[]{:S(2)}, u32[]{:S(2)}) collective-permute-start(bf16[6,32,512]{2,0,1:T(8,128)(2,1)S(1)} %fusion.2), channel_id=1, source_target_pairs={{0,32},{128,160},{256,288},{384,416},{1,33},{129,161},{257,289},{3... | collective-permute-start | bytes 589832 | tf_op jit(solution)/shard_map/ppermute | solution.py:50
  45.6 14.2 %collective-permute-start.4 = (bf16[6,32,512]{2,0,1:T(8,128)(2,1)S(1)}, bf16[6,32,512]{2,0,1:T(8,128)(2,1)S(1)}, u32[]{:S(2)}, u32[]{:S(2)}) collective-permute-start(bf16[6,32,512]{2,0,1:T(8,128)(2,1)S(1)} %fusion.2), channel_id=1, source_target_pairs={{0,64},{128,192},{256,320},{384,448},{1,65},{129,193},{257,321},{3... | collective-permute-start | bytes 589832 | tf_op jit(solution)/shard_map/ppermute | solution.py:50
  47.0 16.6 %collective-permute-start.5 = (bf16[6,32,512]{2,0,1:T(8,128)(2,1)S(1)}, bf16[6,32,512]{2,0,1:T(8,128)(2,1)}, u32[]{:S(2)}, u32[]{:S(2)}) collective-permute-start(bf16[6,32,512]{2,0,1:T(8,128)(2,1)S(1)} %fusion.2), channel_id=1, source_target_pairs={{0,96},{128,224},{256,352},{384,480},{1,97},{129,225},{257,353},{3... | collective-permute-start | bytes 589832 | tf_op jit(solution)/shard_map/ppermute | solution.py:50
  54.0 36.9 %collective-permute-start.11 = (bf16[4,512,256]{2,1,0:T(8,128)(2,1)}, bf16[4,512,256]{2,1,0:T(8,128)(2,1)S(1)}, u32[]{:S(2)}, u32[]{:S(2)}) collective-permute-start(bf16[4,512,256]{2,1,0:T(8,128)(2,1)} %all-to-all-done.1.refs_5_), channel_id=1, source_target_pairs={{0,112},{32,0},{64,32},{96,64},{16,96},{48,16},{80,48},{112,80},{1... | collective-permute-start | bytes 3145736 | tf_op jit(solution)/shard_map/ppermute | solution.py:28
  56.0 29.7 %collective-permute-start.9 = (bf16[4,512,256]{2,1,0:T(8,128)(2,1)}, bf16[4,512,256]{2,1,0:T(8,128)(2,1)S(1)}, u32[]{:S(2)}, u32[]{:S(2)}) collective-permute-start(bf16[4,512,256]{2,1,0:T(8,128)(2,1)} %all-to-all-done.1.refs_5_), channel_id=1, source_target_pairs={{0,32},{32,64},{64,96},{96,16},{16,48},{48,80},{80,112},{112,0},{1... | collective-permute-start | bytes 3145736 | tf_op jit(solution)/shard_map/ppermute | solution.py:28
  79.0 22.2 %copy-start.1 = (bf16[4,6,32,512]{3,2,1,0:T(8,128)(2,1)}, bf16[4,6,32,512]{3,2,1,0:T(8,128)(2,1)S(1)}, u32[]{:S(2)}) copy-start(bf16[4,6,32,512]{3,2,1,0:T(8,128)(2,1)S(1)} %all_to_all.20.refs_3_) | copy-start | bytes 2359300
  79.0 22.2 %collective-permute-start.6 = (bf16[4,6,32,512]{3,2,1,0:T(8,128)(2,1)S(1)}, bf16[4,6,32,512]{3,2,1,0:T(8,128)(2,1)}, u32[]{:S(2)}, u32[]{:S(2)}) collective-permute-start(bf16[4,6,32,512]{3,2,1,0:T(8,128)(2,1)S(1)} %all_to_all.20.refs_3_), channel_id=1, source_target_pairs={{0,1},{1,0},{2,3},{3,2},{4,5},{5,4},{6,7},{7,6},{8,9},{9,8},{10,11... | collective-permute-start | bytes 2359304 | tf_op jit(solution)/shard_map/ppermute | solution.py:32
  85.7 7.1 %copy-start.3 = (bf16[4,512,256]{2,1,0:T(8,128)(2,1)}, bf16[4,512,256]{2,1,0:T(8,128)(2,1)S(1)}, u32[]{:S(2)}) copy-start(bf16[4,512,256]{2,1,0:T(8,128)(2,1)S(1)} %collective-permute-done.9.refs_6_) | copy-start | bytes 3145732
  86.6 32.7 %collective-permute-start.10 = (bf16[2,512,256]{2,1,0:T(8,128)(2,1)}, bf16[2,512,256]{2,1,0:T(8,128)(2,1)}, u32[]{:S(2)}, u32[]{:S(2)}) collective-permute-start(bf16[2,512,256]{2,1,0:T(8,128)(2,1)} %slice.55), channel_id=1, source_target_pairs={{0,32},{32,64},{64,96},{96,16},{16,48},{48,80},{80,112},{112,0},{1... | collective-permute-start | bytes 1572872 | tf_op jit(solution)/shard_map/ppermute | solution.py:28
  90.9 1.0 copy-start.2
  92.8 26.6 %collective-permute-start.12 = (bf16[2,512,256]{2,1,0:T(8,128)(2,1)}, bf16[2,512,256]{2,1,0:T(8,128)(2,1)}, u32[]{:S(2)}, u32[]{:S(2)}) collective-permute-start(bf16[2,512,256]{2,1,0:T(8,128)(2,1)} %slice.56), channel_id=1, source_target_pairs={{0,112},{32,0},{64,32},{96,64},{16,96},{48,16},{80,48},{112,80},{1... | collective-permute-start | bytes 1572872 | tf_op jit(solution)/shard_map/ppermute | solution.py:28
  98.1 3.0 %collective-permute-start.7 = (bf16[6,16]{1,0:T(8,128)(2,1)S(1)}, bf16[6,16]{1,0:T(8,128)(2,1)S(1)}, u32[]{:S(2)}, u32[]{:S(2)}) collective-permute-start(bf16[6,16]{1,0:T(8,128)(2,1)S(1)} %constant_dynamic-slice_fusion), channel_id=1, source_target_pairs={{0,1},{1,0},{2,3},{3,2},{4,5},{5,4},{6,7},{7,6},{8,9},{9,8},{10,11... | collective-permute-start | bytes 584 | tf_op jit(solution)/shard_map/ppermute | solution.py:32
  101.2 1.3 copy-start
  119.4 32.9 %copy-start.5 = (f32[512]{0:T(512)S(1)}, f32[512]{0:T(512)}, u32[]{:S(2)}) copy-start(f32[512]{0:T(512)} %param.10) | copy-start | bytes 6148
  119.4 47.3 %copy-start.4 = (f32[1,6,16]{2,0,1:T(1,128)S(1)}, f32[1,6,16]{2,0,1:T(1,128)}, u32[]{:S(2)}) copy-start(f32[1,6,16]{2,0,1:T(1,128)} %param.9) | copy-start | bytes 1156
  119.4 47.3 %slice-start = ((f32[512]{0:T(512)}), f32[6]{0:T(128)S(1)}, s32[]{:S(2)}) async-start(f32[512]{0:T(512)} %param.10), calls=%async_computation.4 | async-start | bytes 1024 | tf_op jit(solution)/shard_map/slice | solution.py:304
  150.3 16.2 %collective-permute-start.13 = (f32[1,128]{1,0:T(1,128)S(1)}, f32[1,128]{1,0:T(1,128)S(1)}, u32[]{:S(2)}, u32[]{:S(2)}) collective-permute-start(f32[1,128]{1,0:T(1,128)S(1)} %bitcast.36), channel_id=1, source_target_pairs={{0,0},{1,1},{2,32},{3,33},{4,64},{5,65},{6,96},{7,97},{8,128},{9,1... | collective-permute-start | bytes 1544 | tf_op jit(solution)/shard_map/ppermute | solution.py:298

commit v5 on v3

--- a/solution.py
+++ b/solution.py
@@ -52,11 +52,11 @@
     ]
 
 
-def window_collected(mine, spread):
+def window_quarter(mine, spread):
     quarter = jnp.where(lax.axis_index("ylo") == 0, mine, jnp.zeros_like(mine))
     for piece in spread:
         quarter = quarter + piece
-    return collected(quarter)
+    return quarter
 
 
 def collected(array):
@@ -64,12 +64,6 @@
     return lax.all_to_all(
         jnp.broadcast_to(array[None], (parts, *array.shape)), "x", 0, 0, tiled=True
     )
-
-
-def own_half(scalars, factors, f_other, pairs):
-    columns = f_other.shape[2]
-    start = pl.multiple_of(scalars[pairs] * columns, columns)
-    return factors.at[:, :, pl.ds(start, columns)]
 
 
 def half_sums(f_own, f_other, w_own, w_other, chunks, halves):
@@ -119,9 +113,8 @@
     return jnp.sum(jnp.where(lane // width == q, total, 0.0), axis=1)
 
 
-def early_kernel(pairs, scalars, factors, f_other, w_own, w_other, *refs):
+def early_kernel(scalars, f_own, f_other, w_own, w_other, *refs):
     chunks, (sums, heads, halves) = refs[:-3], refs[-3:]
-    f_own = own_half(scalars, factors, f_other, pairs)
     sums[...] = half_sums(f_own, f_other, w_own, w_other, chunks, halves)
     count = 0
     for chunk in chunks:
@@ -130,13 +123,12 @@
             count += 1
 
 
-def late_kernel(chunk_count, scalars, factors, f_other, w_own, w_other, hole_weights, *refs):
+def late_kernel(chunk_count, scalars, f_own, f_other, w_own, w_other, hole_weights, *refs):
     chunks, refs = refs[:chunk_count], refs[chunk_count:]
     early, (out, halves, head, hole) = refs[:-4], refs[-4:]
     rows = w_own.shape[1]
     width = f_other.shape[1]
     pairs = hole_weights.shape[0]
-    f_own = own_half(scalars, factors, f_other, pairs)
     sums = [s[...] for s in early[0::2]]
     sums.append(half_sums(f_own, f_other, w_own, w_other, chunks, halves))
     sums = jnp.concatenate(sums, axis=0)
@@ -191,21 +183,14 @@
     amp = amp.reshape(-1, half)
 
     scattered = window_scattered(factors, rows)
-    amp, scattered = lax.optimization_barrier((amp, scattered))
-
-    spread = window_spread(scattered)
-    chunk = collected(amp)
-    chunk, spread = lax.optimization_barrier((chunk, spread))
-    behind, ahead = shifted(chunk, "y", 1), shifted(chunk, "y", -1)
-    window = window_collected(scattered, spread)
-    window_other = swapped(window)
-    f_other = swapped(lax.dynamic_slice_in_dim(factors, (1 - core) * half, half, 2))
+    f_other = lax.dynamic_slice_in_dim(factors, (1 - core) * half, half, 2)
+    amp, scattered, f_other = lax.optimization_barrier((amp, scattered, f_other))
+    f_other = swapped(f_other)
 
     start = (aux_index * columns) % half
     here = lax.dynamic_slice_in_dim(amp[:rows], start, columns, 1)
     there = lax.dynamic_slice_in_dim(amp[:rows], start + columns * (1 - 2 * core), columns, 1)
     amp_cols = jnp.where(core == yhi, here, swapped(there)).astype(F32)
-    window_other, amp_cols, f_other = lax.optimization_barrier((window_other, amp_cols, f_other))
 
     order = jnp.stack(
         [i * lows + (ylo - k) % lows for k in (0, 1, -1, 2) for i in range(xs)]
@@ -216,10 +201,20 @@
         [order, jnp.stack([core, place, chosen.astype(jnp.int32)]).astype(jnp.int32)]
     )
 
+    spread = window_spread(scattered)
+    chunk = collected(amp)
+    chunk, spread[0], amp_cols, scalars = lax.optimization_barrier(
+        (chunk, spread[0], amp_cols, scalars)
+    )
+    behind, ahead = shifted(chunk, "y", 1), shifted(chunk, "y", -1)
+    window = collected(window_quarter(scattered, spread))
+    window_other = swapped(window)
+
     head_rows = 8
     blocks = factors.shape[0] // BLOCK_Q
     span = rows * BLOCK_Q
     whole = pl.BlockSpec(memory_space=pltpu.VMEM)
+    own_half = pl.BlockSpec((factors.shape[0], width, half), lambda i, s: (0, 0, s[pairs]))
     params = pltpu.CompilerParams(vmem_limit_bytes=44 * 1024 * 1024)
 
     def scratch(count):
@@ -227,17 +222,17 @@
 
     def cost(count):
         return pl.CostEstimate(
-            flops=605_000_000 * count, bytes_accessed=8_000_000, transcendentals=0
+            flops=1_000_000 * count, bytes_accessed=100_000, transcendentals=0
         )
 
     def early(*chunks):
         count = sum(c.shape[0] for c in chunks)
         return pl.pallas_call(
-            lambda *refs: early_kernel(pairs, *refs),
+            early_kernel,
             grid_spec=pltpu.PrefetchScalarGridSpec(
                 num_scalar_prefetch=1,
                 grid=(1,),
-                in_specs=[whole] * (4 + len(chunks)),
+                in_specs=[own_half] + [whole] * (3 + len(chunks)),
                 out_specs=[whole, whole],
                 scratch_shapes=[scratch(count)],
             ),
@@ -249,17 +244,15 @@
             cost_estimate=cost(count),
         )(scalars, factors, f_other, window, window_other, *chunks)
 
-    first = early(chunk)
-    behind, ahead, first = lax.optimization_barrier((behind, ahead, first))
     cut = xs // 2
     last = (shifted(behind[:cut], "y", 1), shifted(ahead[cut:], "y", -1))
-    done = [*first, *early(behind, ahead)]
+    done = early(chunk, behind, ahead)
     tiles = pl.pallas_call(
         lambda *refs: late_kernel(len(last), *refs),
         grid_spec=pltpu.PrefetchScalarGridSpec(
             num_scalar_prefetch=1,
             grid=(1,),
-            in_specs=[whole] * (5 + len(last) + len(done)),
+            in_specs=[own_half] + [whole] * (4 + len(last) + len(done)),
             out_specs=whole,
             scratch_shapes=[
                 scratch(lows),

time: 170 us -> 157 us (0.924)
  waiting for transfers between devices: 51.6 us -> 32.4 us
  blocking collectives: 19.1 us -> 38 us
  local copies, waits for them, and re-layouts: 13.8 us -> 8.71 us
  starting transfers between devices: 60.9 us -> 55.9 us
  Pallas kernels: 21.3 us -> 17 us
  other arithmetic: 0.33 us -> 2.21 us
    all_to_all x0 -> x1, blocking collectives: none -> 13.8 us  [collected(): lax.all_to_all(jnp.broadcast_to(array[None], (parts, *array.shape)), 'x',...]
    ppermute x3, waiting for transfers between devices: 14.8 us -> 6.58 us  [window_spread(): lax.ppermute(mine, PAIR, [(i * lows, i * lows + k) for i in range(parts)])]
    ppermute x4, waiting for transfers between devices: 11.5 us -> 4.95 us  [shifted(): lax.ppermute(array, Y, [(index(y), index((y + by) % full)) for y in range...]
    ppermute x3, waiting for transfers between devices: 11.2 us -> 5.81 us  [window_scattered(): mine = mine + lax.ppermute(pieces[i], PAIR, [(0, i * lows)])]
    all_to_all x1, blocking collectives: 19.1 us -> 24.1 us  [per_device(): summed = jnp.sum(lax.all_to_all(tiles, AUX, 0, 0, tiled=True), axis=0)]
    pallas_call x2 -> x1, Pallas kernels: 15 us -> 11.9 us  [early(): pl.pallas_call(early_kernel, grid_spec=pltpu.PrefetchScalarGridSpec(num_s...]
    all_to_all x2 -> x1, starting transfers between devices: 11.7 us -> 9.34 us  [collected(): lax.all_to_all(jnp.broadcast_to(array[None], (parts, *array.shape)), 'x',...]
    ppermute x4, starting transfers between devices: 16.8 us -> 14.5 us  [shifted(): lax.ppermute(array, Y, [(index(y), index((y + by) % full)) for y in range...]
  transfers between devices with their start and end apart: 17 -> 16, of which waited for: 10 -> 8; matrix products, arithmetic and copies ran while one was open for 4% -> 4% of each run, Pallas kernels for 9% -> 8%
where the time goes in v5:
time: 157 us; the launch traced here: 156 us
  starting transfers between devices  55.9 us (36%)
  blocking collectives  38 us (24%)
  waiting for transfers between devices  32.4 us (21%)
  Pallas kernels  17 us (11%)
  local copies, waits for them, and re-layouts  8.71 us (6%)
  other arithmetic  2.21 us (1%)
  between operations  1.68 us (1%)
    all_to_all x1, blocking collectives, per_device(): summed = jnp.sum(lax.all_to_all(tiles, AUX, 0, 0, tiled=True), axis=0)  24.1 us
    all_to_all x1, starting transfers between devices, per_device(): lax.all_to_all(sent.reshape(-1, *split.shape[1:]), AUX, 0, 0, tiled=True)  16 us
    ppermute x4, starting transfers between devices, shifted(): lax.ppermute(array, Y, [(index(y), index((y + by) % full)) for y in range...  14.5 us
    all_to_all x1, blocking collectives, collected(): lax.all_to_all(jnp.broadcast_to(array[None], (parts, *array.shape)), 'x',...  13.8 us
    ppermute x1, waiting for transfers between devices, per_device(): summed = lax.ppermute(summed, AXES, moves)  13.6 us
    pallas_call x1, Pallas kernels, early(): pl.pallas_call(early_kernel, grid_spec=pltpu.PrefetchScalarGridSpec(num_s...  11.9 us
    all_to_all x1, starting transfers between devices, collected(): lax.all_to_all(jnp.broadcast_to(array[None], (parts, *array.shape)), 'x',...  9.34 us
    ppermute x3, waiting for transfers between devices, window_spread(): lax.ppermute(mine, PAIR, [(i * lows, i * lows + k) for i in range(parts)])  6.58 us
  transfers between devices with their start and end apart: 16, of which 8 were waited for; matrix products, arithmetic and copies ran while one was open for 4% of the time, Pallas kernels for 8%

profile of v5, /device:TPU:6, one launch (start us, length us, event | category | flops | bytes accessed | tf_op | source)
XLA Modules:
  0.0 155.8 jit_solution(1907601560511847087)
XLA Ops:
  0.6 0.7 slice_bitcast_fusion.2
  1.4 0.7 tile.7
  2.1 16.0 %all-to-all-start = ((bf16[32,16,256]{2,1,0:T(8,128)(2,1)}), bf16[32,16,256]{2,1,0:T(8,128)(2,1)S(1)}, u32[]{:S(2)}, u32[]{:S(2)}) async-start(bf16[32,16,256]{2,1,0:T(8,128)(2,1)} %bitcast.3), calls=%async_computation | async-start | bytes 524288 | tf_op jit(solution)/shard_map/all_to_all | solution.py:182
  18.1 1.3 slice_bitcast_fusion
  19.4 1.3 collective-permute-start.2
  20.7 0.7 collective-permute-start.1
  22.1 3.1 %constant_dynamic-slice_fusion.1 = bf16[128,32,256]{2,1,0:T(8,128)(2,1)} fusion(bf16[128,32,512]{2,1,0:T(8,128)(2,1)} %refs_1_.1, s32[]{:T(128)S(6)} %select_n.91), kind=kLoop, calls=%fused_computation.13 | loop fusion | bytes 4194308 | tf_op jit(solution)/shard_map/dynamic_slice | solution.py:186
  25.2 5.8 %collective-permute-done.2 = bf16[6,32,512]{2,0,1:T(8,128)(2,1)S(1)} collective-permute-done((bf16[6,32,512]{2,0,1:T(8,128)(2,1)S(1)}, bf16[6,32,512]{2,0,1:T(8,128)(2,1)S(1)}, u32[]{:S(2)}, u32[]{:S(2)}) %collective-permute-start.2) | collective-permute-done | bytes 196640 | tf_op jit(solution)/shard_map/ppermute | solution.py:43
  31.0 0.8 fusion.2
  31.8 0.9 all-to-all-done
  32.6 1.0 broadcast_in_dim.6
  33.7 9.3 %all-to-all-start.1 = ((bf16[4,512,256]{2,1,0:T(8,128)(2,1)}), bf16[4,512,256]{2,1,0:T(8,128)(2,1)S(1)}, u32[]{:S(2)}, u32[]{:S(2)}) async-start(bf16[4,512,256]{2,1,0:T(8,128)(2,1)} %broadcast_in_dim.6), calls=%async_computation.1 | async-start | bytes 2097152 | tf_op jit(solution)/shard_map/all_to_all | solution.py:64
  43.0 1.9 %collective-permute-start.5 = (bf16[128,32,256]{2,1,0:T(8,128)(2,1)}, bf16[128,32,256]{2,1,0:T(8,128)(2,1)S(1)}, u32[]{:S(2)}, u32[]{:S(2)}) collective-permute-start(bf16[128,32,256]{2,1,0:T(8,128)(2,1)} %constant_dynamic-slice_fusion.1), channel_id=1, source_target_pairs={{0,1},{1,0},{2,3},{3,2},{4,5},{5,4},{6,7},{7,6},{8,9},{9,8},{10,11... | collective-permute-start | bytes 6291464 | tf_op jit(solution)/shard_map/ppermute | solution.py:32
  45.3 2.4 %collective-permute-start.4 = (bf16[6,16]{1,0:T(8,128)(2,1)S(1)}, bf16[6,16]{1,0:T(8,128)(2,1)S(1)}, u32[]{:S(2)}, u32[]{:S(2)}) collective-permute-start(bf16[6,16]{1,0:T(8,128)(2,1)S(1)} %constant_dynamic-slice_fusion), channel_id=1, source_target_pairs={{0,1},{1,0},{2,3},{3,2},{4,5},{5,4},{6,7},{7,6},{8,9},{9,8},{10,11... | collective-permute-start | bytes 584 | tf_op jit(solution)/shard_map/ppermute | solution.py:32
  47.7 1.3 collective-permute-start.3
  49.0 2.0 %collective-permute-start.7 = (bf16[6,32,512]{2,0,1:T(8,128)(2,1)}, bf16[6,32,512]{2,0,1:T(8,128)(2,1)}, u32[]{:S(2)}, u32[]{:S(2)}) collective-permute-start(bf16[6,32,512]{2,0,1:T(8,128)(2,1)} %fusion.2), channel_id=1, source_target_pairs={{0,96},{128,224},{256,352},{384,480},{1,97},{129,225},{257,353},{3... | collective-permute-start | bytes 589832 | tf_op jit(solution)/shard_map/ppermute | solution.py:50
  51.0 2.0 %collective-permute-start.6 = (bf16[6,32,512]{2,0,1:T(8,128)(2,1)}, bf16[6,32,512]{2,0,1:T(8,128)(2,1)}, u32[]{:S(2)}, u32[]{:S(2)}) collective-permute-start(bf16[6,32,512]{2,0,1:T(8,128)(2,1)} %fusion.2), channel_id=1, source_target_pairs={{0,64},{128,192},{256,320},{384,448},{1,65},{129,193},{257,321},{3... | collective-permute-start | bytes 589832 | tf_op jit(solution)/shard_map/ppermute | solution.py:50
  53.0 2.9 %collective-permute-done.3 = bf16[6,32,512]{2,0,1:T(8,128)(2,1)S(1)} collective-permute-done((bf16[6,32,512]{2,0,1:T(8,128)(2,1)}, bf16[6,32,512]{2,0,1:T(8,128)(2,1)S(1)}, u32[]{:S(2)}, u32[]{:S(2)}) %collective-permute-start.3) | collective-permute-done | bytes 196640 | tf_op jit(solution)/shard_map/ppermute | solution.py:50
  56.5 3.7 %collective-permute-start.9 = (bf16[4,512,256]{2,1,0:T(8,128)(2,1)S(1)}, bf16[4,512,256]{2,1,0:T(8,128)(2,1)S(1)}, u32[]{:S(2)}, u32[]{:S(2)}) collective-permute-start(bf16[4,512,256]{2,1,0:T(8,128)(2,1)S(1)} %all-to-all-done.1.refs_0_), channel_id=1, source_target_pairs={{0,32},{32,64},{64,96},{96,16},{16,48},{48,80},{80,112},{112,0},{1... | collective-permute-start | bytes 3145736 | tf_op jit(solution)/shard_map/ppermute | solution.py:28
  60.2 3.3 %collective-permute-start.11 = (bf16[4,512,256]{2,1,0:T(8,128)(2,1)S(1)}, bf16[4,512,256]{2,1,0:T(8,128)(2,1)S(1)}, u32[]{:S(2)}, u32[]{:S(2)}) collective-permute-start(bf16[4,512,256]{2,1,0:T(8,128)(2,1)S(1)} %all-to-all-done.1.refs_0_), channel_id=1, source_target_pairs={{0,112},{32,0},{64,32},{96,64},{16,96},{48,16},{80,48},{112,80},{1... | collective-permute-start | bytes 3145736 | tf_op jit(solution)/shard_map/ppermute | solution.py:28
  63.5 3.7 %collective-permute-done.6 = bf16[6,32,512]{2,0,1:T(8,128)(2,1)} collective-permute-done((bf16[6,32,512]{2,0,1:T(8,128)(2,1)}, bf16[6,32,512]{2,0,1:T(8,128)(2,1)}, u32[]{:S(2)}, u32[]{:S(2)}) %collective-permute-start.6) | collective-permute-done | bytes 196640 | tf_op jit(solution)/shard_map/ppermute | solution.py:50
  67.2 1.3 add_add_fusion
  68.6 13.8 %all_to_all.20.w_own.refs_3_ = bf16[4,6,32,512]{3,2,1,0:T(8,128)(2,1)S(1)} all-to-all(bf16[4,6,32,512]{3,2,1,0:T(8,128)(2,1)S(1)} %broadcast_in_dim.7), channel_id=1, replica_groups=mesh['x'=4,'ylo'=4,'yhi'=2,'z'=8,'core'=2] {'x'}, dimensions={0} | all-to-all | bytes 1572864 | tf_op jit(solution)/shard_map/all_to_all | solution.py:64
  82.5 1.9 %collective-permute-start.8 = (bf16[4,6,32,512]{3,2,1,0:T(8,128)(2,1)S(1)}, bf16[4,6,32,512]{3,2,1,0:T(8,128)(2,1)S(1)}, u32[]{:S(2)}, u32[]{:S(2)}) collective-permute-start(bf16[4,6,32,512]{3,2,1,0:T(8,128)(2,1)S(1)} %all_to_all.20.w_own.refs_3_), channel_id=1, source_target_pairs={{0,1},{1,0},{2,3},{3,2},{4,5},{5,4},{6,7},{7,6},{8,9},{9,8},{10,11... | collective-permute-start | bytes 2359304 | tf_op jit(solution)/shard_map/ppermute | solution.py:32
  84.4 4.6 %collective-permute-done.9.refs_1_ = bf16[4,512,256]{2,1,0:T(8,128)(2,1)S(1)} collective-permute-done((bf16[4,512,256]{2,1,0:T(8,128)(2,1)S(1)}, bf16[4,512,256]{2,1,0:T(8,128)(2,1)S(1)}, u32[]{:S(2)}, u32[]{:S(2)}) %collective-permute-start.9) | collective-permute-done | bytes 1048608 | tf_op jit(solution)/shard_map/ppermute | solution.py:28
  89.0 4.4 %collective-permute-start.10 = (bf16[2,512,256]{2,1,0:T(8,128)(2,1)S(1)}, bf16[2,512,256]{2,1,0:T(8,128)(2,1)S(1)}, u32[]{:S(2)}, u32[]{:S(2)}) collective-permute-start(bf16[2,512,256]{2,1,0:T(8,128)(2,1)S(1)} %slice.55), channel_id=1, source_target_pairs={{0,32},{32,64},{64,96},{96,16},{16,48},{48,80},{80,112},{112,0},{1... | collective-permute-start | bytes 1572872 | tf_op jit(solution)/shard_map/ppermute | solution.py:28
  93.5 3.1 %collective-permute-start.12 = (bf16[2,512,256]{2,1,0:T(8,128)(2,1)S(1)}, bf16[2,512,256]{2,1,0:T(8,128)(2,1)S(1)}, u32[]{:S(2)}, u32[]{:S(2)}) collective-permute-start(bf16[2,512,256]{2,1,0:T(8,128)(2,1)S(1)} %slice.56), channel_id=1, source_target_pairs={{0,112},{32,0},{64,32},{96,64},{16,96},{48,16},{80,48},{112,80},{1... | collective-permute-start | bytes 1572872 | tf_op jit(solution)/shard_map/ppermute | solution.py:28
  96.6 11.9 %shard_map.77 = (f32[72,256]{1,0:T(8,128)S(1)}, f32[12,8,256]{2,1,0:T(8,128)S(1)}) custom-call(s32[19]{0:T(128)S(1)} %concatenate.3.scalars.refs_0_, bf16[128,32,512]{2,1,0:T(8,128)(2,1)} %refs_1_.1, bf16[128,32,256]{2,1,0:T(8,128)(2,1)S(1)} %collective-permute-done.5.f_other.refs_2_, bf16[4,6,32,512]{3,2,1,0:T(8,128)(2,1)S(1)} %all_to_all.20.w_own.refs_3_, ...), custom_call_target="tpu_custom_call" | custom-call | flops 12000000 | bytes 100000 | tf_op jit(solution)/shard_map/pallas_call | solution.py:230
  108.9 5.1 %shard_map.78 = f32[32,1,128]{2,1,0:T(1,128)S(1)} custom-call(s32[19]{0:T(128)S(1)} %concatenate.3.scalars.refs_0_, bf16[128,32,512]{2,1,0:T(8,128)(2,1)S(1)} %copy-done, bf16[128,32,256]{2,1,0:T(8,128)(2,1)S(1)} %collective-permute-done.5.f_other.refs_2_, bf16[4,6,32,512]{3,2,1,0:T(8,128)(2,1)S(1)} %all_to_all.20.w_own.refs_3_, ...), custom_call_target="tpu_custom_call" | custom-call | flops 4000000 | bytes 100000 | tf_op jit(solution)/shard_map/pallas_call | solution.py:250
  114.0 24.1 %all_to_all.21 = f32[32,1,128]{2,1,0:T(1,128)S(1)} all-to-all(f32[32,1,128]{2,1,0:T(1,128)S(1)} %shard_map.78), channel_id=1, replica_groups=mesh['x'=4,'ylo'=4,'yhi'=2,'z'=8,'core'=2] {'yhi','z','core'}, dimensions={0} | all-to-all | bytes 32768 | tf_op jit(solution)/shard_map/all_to_all | solution.py:268
  138.2 1.9 %collective-permute-start.13 = (f32[1,128]{1,0:T(1,128)S(1)}, f32[1,128]{1,0:T(1,128)S(1)}, u32[]{:S(2)}, u32[]{:S(2)}) collective-permute-start(f32[1,128]{1,0:T(1,128)S(1)} %bitcast.36), channel_id=1, source_target_pairs={{0,0},{1,1},{2,32},{3,33},{4,64},{5,65},{6,96},{7,97},{8,128},{9,1... | collective-permute-start | bytes 1544 | tf_op jit(solution)/shard_map/ppermute | solution.py:275
  140.9 13.6 %collective-permute-done.13 = f32[1,128]{1,0:T(1,128)S(1)} collective-permute-done((f32[1,128]{1,0:T(1,128)S(1)}, f32[1,128]{1,0:T(1,128)S(1)}, u32[]{:S(2)}, u32[]{:S(2)}) %collective-permute-start.13) | collective-permute-done | bytes 544 | tf_op jit(solution)/shard_map/ppermute | solution.py:275
  (40 shorter events, 3.6 us)
Async XLA Ops:
  2.1 30.6 %all-to-all-start = ((bf16[32,16,256]{2,1,0:T(8,128)(2,1)}), bf16[32,16,256]{2,1,0:T(8,128)(2,1)S(1)}, u32[]{:S(2)}, u32[]{:S(2)}) async-start(bf16[32,16,256]{2,1,0:T(8,128)(2,1)} %bitcast.3), calls=%async_computation | async-start | bytes 524288 | tf_op jit(solution)/shard_map/all_to_all | solution.py:182
  19.4 11.6 %collective-permute-start.2 = (bf16[6,32,512]{2,0,1:T(8,128)(2,1)S(1)}, bf16[6,32,512]{2,0,1:T(8,128)(2,1)S(1)}, u32[]{:S(2)}, u32[]{:S(2)}) collective-permute-start(bf16[6,32,512]{2,0,1:T(8,128)(2,1)S(1)} %get-tuple-element.27), channel_id=1, source_target_pairs={{0,384},{1,385},{2,386},{3,387},{4,388},{5,389},{6,390},{7,391},{8... | collective-permute-start | bytes 589832 | tf_op jit(solution)/shard_map/ppermute | solution.py:43
  20.7 10.3 %collective-permute-start.1 = (bf16[6,32,512]{2,0,1:T(8,128)(2,1)S(1)}, bf16[6,32,512]{2,0,1:T(8,128)(2,1)S(1)}, u32[]{:S(2)}, u32[]{:S(2)}) collective-permute-start(bf16[6,32,512]{2,0,1:T(8,128)(2,1)S(1)} %get-tuple-element.28), channel_id=1, source_target_pairs={{0,256},{1,257},{2,258},{3,259},{4,260},{5,261},{6,262},{7,263},{8... | collective-permute-start | bytes 589832 | tf_op jit(solution)/shard_map/ppermute | solution.py:43
  21.4 9.6 %collective-permute-start = (bf16[6,32,512]{2,0,1:T(8,128)(2,1)S(1)}, bf16[6,32,512]{2,0,1:T(8,128)(2,1)S(1)}, u32[]{:S(2)}, u32[]{:S(2)}) collective-permute-start(bf16[6,32,512]{2,0,1:T(8,128)(2,1)S(1)} %get-tuple-element.26), channel_id=1, source_target_pairs={{0,128},{1,129},{2,130},{3,131},{4,132},{5,133},{6,134},{7,135},{8... | collective-permute-start | bytes 589832 | tf_op jit(solution)/shard_map/ppermute | solution.py:43
  33.7 22.8 %all-to-all-start.1 = ((bf16[4,512,256]{2,1,0:T(8,128)(2,1)}), bf16[4,512,256]{2,1,0:T(8,128)(2,1)S(1)}, u32[]{:S(2)}, u32[]{:S(2)}) async-start(bf16[4,512,256]{2,1,0:T(8,128)(2,1)} %broadcast_in_dim.6), calls=%async_computation.1 | async-start | bytes 2097152 | tf_op jit(solution)/shard_map/all_to_all | solution.py:64
  43.0 53.6 %collective-permute-start.5 = (bf16[128,32,256]{2,1,0:T(8,128)(2,1)}, bf16[128,32,256]{2,1,0:T(8,128)(2,1)S(1)}, u32[]{:S(2)}, u32[]{:S(2)}) collective-permute-start(bf16[128,32,256]{2,1,0:T(8,128)(2,1)} %constant_dynamic-slice_fusion.1), channel_id=1, source_target_pairs={{0,1},{1,0},{2,3},{3,2},{4,5},{5,4},{6,7},{7,6},{8,9},{9,8},{10,11... | collective-permute-start | bytes 6291464 | tf_op jit(solution)/shard_map/ppermute | solution.py:32
  45.3 7.7 %collective-permute-start.4 = (bf16[6,16]{1,0:T(8,128)(2,1)S(1)}, bf16[6,16]{1,0:T(8,128)(2,1)S(1)}, u32[]{:S(2)}, u32[]{:S(2)}) collective-permute-start(bf16[6,16]{1,0:T(8,128)(2,1)S(1)} %constant_dynamic-slice_fusion), channel_id=1, source_target_pairs={{0,1},{1,0},{2,3},{3,2},{4,5},{5,4},{6,7},{7,6},{8,9},{9,8},{10,11... | collective-permute-start | bytes 584 | tf_op jit(solution)/shard_map/ppermute | solution.py:32
  47.7 8.2 %collective-permute-start.3 = (bf16[6,32,512]{2,0,1:T(8,128)(2,1)}, bf16[6,32,512]{2,0,1:T(8,128)(2,1)S(1)}, u32[]{:S(2)}, u32[]{:S(2)}) collective-permute-start(bf16[6,32,512]{2,0,1:T(8,128)(2,1)} %fusion.2), channel_id=1, source_target_pairs={{0,32},{128,160},{256,288},{384,416},{1,33},{129,161},{257,289},{3... | collective-permute-start | bytes 589832 | tf_op jit(solution)/shard_map/ppermute | solution.py:50
  49.0 14.5 %collective-permute-start.7 = (bf16[6,32,512]{2,0,1:T(8,128)(2,1)}, bf16[6,32,512]{2,0,1:T(8,128)(2,1)}, u32[]{:S(2)}, u32[]{:S(2)}) collective-permute-start(bf16[6,32,512]{2,0,1:T(8,128)(2,1)} %fusion.2), channel_id=1, source_target_pairs={{0,96},{128,224},{256,352},{384,480},{1,97},{129,225},{257,353},{3... | collective-permute-start | bytes 589832 | tf_op jit(solution)/shard_map/ppermute | solution.py:50
  51.0 16.3 %collective-permute-start.6 = (bf16[6,32,512]{2,0,1:T(8,128)(2,1)}, bf16[6,32,512]{2,0,1:T(8,128)(2,1)}, u32[]{:S(2)}, u32[]{:S(2)}) collective-permute-start(bf16[6,32,512]{2,0,1:T(8,128)(2,1)} %fusion.2), channel_id=1, source_target_pairs={{0,64},{128,192},{256,320},{384,448},{1,65},{129,193},{257,321},{3... | collective-permute-start | bytes 589832 | tf_op jit(solution)/shard_map/ppermute | solution.py:50
  55.9 7.6 %copy-start.2 = (bf16[6,32,512]{2,0,1:T(8,128)(2,1)}, bf16[6,32,512]{2,0,1:T(8,128)(2,1)S(1)}, u32[]{:S(2)}) copy-start(bf16[6,32,512]{2,0,1:T(8,128)(2,1)S(1)} %collective-permute-done.3) | copy-start | bytes 589828
  56.5 32.5 %collective-permute-start.9 = (bf16[4,512,256]{2,1,0:T(8,128)(2,1)S(1)}, bf16[4,512,256]{2,1,0:T(8,128)(2,1)S(1)}, u32[]{:S(2)}, u32[]{:S(2)}) collective-permute-start(bf16[4,512,256]{2,1,0:T(8,128)(2,1)S(1)} %all-to-all-done.1.refs_0_), channel_id=1, source_target_pairs={{0,32},{32,64},{64,96},{96,16},{16,48},{48,80},{80,112},{112,0},{1... | collective-permute-start | bytes 3145736 | tf_op jit(solution)/shard_map/ppermute | solution.py:28
  60.2 33.2 %collective-permute-start.11 = (bf16[4,512,256]{2,1,0:T(8,128)(2,1)S(1)}, bf16[4,512,256]{2,1,0:T(8,128)(2,1)S(1)}, u32[]{:S(2)}, u32[]{:S(2)}) collective-permute-start(bf16[4,512,256]{2,1,0:T(8,128)(2,1)S(1)} %all-to-all-done.1.refs_0_), channel_id=1, source_target_pairs={{0,112},{32,0},{64,32},{96,64},{16,96},{48,16},{80,48},{112,80},{1... | collective-permute-start | bytes 3145736 | tf_op jit(solution)/shard_map/ppermute | solution.py:28
  82.5 14.1 %collective-permute-start.8 = (bf16[4,6,32,512]{3,2,1,0:T(8,128)(2,1)S(1)}, bf16[4,6,32,512]{3,2,1,0:T(8,128)(2,1)S(1)}, u32[]{:S(2)}, u32[]{:S(2)}) collective-permute-start(bf16[4,6,32,512]{3,2,1,0:T(8,128)(2,1)S(1)} %all_to_all.20.w_own.refs_3_), channel_id=1, source_target_pairs={{0,1},{1,0},{2,3},{3,2},{4,5},{5,4},{6,7},{7,6},{8,9},{9,8},{10,11... | collective-permute-start | bytes 2359304 | tf_op jit(solution)/shard_map/ppermute | solution.py:32
  89.0 19.5 %collective-permute-start.10 = (bf16[2,512,256]{2,1,0:T(8,128)(2,1)S(1)}, bf16[2,512,256]{2,1,0:T(8,128)(2,1)S(1)}, u32[]{:S(2)}, u32[]{:S(2)}) collective-permute-start(bf16[2,512,256]{2,1,0:T(8,128)(2,1)S(1)} %slice.55), channel_id=1, source_target_pairs={{0,32},{32,64},{64,96},{96,16},{16,48},{48,80},{80,112},{112,0},{1... | collective-permute-start | bytes 1572872 | tf_op jit(solution)/shard_map/ppermute | solution.py:28
  93.5 15.4 %copy-start = (bf16[128,32,512]{2,1,0:T(8,128)(2,1)S(1)}, bf16[128,32,512]{2,1,0:T(8,128)(2,1)}, u32[]{:S(2)}) copy-start(bf16[128,32,512]{2,1,0:T(8,128)(2,1)} %refs_1_.1) | copy-start | bytes 12582916
  93.5 15.4 %copy-start.1 = (f32[16,16]{1,0:T(8,128)S(1)}, f32[16,16]{1,0:T(8,128)}, u32[]{:S(2)}) copy-start(f32[16,16]{1,0:T(8,128)} %refs_5_.1) | copy-start | bytes 3076
  93.5 15.4 %collective-permute-start.12 = (bf16[2,512,256]{2,1,0:T(8,128)(2,1)S(1)}, bf16[2,512,256]{2,1,0:T(8,128)(2,1)S(1)}, u32[]{:S(2)}, u32[]{:S(2)}) collective-permute-start(bf16[2,512,256]{2,1,0:T(8,128)(2,1)S(1)} %slice.56), channel_id=1, source_target_pairs={{0,112},{32,0},{64,32},{96,64},{16,96},{48,16},{80,48},{112,80},{1... | collective-permute-start | bytes 1572872 | tf_op jit(solution)/shard_map/ppermute | solution.py:28
  108.9 31.9 %copy-start.4 = (f32[512]{0:T(512)S(1)}, f32[512]{0:T(512)}, u32[]{:S(2)}) copy-start(f32[512]{0:T(512)} %param.10) | copy-start | bytes 6148
  108.9 45.7 %copy-start.3 = (f32[1,6,16]{2,0,1:T(1,128)S(1)}, f32[1,6,16]{2,0,1:T(1,128)}, u32[]{:S(2)}) copy-start(f32[1,6,16]{2,0,1:T(1,128)} %param.9) | copy-start | bytes 1156
  108.9 45.7 %slice-start = ((f32[512]{0:T(512)}), f32[6]{0:T(128)S(1)}, s32[]{:S(2)}) async-start(f32[512]{0:T(512)} %param.10), calls=%async_computation.4 | async-start | bytes 1024 | tf_op jit(solution)/shard_map/slice | solution.py:281
  138.2 16.2 %collective-permute-start.13 = (f32[1,128]{1,0:T(1,128)S(1)}, f32[1,128]{1,0:T(1,128)S(1)}, u32[]{:S(2)}, u32[]{:S(2)}) collective-permute-start(f32[1,128]{1,0:T(1,128)S(1)} %bitcast.36), channel_id=1, source_target_pairs={{0,0},{1,1},{2,32},{3,33},{4,64},{5,65},{6,96},{7,97},{8,128},{9,1... | collective-permute-start | bytes 1544 | tf_op jit(solution)/shard_map/ppermute | solution.py:275

commit v6 on v5

--- a/solution.py
+++ b/solution.py
@@ -184,7 +184,7 @@
 
     scattered = window_scattered(factors, rows)
     f_other = lax.dynamic_slice_in_dim(factors, (1 - core) * half, half, 2)
-    amp, scattered, f_other = lax.optimization_barrier((amp, scattered, f_other))
+    amp, f_other = lax.optimization_barrier((amp, f_other))
     f_other = swapped(f_other)
 
     start = (aux_index * columns) % half

time: 157 us -> 153 us (0.975)
  blocking collectives: 38 us -> 33.1 us
    ppermute x3, waiting for transfers between devices: 5.81 us -> 0.01 us  [window_scattered(): mine = mine + lax.ppermute(pieces[i], PAIR, [(0, i * lows)])]
    all_to_all x1, starting transfers between devices: 9.34 us -> 4.77 us  [collected(): lax.all_to_all(jnp.broadcast_to(array[None], (parts, *array.shape)), 'x',...]
    all_to_all x1, waiting for transfers between devices: 0.88 us -> 5.19 us  [per_device(): lax.all_to_all(sent.reshape(-1, *split.shape[1:]), AUX, 0, 0, tiled=True)]
    all_to_all x1, blocking collectives: 24.1 us -> 19.9 us  [per_device(): summed = jnp.sum(lax.all_to_all(tiles, AUX, 0, 0, tiled=True), axis=0)]
    ppermute x3, starting transfers between devices: 5.27 us -> 9.29 us  [window_spread(): lax.ppermute(mine, PAIR, [(i * lows, i * lows + k) for i in range(parts)])]
  transfers between devices with their start and end apart: 16 -> 16, of which waited for: 8 -> 6; matrix products, arithmetic and copies ran while one was open for 4% -> 7% of each run, Pallas kernels for 8% -> 8%
where the time goes in v6:
time: 153 us
  starting transfers between devices  56.9 us (37%)
  blocking collectives  33.1 us (22%)
  waiting for transfers between devices  31.1 us (20%)
  Pallas kernels  17 us (11%)
  local copies, waits for them, and re-layouts  9.55 us (6%)
  other arithmetic  3.34 us (2%)
  between operations  1.54 us (1%)
    all_to_all x1, blocking collectives, per_device(): summed = jnp.sum(lax.all_to_all(tiles, AUX, 0, 0, tiled=True), axis=0)  19.9 us
    all_to_all x1, starting transfers between devices, per_device(): lax.all_to_all(sent.reshape(-1, *split.shape[1:]), AUX, 0, 0, tiled=True)  16 us
    ppermute x4, starting transfers between devices, shifted(): lax.ppermute(array, Y, [(index(y), index((y + by) % full)) for y in range...  14.5 us
    ppermute x1, waiting for transfers between devices, per_device(): summed = lax.ppermute(summed, AXES, moves)  13.4 us
    all_to_all x1, blocking collectives, collected(): lax.all_to_all(jnp.broadcast_to(array[None], (parts, *array.shape)), 'x',...  13.2 us
    pallas_call x1, Pallas kernels, early(): pl.pallas_call(early_kernel, grid_spec=pltpu.PrefetchScalarGridSpec(num_s...  11.9 us
    ppermute x3, starting transfers between devices, window_spread(): lax.ppermute(mine, PAIR, [(i * lows, i * lows + k) for i in range(parts)])  9.29 us
    ppermute x3, waiting for transfers between devices, window_spread(): lax.ppermute(mine, PAIR, [(i * lows, i * lows + k) for i in range(parts)])  7.13 us
  transfers between devices with their start and end apart: 16, of which 6 were waited for; matrix products, arithmetic and copies ran while one was open for 7% of the time, Pallas kernels for 8%

profile of v6, /device:TPU:6, one launch (start us, length us, event | category | flops | bytes accessed | tf_op | source)
XLA Modules:
  0.0 152.6 jit_solution(5427799535570713829)
XLA Ops:
  0.6 0.7 slice_bitcast_fusion.2
  2.1 16.0 %all-to-all-start = ((bf16[32,16,256]{2,1,0:T(8,128)(2,1)}), bf16[32,16,256]{2,1,0:T(8,128)(2,1)S(1)}, u32[]{:S(2)}, u32[]{:S(2)}) async-start(bf16[32,16,256]{2,1,0:T(8,128)(2,1)} %bitcast.3), calls=%async_computation | async-start | bytes 524288 | tf_op jit(solution)/shard_map/all_to_all | solution.py:182
  18.0 1.3 slice_bitcast_fusion
  19.3 1.0 fusion.3
  20.3 1.3 collective-permute-start.2
  21.6 1.4 collective-permute-start.1
  23.0 1.4 collective-permute-start
  24.3 3.1 %constant_dynamic-slice_fusion.1 = bf16[128,32,256]{2,1,0:T(8,128)(2,1)} fusion(bf16[128,32,512]{2,1,0:T(8,128)(2,1)} %refs_1_.1, s32[]{:T(128)S(6)} %select_n.89), kind=kLoop, calls=%fused_computation.13 | loop fusion | bytes 4194308 | tf_op jit(solution)/shard_map/dynamic_slice | solution.py:186
  27.4 5.2 %all-to-all-done = bf16[32,16,256]{2,1,0:T(8,128)(2,1)S(1)} async-done(((bf16[32,16,256]{2,1,0:T(8,128)(2,1)}), bf16[32,16,256]{2,1,0:T(8,128)(2,1)S(1)}, u32[]{:S(2)}, u32[]{:S(2)}) %all-to-all-start) | async-done | bytes 262176 | tf_op jit(solution)/shard_map/all_to_all | solution.py:182
  32.6 1.0 broadcast_in_dim.6
  33.7 4.8 %all-to-all-start.1 = ((bf16[4,512,256]{2,1,0:T(8,128)(2,1)}), bf16[4,512,256]{2,1,0:T(8,128)(2,1)S(1)}, u32[]{:S(2)}, u32[]{:S(2)}) async-start(bf16[4,512,256]{2,1,0:T(8,128)(2,1)} %broadcast_in_dim.6), calls=%async_computation.1 | async-start | bytes 2097152 | tf_op jit(solution)/shard_map/all_to_all | solution.py:64
  38.5 1.9 %collective-permute-start.5 = (bf16[128,32,256]{2,1,0:T(8,128)(2,1)}, bf16[128,32,256]{2,1,0:T(8,128)(2,1)S(1)}, u32[]{:S(2)}, u32[]{:S(2)}) collective-permute-start(bf16[128,32,256]{2,1,0:T(8,128)(2,1)} %constant_dynamic-slice_fusion.1), channel_id=1, source_target_pairs={{0,1},{1,0},{2,3},{3,2},{4,5},{5,4},{6,7},{7,6},{8,9},{9,8},{10,11... | collective-permute-start | bytes 6291464 | tf_op jit(solution)/shard_map/ppermute | solution.py:32
  40.5 2.0 %fusion.2 = bf16[6,32,512]{2,0,1:T(8,128)(2,1)} fusion(bf16[6,32,512]{2,0,1:T(8,128)(2,1)} %collective-permute-done.2, bf16[6,32,512]{2,0,1:T(8,128)(2,1)} %collective-permute-done.1, bf16[6,32,512]{2,0,1:T(8,128)(2,1)} %collective-permute-done, bf16[6,128,512]{2,0,1:T(8,128)(2,1)} %copy-done.2, pred[]{:T(512)S(6)} %and.56), kind=kLoop, calls=%fused_computation.4 | loop fusion | flops 393216 | bytes 983041 | tf_op jit(solution)/shard_map/add | solution.py:43
  42.5 2.4 %collective-permute-start.4 = (bf16[6,16]{1,0:T(8,128)(2,1)S(1)}, bf16[6,16]{1,0:T(8,128)(2,1)S(1)}, u32[]{:S(2)}, u32[]{:S(2)}) collective-permute-start(bf16[6,16]{1,0:T(8,128)(2,1)S(1)} %constant_dynamic-slice_fusion), channel_id=1, source_target_pairs={{0,1},{1,0},{2,3},{3,2},{4,5},{5,4},{6,7},{7,6},{8,9},{9,8},{10,11... | collective-permute-start | bytes 584 | tf_op jit(solution)/shard_map/ppermute | solution.py:32
  44.9 5.3 %collective-permute-start.3 = (bf16[6,32,512]{2,0,1:T(8,128)(2,1)}, bf16[6,32,512]{2,0,1:T(8,128)(2,1)S(1)}, u32[]{:S(2)}, u32[]{:S(2)}) collective-permute-start(bf16[6,32,512]{2,0,1:T(8,128)(2,1)} %fusion.2), channel_id=1, source_target_pairs={{0,32},{128,160},{256,288},{384,416},{1,33},{129,161},{257,289},{3... | collective-permute-start | bytes 589832 | tf_op jit(solution)/shard_map/ppermute | solution.py:50
  50.2 2.0 %collective-permute-start.7 = (bf16[6,32,512]{2,0,1:T(8,128)(2,1)}, bf16[6,32,512]{2,0,1:T(8,128)(2,1)}, u32[]{:S(2)}, u32[]{:S(2)}) collective-permute-start(bf16[6,32,512]{2,0,1:T(8,128)(2,1)} %fusion.2), channel_id=1, source_target_pairs={{0,96},{128,224},{256,352},{384,480},{1,97},{129,225},{257,353},{3... | collective-permute-start | bytes 589832 | tf_op jit(solution)/shard_map/ppermute | solution.py:50
  52.2 2.0 %collective-permute-start.6 = (bf16[6,32,512]{2,0,1:T(8,128)(2,1)}, bf16[6,32,512]{2,0,1:T(8,128)(2,1)}, u32[]{:S(2)}, u32[]{:S(2)}) collective-permute-start(bf16[6,32,512]{2,0,1:T(8,128)(2,1)} %fusion.2), channel_id=1, source_target_pairs={{0,64},{128,192},{256,320},{384,448},{1,65},{129,193},{257,321},{3... | collective-permute-start | bytes 589832 | tf_op jit(solution)/shard_map/ppermute | solution.py:50
  54.3 2.9 %collective-permute-done.3 = bf16[6,32,512]{2,0,1:T(8,128)(2,1)S(1)} collective-permute-done((bf16[6,32,512]{2,0,1:T(8,128)(2,1)}, bf16[6,32,512]{2,0,1:T(8,128)(2,1)S(1)}, u32[]{:S(2)}, u32[]{:S(2)}) %collective-permute-start.3) | collective-permute-done | bytes 196640 | tf_op jit(solution)/shard_map/ppermute | solution.py:50
  57.2 4.3 %collective-permute-start.9 = (bf16[4,512,256]{2,1,0:T(8,128)(2,1)S(1)}, bf16[4,512,256]{2,1,0:T(8,128)(2,1)S(1)}, u32[]{:S(2)}, u32[]{:S(2)}) collective-permute-start(bf16[4,512,256]{2,1,0:T(8,128)(2,1)S(1)} %all-to-all-done.1.refs_0_), channel_id=1, source_target_pairs={{0,32},{32,64},{64,96},{96,16},{16,48},{48,80},{80,112},{112,0},{1... | collective-permute-start | bytes 3145736 | tf_op jit(solution)/shard_map/ppermute | solution.py:28
  61.5 2.8 %collective-permute-start.11 = (bf16[4,512,256]{2,1,0:T(8,128)(2,1)S(1)}, bf16[4,512,256]{2,1,0:T(8,128)(2,1)S(1)}, u32[]{:S(2)}, u32[]{:S(2)}) collective-permute-start(bf16[4,512,256]{2,1,0:T(8,128)(2,1)S(1)} %all-to-all-done.1.refs_0_), channel_id=1, source_target_pairs={{0,112},{32,0},{64,32},{96,64},{16,96},{48,16},{80,48},{112,80},{1... | collective-permute-start | bytes 3145736 | tf_op jit(solution)/shard_map/ppermute | solution.py:28
  64.2 4.3 %collective-permute-done.6 = bf16[6,32,512]{2,0,1:T(8,128)(2,1)} collective-permute-done((bf16[6,32,512]{2,0,1:T(8,128)(2,1)}, bf16[6,32,512]{2,0,1:T(8,128)(2,1)}, u32[]{:S(2)}, u32[]{:S(2)}) %collective-permute-start.6) | collective-permute-done | bytes 196640 | tf_op jit(solution)/shard_map/ppermute | solution.py:50
  68.5 1.2 add_add_fusion
  69.8 13.2 %all_to_all.20.w_own.refs_3_ = bf16[4,6,32,512]{3,2,1,0:T(8,128)(2,1)S(1)} all-to-all(bf16[4,6,32,512]{3,2,1,0:T(8,128)(2,1)S(1)} %broadcast_in_dim.7), channel_id=1, replica_groups=mesh['x'=4,'ylo'=4,'yhi'=2,'z'=8,'core'=2] {'x'}, dimensions={0} | all-to-all | bytes 1572864 | tf_op jit(solution)/shard_map/all_to_all | solution.py:64
  83.0 1.9 %collective-permute-start.8 = (bf16[4,6,32,512]{3,2,1,0:T(8,128)(2,1)S(1)}, bf16[4,6,32,512]{3,2,1,0:T(8,128)(2,1)S(1)}, u32[]{:S(2)}, u32[]{:S(2)}) collective-permute-start(bf16[4,6,32,512]{3,2,1,0:T(8,128)(2,1)S(1)} %all_to_all.20.w_own.refs_3_), channel_id=1, source_target_pairs={{0,1},{1,0},{2,3},{3,2},{4,5},{5,4},{6,7},{7,6},{8,9},{9,8},{10,11... | collective-permute-start | bytes 2359304 | tf_op jit(solution)/shard_map/ppermute | solution.py:32
  84.9 5.0 %collective-permute-done.9.refs_1_ = bf16[4,512,256]{2,1,0:T(8,128)(2,1)S(1)} collective-permute-done((bf16[4,512,256]{2,1,0:T(8,128)(2,1)S(1)}, bf16[4,512,256]{2,1,0:T(8,128)(2,1)S(1)}, u32[]{:S(2)}, u32[]{:S(2)}) %collective-permute-start.9) | collective-permute-done | bytes 1048608 | tf_op jit(solution)/shard_map/ppermute | solution.py:28
  90.0 4.4 %collective-permute-start.10 = (bf16[2,512,256]{2,1,0:T(8,128)(2,1)S(1)}, bf16[2,512,256]{2,1,0:T(8,128)(2,1)S(1)}, u32[]{:S(2)}, u32[]{:S(2)}) collective-permute-start(bf16[2,512,256]{2,1,0:T(8,128)(2,1)S(1)} %slice.55), channel_id=1, source_target_pairs={{0,32},{32,64},{64,96},{96,16},{16,48},{48,80},{80,112},{112,0},{1... | collective-permute-start | bytes 1572872 | tf_op jit(solution)/shard_map/ppermute | solution.py:28
  94.4 3.1 %collective-permute-start.12 = (bf16[2,512,256]{2,1,0:T(8,128)(2,1)S(1)}, bf16[2,512,256]{2,1,0:T(8,128)(2,1)S(1)}, u32[]{:S(2)}, u32[]{:S(2)}) collective-permute-start(bf16[2,512,256]{2,1,0:T(8,128)(2,1)S(1)} %slice.56), channel_id=1, source_target_pairs={{0,112},{32,0},{64,32},{96,64},{16,96},{48,16},{80,48},{112,80},{1... | collective-permute-start | bytes 1572872 | tf_op jit(solution)/shard_map/ppermute | solution.py:28
  97.6 11.9 %shard_map.77 = (f32[72,256]{1,0:T(8,128)S(1)}, f32[12,8,256]{2,1,0:T(8,128)S(1)}) custom-call(s32[19]{0:T(128)S(1)} %concatenate.3.scalars.refs_0_, bf16[128,32,512]{2,1,0:T(8,128)(2,1)} %refs_1_.1, bf16[128,32,256]{2,1,0:T(8,128)(2,1)S(1)} %collective-permute-done.5.f_other.refs_2_, bf16[4,6,32,512]{3,2,1,0:T(8,128)(2,1)S(1)} %all_to_all.20.w_own.refs_3_, ...), custom_call_target="tpu_custom_call" | custom-call | flops 12000000 | bytes 100000 | tf_op jit(solution)/shard_map/pallas_call | solution.py:230
  109.9 5.1 %shard_map.78 = f32[32,1,128]{2,1,0:T(1,128)S(1)} custom-call(s32[19]{0:T(128)S(1)} %concatenate.3.scalars.refs_0_, bf16[128,32,512]{2,1,0:T(8,128)(2,1)S(1)} %copy-done, bf16[128,32,256]{2,1,0:T(8,128)(2,1)S(1)} %collective-permute-done.5.f_other.refs_2_, bf16[4,6,32,512]{3,2,1,0:T(8,128)(2,1)S(1)} %all_to_all.20.w_own.refs_3_, ...), custom_call_target="tpu_custom_call" | custom-call | flops 4000000 | bytes 100000 | tf_op jit(solution)/shard_map/pallas_call | solution.py:250
  115.0 19.9 %all_to_all.21 = f32[32,1,128]{2,1,0:T(1,128)S(1)} all-to-all(f32[32,1,128]{2,1,0:T(1,128)S(1)} %shard_map.78), channel_id=1, replica_groups=mesh['x'=4,'ylo'=4,'yhi'=2,'z'=8,'core'=2] {'yhi','z','core'}, dimensions={0} | all-to-all | bytes 32768 | tf_op jit(solution)/shard_map/all_to_all | solution.py:268
  135.0 2.1 %collective-permute-start.13 = (f32[1,128]{1,0:T(1,128)S(1)}, f32[1,128]{1,0:T(1,128)S(1)}, u32[]{:S(2)}, u32[]{:S(2)}) collective-permute-start(f32[1,128]{1,0:T(1,128)S(1)} %bitcast.36), channel_id=1, source_target_pairs={{0,0},{1,1},{2,32},{3,33},{4,64},{5,65},{6,96},{7,97},{8,128},{9,1... | collective-permute-start | bytes 1544 | tf_op jit(solution)/shard_map/ppermute | solution.py:275
  137.8 13.4 %collective-permute-done.13 = f32[1,128]{1,0:T(1,128)S(1)} collective-permute-done((f32[1,128]{1,0:T(1,128)S(1)}, f32[1,128]{1,0:T(1,128)S(1)}, u32[]{:S(2)}, u32[]{:S(2)}) %collective-permute-start.13) | collective-permute-done | bytes 544 | tf_op jit(solution)/shard_map/ppermute | solution.py:275
  (40 shorter events, 3.1 us)
Async XLA Ops:
  2.1 30.6 %all-to-all-start = ((bf16[32,16,256]{2,1,0:T(8,128)(2,1)}), bf16[32,16,256]{2,1,0:T(8,128)(2,1)S(1)}, u32[]{:S(2)}, u32[]{:S(2)}) async-start(bf16[32,16,256]{2,1,0:T(8,128)(2,1)} %bitcast.3), calls=%async_computation | async-start | bytes 524288 | tf_op jit(solution)/shard_map/all_to_all | solution.py:182
  19.3 14.3 %copy-start.2 = (bf16[6,128,512]{2,0,1:T(8,128)(2,1)}, bf16[6,128,512]{2,0,1:T(8,128)(2,1)S(1)}, u32[]{:S(2)}) copy-start(bf16[6,128,512]{2,0,1:T(8,128)(2,1)S(1)} %slice_bitcast_fusion) | copy-start | bytes 2359300
  20.3 20.1 %collective-permute-start.2 = (bf16[6,32,512]{2,0,1:T(8,128)(2,1)}, bf16[6,32,512]{2,0,1:T(8,128)(2,1)}, u32[]{:S(2)}, u32[]{:S(2)}) collective-permute-start(bf16[6,32,512]{2,0,1:T(8,128)(2,1)} %get-tuple-element.25), channel_id=1, source_target_pairs={{0,384},{1,385},{2,386},{3,387},{4,388},{5,389},{6,390},{7,391},{8... | collective-permute-start | bytes 589832 | tf_op jit(solution)/shard_map/ppermute | solution.py:43
  21.6 18.9 %collective-permute-start.1 = (bf16[6,32,512]{2,0,1:T(8,128)(2,1)}, bf16[6,32,512]{2,0,1:T(8,128)(2,1)}, u32[]{:S(2)}, u32[]{:S(2)}) collective-permute-start(bf16[6,32,512]{2,0,1:T(8,128)(2,1)} %get-tuple-element.26), channel_id=1, source_target_pairs={{0,256},{1,257},{2,258},{3,259},{4,260},{5,261},{6,262},{7,263},{8... | collective-permute-start | bytes 589832 | tf_op jit(solution)/shard_map/ppermute | solution.py:43
  23.0 17.5 %collective-permute-start = (bf16[6,32,512]{2,0,1:T(8,128)(2,1)}, bf16[6,32,512]{2,0,1:T(8,128)(2,1)}, u32[]{:S(2)}, u32[]{:S(2)}) collective-permute-start(bf16[6,32,512]{2,0,1:T(8,128)(2,1)} %get-tuple-element.24), channel_id=1, source_target_pairs={{0,128},{1,129},{2,130},{3,131},{4,132},{5,133},{6,134},{7,135},{8... | collective-permute-start | bytes 589832 | tf_op jit(solution)/shard_map/ppermute | solution.py:43
  33.7 23.5 %all-to-all-start.1 = ((bf16[4,512,256]{2,1,0:T(8,128)(2,1)}), bf16[4,512,256]{2,1,0:T(8,128)(2,1)S(1)}, u32[]{:S(2)}, u32[]{:S(2)}) async-start(bf16[4,512,256]{2,1,0:T(8,128)(2,1)} %broadcast_in_dim.6), calls=%async_computation.1 | async-start | bytes 2097152 | tf_op jit(solution)/shard_map/all_to_all | solution.py:64
  38.5 59.0 %collective-permute-start.5 = (bf16[128,32,256]{2,1,0:T(8,128)(2,1)}, bf16[128,32,256]{2,1,0:T(8,128)(2,1)S(1)}, u32[]{:S(2)}, u32[]{:S(2)}) collective-permute-start(bf16[128,32,256]{2,1,0:T(8,128)(2,1)} %constant_dynamic-slice_fusion.1), channel_id=1, source_target_pairs={{0,1},{1,0},{2,3},{3,2},{4,5},{5,4},{6,7},{7,6},{8,9},{9,8},{10,11... | collective-permute-start | bytes 6291464 | tf_op jit(solution)/shard_map/ppermute | solution.py:32
  42.5 11.7 %collective-permute-start.4 = (bf16[6,16]{1,0:T(8,128)(2,1)S(1)}, bf16[6,16]{1,0:T(8,128)(2,1)S(1)}, u32[]{:S(2)}, u32[]{:S(2)}) collective-permute-start(bf16[6,16]{1,0:T(8,128)(2,1)S(1)} %constant_dynamic-slice_fusion), channel_id=1, source_target_pairs={{0,1},{1,0},{2,3},{3,2},{4,5},{5,4},{6,7},{7,6},{8,9},{9,8},{10,11... | collective-permute-start | bytes 584 | tf_op jit(solution)/shard_map/ppermute | solution.py:32
  44.9 12.3 %collective-permute-start.3 = (bf16[6,32,512]{2,0,1:T(8,128)(2,1)}, bf16[6,32,512]{2,0,1:T(8,128)(2,1)S(1)}, u32[]{:S(2)}, u32[]{:S(2)}) collective-permute-start(bf16[6,32,512]{2,0,1:T(8,128)(2,1)} %fusion.2), channel_id=1, source_target_pairs={{0,32},{128,160},{256,288},{384,416},{1,33},{129,161},{257,289},{3... | collective-permute-start | bytes 589832 | tf_op jit(solution)/shard_map/ppermute | solution.py:50
  50.2 14.0 %collective-permute-start.7 = (bf16[6,32,512]{2,0,1:T(8,128)(2,1)}, bf16[6,32,512]{2,0,1:T(8,128)(2,1)}, u32[]{:S(2)}, u32[]{:S(2)}) collective-permute-start(bf16[6,32,512]{2,0,1:T(8,128)(2,1)} %fusion.2), channel_id=1, source_target_pairs={{0,96},{128,224},{256,352},{384,480},{1,97},{129,225},{257,353},{3... | collective-permute-start | bytes 589832 | tf_op jit(solution)/shard_map/ppermute | solution.py:50
  52.2 16.3 %collective-permute-start.6 = (bf16[6,32,512]{2,0,1:T(8,128)(2,1)}, bf16[6,32,512]{2,0,1:T(8,128)(2,1)}, u32[]{:S(2)}, u32[]{:S(2)}) collective-permute-start(bf16[6,32,512]{2,0,1:T(8,128)(2,1)} %fusion.2), channel_id=1, source_target_pairs={{0,64},{128,192},{256,320},{384,448},{1,65},{129,193},{257,321},{3... | collective-permute-start | bytes 589832 | tf_op jit(solution)/shard_map/ppermute | solution.py:50
  57.2 32.7 %collective-permute-start.9 = (bf16[4,512,256]{2,1,0:T(8,128)(2,1)S(1)}, bf16[4,512,256]{2,1,0:T(8,128)(2,1)S(1)}, u32[]{:S(2)}, u32[]{:S(2)}) collective-permute-start(bf16[4,512,256]{2,1,0:T(8,128)(2,1)S(1)} %all-to-all-done.1.refs_0_), channel_id=1, source_target_pairs={{0,32},{32,64},{64,96},{96,16},{16,48},{48,80},{80,112},{112,0},{1... | collective-permute-start | bytes 3145736 | tf_op jit(solution)/shard_map/ppermute | solution.py:28
  61.5 32.9 %collective-permute-start.11 = (bf16[4,512,256]{2,1,0:T(8,128)(2,1)S(1)}, bf16[4,512,256]{2,1,0:T(8,128)(2,1)S(1)}, u32[]{:S(2)}, u32[]{:S(2)}) collective-permute-start(bf16[4,512,256]{2,1,0:T(8,128)(2,1)S(1)} %all-to-all-done.1.refs_0_), channel_id=1, source_target_pairs={{0,112},{32,0},{64,32},{96,64},{16,96},{48,16},{80,48},{112,80},{1... | collective-permute-start | bytes 3145736 | tf_op jit(solution)/shard_map/ppermute | solution.py:28
  83.0 14.5 %collective-permute-start.8 = (bf16[4,6,32,512]{3,2,1,0:T(8,128)(2,1)S(1)}, bf16[4,6,32,512]{3,2,1,0:T(8,128)(2,1)S(1)}, u32[]{:S(2)}, u32[]{:S(2)}) collective-permute-start(bf16[4,6,32,512]{3,2,1,0:T(8,128)(2,1)S(1)} %all_to_all.20.w_own.refs_3_), channel_id=1, source_target_pairs={{0,1},{1,0},{2,3},{3,2},{4,5},{5,4},{6,7},{7,6},{8,9},{9,8},{10,11... | collective-permute-start | bytes 2359304 | tf_op jit(solution)/shard_map/ppermute | solution.py:32
  90.0 19.5 %collective-permute-start.10 = (bf16[2,512,256]{2,1,0:T(8,128)(2,1)S(1)}, bf16[2,512,256]{2,1,0:T(8,128)(2,1)S(1)}, u32[]{:S(2)}, u32[]{:S(2)}) collective-permute-start(bf16[2,512,256]{2,1,0:T(8,128)(2,1)S(1)} %slice.55), channel_id=1, source_target_pairs={{0,32},{32,64},{64,96},{96,16},{16,48},{48,80},{80,112},{112,0},{1... | collective-permute-start | bytes 1572872 | tf_op jit(solution)/shard_map/ppermute | solution.py:28
  94.4 15.4 %copy-start = (bf16[128,32,512]{2,1,0:T(8,128)(2,1)S(1)}, bf16[128,32,512]{2,1,0:T(8,128)(2,1)}, u32[]{:S(2)}) copy-start(bf16[128,32,512]{2,1,0:T(8,128)(2,1)} %refs_1_.1) | copy-start | bytes 12582916
  94.4 15.4 %copy-start.1 = (f32[16,16]{1,0:T(8,128)S(1)}, f32[16,16]{1,0:T(8,128)}, u32[]{:S(2)}) copy-start(f32[16,16]{1,0:T(8,128)} %refs_5_.1) | copy-start | bytes 3076
  94.4 15.4 %collective-permute-start.12 = (bf16[2,512,256]{2,1,0:T(8,128)(2,1)S(1)}, bf16[2,512,256]{2,1,0:T(8,128)(2,1)S(1)}, u32[]{:S(2)}, u32[]{:S(2)}) collective-permute-start(bf16[2,512,256]{2,1,0:T(8,128)(2,1)S(1)} %slice.56), channel_id=1, source_target_pairs={{0,112},{32,0},{64,32},{96,64},{16,96},{48,16},{80,48},{112,80},{1... | collective-permute-start | bytes 1572872 | tf_op jit(solution)/shard_map/ppermute | solution.py:28
  109.8 27.9 %copy-start.4 = (f32[512]{0:T(512)S(1)}, f32[512]{0:T(512)}, u32[]{:S(2)}) copy-start(f32[512]{0:T(512)} %param.10) | copy-start | bytes 6148
  109.8 41.5 %copy-start.3 = (f32[1,6,16]{2,0,1:T(1,128)S(1)}, f32[1,6,16]{2,0,1:T(1,128)}, u32[]{:S(2)}) copy-start(f32[1,6,16]{2,0,1:T(1,128)} %param.9) | copy-start | bytes 1156
  109.9 41.4 %slice-start = ((f32[512]{0:T(512)}), f32[6]{0:T(128)S(1)}, s32[]{:S(2)}) async-start(f32[512]{0:T(512)} %param.10), calls=%async_computation.4 | async-start | bytes 1024 | tf_op jit(solution)/shard_map/slice | solution.py:281
  135.0 16.2 %collective-permute-start.13 = (f32[1,128]{1,0:T(1,128)S(1)}, f32[1,128]{1,0:T(1,128)S(1)}, u32[]{:S(2)}, u32[]{:S(2)}) collective-permute-start(f32[1,128]{1,0:T(1,128)S(1)} %bitcast.36), channel_id=1, source_target_pairs={{0,0},{1,1},{2,32},{3,33},{4,64},{5,65},{6,96},{7,97},{8,128},{9,1... | collective-permute-start | bytes 1544 | tf_op jit(solution)/shard_map/ppermute | solution.py:275

commit v7 on v6

--- a/solution.py
+++ b/solution.py
@@ -203,9 +203,7 @@
 
     spread = window_spread(scattered)
     chunk = collected(amp)
-    chunk, spread[0], amp_cols, scalars = lax.optimization_barrier(
-        (chunk, spread[0], amp_cols, scalars)
-    )
+    chunk, amp_cols, scalars = lax.optimization_barrier((chunk, amp_cols, scalars))
     behind, ahead = shifted(chunk, "y", 1), shifted(chunk, "y", -1)
     window = collected(window_quarter(scattered, spread))
     window_other = swapped(window)

time: 153 us -> 153 us (level)
  waiting for transfers between devices: 31.1 us -> 28.4 us
  blocking collectives: 33.1 us -> 35.7 us
    all_to_all x1, blocking collectives: 19.9 us -> 22.5 us  [per_device(): summed = jnp.sum(lax.all_to_all(tiles, AUX, 0, 0, tiled=True), axis=0)]
    ppermute x3, waiting for transfers between devices: 7.13 us -> 4.88 us  [window_spread(): lax.ppermute(mine, PAIR, [(i * lows, i * lows + k) for i in range(parts)])]
  transfers between devices with their start and end apart: 16 -> 16, of which waited for: 6 -> 4; matrix products, arithmetic and copies ran while one was open for 7% -> 7% of each run, Pallas kernels for 8% -> 8%
where the time goes in v7:
time: 153 us; the launch traced here: 152 us
  starting transfers between devices  56.7 us (37%)
  blocking collectives  35.7 us (23%)
  waiting for transfers between devices  28.4 us (19%)
  Pallas kernels  17 us (11%)
  local copies, waits for them, and re-layouts  9.56 us (6%)
  other arithmetic  3.37 us (2%)
  between operations  1.58 us (1%)
    all_to_all x1, blocking collectives, per_device(): summed = jnp.sum(lax.all_to_all(tiles, AUX, 0, 0, tiled=True), axis=0)  22.5 us
    all_to_all x1, starting transfers between devices, per_device(): lax.all_to_all(sent.reshape(-1, *split.shape[1:]), AUX, 0, 0, tiled=True)  16 us
    ppermute x4, starting transfers between devices, shifted(): lax.ppermute(array, Y, [(index(y), index((y + by) % full)) for y in range...  14.9 us
    ppermute x1, waiting for transfers between devices, per_device(): summed = lax.ppermute(summed, AXES, moves)  13.3 us
    all_to_all x1, blocking collectives, collected(): lax.all_to_all(jnp.broadcast_to(array[None], (parts, *array.shape)), 'x',...  13.2 us
    pallas_call x1, Pallas kernels, early(): pl.pallas_call(early_kernel, grid_spec=pltpu.PrefetchScalarGridSpec(num_s...  11.9 us
    ppermute x3, starting transfers between devices, window_spread(): lax.ppermute(mine, PAIR, [(i * lows, i * lows + k) for i in range(parts)])  8.73 us
    ppermute x3, starting transfers between devices, swapped(): return lax.ppermute(array, 'core', [(0, 1), (1, 0)])  6.22 us
  transfers between devices with their start and end apart: 16, of which 4 were waited for; matrix products, arithmetic and copies ran while one was open for 7% of the time, Pallas kernels for 8%

profile of v7, /device:TPU:6, one launch (start us, length us, event | category | flops | bytes accessed | tf_op | source)
XLA Modules:
  0.0 152.3 jit_solution(16850212212989985547)
XLA Ops:
  0.6 0.7 slice_bitcast_fusion.2
  1.4 0.7 tile.7
  2.1 16.0 %all-to-all-start = ((bf16[32,16,256]{2,1,0:T(8,128)(2,1)}), bf16[32,16,256]{2,1,0:T(8,128)(2,1)S(1)}, u32[]{:S(2)}, u32[]{:S(2)}) async-start(bf16[32,16,256]{2,1,0:T(8,128)(2,1)} %bitcast.3), calls=%async_computation | async-start | bytes 524288 | tf_op jit(solution)/shard_map/all_to_all | solution.py:182
  18.0 1.3 slice_bitcast_fusion
  19.3 1.0 fusion.3
  20.3 1.3 collective-permute-start.4
  21.6 1.4 collective-permute-start.3
  23.0 1.4 collective-permute-start.2
  24.3 3.1 %constant_dynamic-slice_fusion.1 = bf16[128,32,256]{2,1,0:T(8,128)(2,1)} fusion(bf16[128,32,512]{2,1,0:T(8,128)(2,1)} %refs_1_.1, s32[]{:T(128)S(6)} %select_n.89), kind=kLoop, calls=%fused_computation.13 | loop fusion | bytes 4194308 | tf_op jit(solution)/shard_map/dynamic_slice | solution.py:186
  27.4 5.2 %all-to-all-done = bf16[32,16,256]{2,1,0:T(8,128)(2,1)S(1)} async-done(((bf16[32,16,256]{2,1,0:T(8,128)(2,1)}), bf16[32,16,256]{2,1,0:T(8,128)(2,1)S(1)}, u32[]{:S(2)}, u32[]{:S(2)}) %all-to-all-start) | async-done | bytes 262176 | tf_op jit(solution)/shard_map/all_to_all | solution.py:182
  32.6 1.0 broadcast_in_dim.6
  33.7 4.8 %all-to-all-start.1 = ((bf16[4,512,256]{2,1,0:T(8,128)(2,1)}), bf16[4,512,256]{2,1,0:T(8,128)(2,1)S(1)}, u32[]{:S(2)}, u32[]{:S(2)}) async-start(bf16[4,512,256]{2,1,0:T(8,128)(2,1)} %broadcast_in_dim.6), calls=%async_computation.1 | async-start | bytes 2097152 | tf_op jit(solution)/shard_map/all_to_all | solution.py:64
  38.5 1.9 %collective-permute-start.1 = (bf16[128,32,256]{2,1,0:T(8,128)(2,1)}, bf16[128,32,256]{2,1,0:T(8,128)(2,1)S(1)}, u32[]{:S(2)}, u32[]{:S(2)}) collective-permute-start(bf16[128,32,256]{2,1,0:T(8,128)(2,1)} %constant_dynamic-slice_fusion.1), channel_id=1, source_target_pairs={{0,1},{1,0},{2,3},{3,2},{4,5},{5,4},{6,7},{7,6},{8,9},{9,8},{10,11... | collective-permute-start | bytes 6291464 | tf_op jit(solution)/shard_map/ppermute | solution.py:32
  40.5 2.0 %fusion.2 = bf16[6,32,512]{2,0,1:T(8,128)(2,1)} fusion(bf16[6,32,512]{2,0,1:T(8,128)(2,1)} %collective-permute-done.4, bf16[6,32,512]{2,0,1:T(8,128)(2,1)} %collective-permute-done.3, bf16[6,32,512]{2,0,1:T(8,128)(2,1)} %collective-permute-done.2, bf16[6,128,512]{2,0,1:T(8,128)(2,1)} %copy-done.2, pred[]{:T(512)S(6)} %and.65), kind=kLoop, calls=%fused_computation.4 | loop fusion | flops 393216 | bytes 983041 | tf_op jit(solution)/shard_map/add | solution.py:43
  42.5 2.4 %collective-permute-start = (bf16[6,16]{1,0:T(8,128)(2,1)S(1)}, bf16[6,16]{1,0:T(8,128)(2,1)S(1)}, u32[]{:S(2)}, u32[]{:S(2)}) collective-permute-start(bf16[6,16]{1,0:T(8,128)(2,1)S(1)} %constant_dynamic-slice_fusion), channel_id=1, source_target_pairs={{0,1},{1,0},{2,3},{3,2},{4,5},{5,4},{6,7},{7,6},{8,9},{9,8},{10,11... | collective-permute-start | bytes 584 | tf_op jit(solution)/shard_map/ppermute | solution.py:32
  44.9 2.8 %collective-permute-start.7 = (bf16[6,32,512]{2,0,1:T(8,128)(2,1)}, bf16[6,32,512]{2,0,1:T(8,128)(2,1)S(1)}, u32[]{:S(2)}, u32[]{:S(2)}) collective-permute-start(bf16[6,32,512]{2,0,1:T(8,128)(2,1)} %fusion.2), channel_id=1, source_target_pairs={{0,96},{128,224},{256,352},{384,480},{1,97},{129,225},{257,353},{3... | collective-permute-start | bytes 589832 | tf_op jit(solution)/shard_map/ppermute | solution.py:50
  47.8 3.9 %collective-permute-start.6 = (bf16[6,32,512]{2,0,1:T(8,128)(2,1)}, bf16[6,32,512]{2,0,1:T(8,128)(2,1)}, u32[]{:S(2)}, u32[]{:S(2)}) collective-permute-start(bf16[6,32,512]{2,0,1:T(8,128)(2,1)} %fusion.2), channel_id=1, source_target_pairs={{0,64},{128,192},{256,320},{384,448},{1,65},{129,193},{257,321},{3... | collective-permute-start | bytes 589832 | tf_op jit(solution)/shard_map/ppermute | solution.py:50
  51.7 2.0 %collective-permute-start.5 = (bf16[6,32,512]{2,0,1:T(8,128)(2,1)}, bf16[6,32,512]{2,0,1:T(8,128)(2,1)}, u32[]{:S(2)}, u32[]{:S(2)}) collective-permute-start(bf16[6,32,512]{2,0,1:T(8,128)(2,1)} %fusion.2), channel_id=1, source_target_pairs={{0,32},{128,160},{256,288},{384,416},{1,33},{129,161},{257,289},{3... | collective-permute-start | bytes 589832 | tf_op jit(solution)/shard_map/ppermute | solution.py:50
  53.7 2.3 %collective-permute-start.9 = (bf16[4,512,256]{2,1,0:T(8,128)(2,1)S(1)}, bf16[4,512,256]{2,1,0:T(8,128)(2,1)S(1)}, u32[]{:S(2)}, u32[]{:S(2)}) collective-permute-start(bf16[4,512,256]{2,1,0:T(8,128)(2,1)S(1)} %all-to-all-done.1.refs_0_), channel_id=1, source_target_pairs={{0,32},{32,64},{64,96},{96,16},{16,48},{48,80},{80,112},{112,0},{1... | collective-permute-start | bytes 3145736 | tf_op jit(solution)/shard_map/ppermute | solution.py:28
  56.0 5.1 %collective-permute-start.11 = (bf16[4,512,256]{2,1,0:T(8,128)(2,1)S(1)}, bf16[4,512,256]{2,1,0:T(8,128)(2,1)S(1)}, u32[]{:S(2)}, u32[]{:S(2)}) collective-permute-start(bf16[4,512,256]{2,1,0:T(8,128)(2,1)S(1)} %all-to-all-done.1.refs_0_), channel_id=1, source_target_pairs={{0,112},{32,0},{64,32},{96,64},{16,96},{48,16},{80,48},{112,80},{1... | collective-permute-start | bytes 3145736 | tf_op jit(solution)/shard_map/ppermute | solution.py:28
  61.1 4.9 %collective-permute-done.5 = bf16[6,32,512]{2,0,1:T(8,128)(2,1)} collective-permute-done((bf16[6,32,512]{2,0,1:T(8,128)(2,1)}, bf16[6,32,512]{2,0,1:T(8,128)(2,1)}, u32[]{:S(2)}, u32[]{:S(2)}) %collective-permute-start.5) | collective-permute-done | bytes 196640 | tf_op jit(solution)/shard_map/ppermute | solution.py:50
  66.0 1.2 add_add_fusion
  67.4 13.2 %all_to_all.20.w_own.refs_3_ = bf16[4,6,32,512]{3,2,1,0:T(8,128)(2,1)S(1)} all-to-all(bf16[4,6,32,512]{3,2,1,0:T(8,128)(2,1)S(1)} %broadcast_in_dim.7), channel_id=1, replica_groups=mesh['x'=4,'ylo'=4,'yhi'=2,'z'=8,'core'=2] {'x'}, dimensions={0} | all-to-all | bytes 1572864 | tf_op jit(solution)/shard_map/all_to_all | solution.py:64
  80.6 1.9 %collective-permute-start.8 = (bf16[4,6,32,512]{3,2,1,0:T(8,128)(2,1)S(1)}, bf16[4,6,32,512]{3,2,1,0:T(8,128)(2,1)S(1)}, u32[]{:S(2)}, u32[]{:S(2)}) collective-permute-start(bf16[4,6,32,512]{3,2,1,0:T(8,128)(2,1)S(1)} %all_to_all.20.w_own.refs_3_), channel_id=1, source_target_pairs={{0,1},{1,0},{2,3},{3,2},{4,5},{5,4},{6,7},{7,6},{8,9},{9,8},{10,11... | collective-permute-start | bytes 2359304 | tf_op jit(solution)/shard_map/ppermute | solution.py:32
  82.5 4.9 %collective-permute-done.9.refs_1_ = bf16[4,512,256]{2,1,0:T(8,128)(2,1)S(1)} collective-permute-done((bf16[4,512,256]{2,1,0:T(8,128)(2,1)S(1)}, bf16[4,512,256]{2,1,0:T(8,128)(2,1)S(1)}, u32[]{:S(2)}, u32[]{:S(2)}) %collective-permute-start.9) | collective-permute-done | bytes 1048608 | tf_op jit(solution)/shard_map/ppermute | solution.py:28
  87.5 4.4 %collective-permute-start.10 = (bf16[2,512,256]{2,1,0:T(8,128)(2,1)S(1)}, bf16[2,512,256]{2,1,0:T(8,128)(2,1)S(1)}, u32[]{:S(2)}, u32[]{:S(2)}) collective-permute-start(bf16[2,512,256]{2,1,0:T(8,128)(2,1)S(1)} %slice.55), channel_id=1, source_target_pairs={{0,32},{32,64},{64,96},{96,16},{16,48},{48,80},{80,112},{112,0},{1... | collective-permute-start | bytes 1572872 | tf_op jit(solution)/shard_map/ppermute | solution.py:28
  91.9 3.1 %collective-permute-start.12 = (bf16[2,512,256]{2,1,0:T(8,128)(2,1)S(1)}, bf16[2,512,256]{2,1,0:T(8,128)(2,1)S(1)}, u32[]{:S(2)}, u32[]{:S(2)}) collective-permute-start(bf16[2,512,256]{2,1,0:T(8,128)(2,1)S(1)} %slice.56), channel_id=1, source_target_pairs={{0,112},{32,0},{64,32},{96,64},{16,96},{48,16},{80,48},{112,80},{1... | collective-permute-start | bytes 1572872 | tf_op jit(solution)/shard_map/ppermute | solution.py:28
  95.1 11.9 %shard_map.77 = (f32[72,256]{1,0:T(8,128)S(1)}, f32[12,8,256]{2,1,0:T(8,128)S(1)}) custom-call(s32[19]{0:T(128)S(1)} %concatenate.3.scalars.refs_0_, bf16[128,32,512]{2,1,0:T(8,128)(2,1)} %refs_1_.1, bf16[128,32,256]{2,1,0:T(8,128)(2,1)S(1)} %collective-permute-done.1.f_other.refs_2_, bf16[4,6,32,512]{3,2,1,0:T(8,128)(2,1)S(1)} %all_to_all.20.w_own.refs_3_, ...), custom_call_target="tpu_custom_call" | custom-call | flops 12000000 | bytes 100000 | tf_op jit(solution)/shard_map/pallas_call | solution.py:228
  107.0 5.1 %shard_map.78 = f32[32,1,128]{2,1,0:T(1,128)S(1)} custom-call(s32[19]{0:T(128)S(1)} %concatenate.3.scalars.refs_0_, bf16[128,32,512]{2,1,0:T(8,128)(2,1)S(1)} %copy-done, bf16[128,32,256]{2,1,0:T(8,128)(2,1)S(1)} %collective-permute-done.1.f_other.refs_2_, bf16[4,6,32,512]{3,2,1,0:T(8,128)(2,1)S(1)} %all_to_all.20.w_own.refs_3_, ...), custom_call_target="tpu_custom_call" | custom-call | flops 4000000 | bytes 100000 | tf_op jit(solution)/shard_map/pallas_call | solution.py:248
  112.2 22.5 %all_to_all.21 = f32[32,1,128]{2,1,0:T(1,128)S(1)} all-to-all(f32[32,1,128]{2,1,0:T(1,128)S(1)} %shard_map.78), channel_id=1, replica_groups=mesh['x'=4,'ylo'=4,'yhi'=2,'z'=8,'core'=2] {'yhi','z','core'}, dimensions={0} | all-to-all | bytes 32768 | tf_op jit(solution)/shard_map/all_to_all | solution.py:266
  134.7 2.2 %collective-permute-start.13 = (f32[1,128]{1,0:T(1,128)S(1)}, f32[1,128]{1,0:T(1,128)S(1)}, u32[]{:S(2)}, u32[]{:S(2)}) collective-permute-start(f32[1,128]{1,0:T(1,128)S(1)} %bitcast.36), channel_id=1, source_target_pairs={{0,0},{1,1},{2,32},{3,33},{4,64},{5,65},{6,96},{7,97},{8,128},{9,1... | collective-permute-start | bytes 1544 | tf_op jit(solution)/shard_map/ppermute | solution.py:273
  137.6 13.3 %collective-permute-done.13 = f32[1,128]{1,0:T(1,128)S(1)} collective-permute-done((f32[1,128]{1,0:T(1,128)S(1)}, f32[1,128]{1,0:T(1,128)S(1)}, u32[]{:S(2)}, u32[]{:S(2)}) %collective-permute-start.13) | collective-permute-done | bytes 544 | tf_op jit(solution)/shard_map/ppermute | solution.py:273
  (40 shorter events, 2.0 us)
Async XLA Ops:
  2.1 30.6 %all-to-all-start = ((bf16[32,16,256]{2,1,0:T(8,128)(2,1)}), bf16[32,16,256]{2,1,0:T(8,128)(2,1)S(1)}, u32[]{:S(2)}, u32[]{:S(2)}) async-start(bf16[32,16,256]{2,1,0:T(8,128)(2,1)} %bitcast.3), calls=%async_computation | async-start | bytes 524288 | tf_op jit(solution)/shard_map/all_to_all | solution.py:182
  19.3 14.3 %copy-start.2 = (bf16[6,128,512]{2,0,1:T(8,128)(2,1)}, bf16[6,128,512]{2,0,1:T(8,128)(2,1)S(1)}, u32[]{:S(2)}) copy-start(bf16[6,128,512]{2,0,1:T(8,128)(2,1)S(1)} %slice_bitcast_fusion) | copy-start | bytes 2359300
  20.3 20.1 %collective-permute-start.4 = (bf16[6,32,512]{2,0,1:T(8,128)(2,1)}, bf16[6,32,512]{2,0,1:T(8,128)(2,1)}, u32[]{:S(2)}, u32[]{:S(2)}) collective-permute-start(bf16[6,32,512]{2,0,1:T(8,128)(2,1)} %get-tuple-element.23), channel_id=1, source_target_pairs={{0,384},{1,385},{2,386},{3,387},{4,388},{5,389},{6,390},{7,391},{8... | collective-permute-start | bytes 589832 | tf_op jit(solution)/shard_map/ppermute | solution.py:43
  21.6 18.9 %collective-permute-start.3 = (bf16[6,32,512]{2,0,1:T(8,128)(2,1)}, bf16[6,32,512]{2,0,1:T(8,128)(2,1)}, u32[]{:S(2)}, u32[]{:S(2)}) collective-permute-start(bf16[6,32,512]{2,0,1:T(8,128)(2,1)} %get-tuple-element.24), channel_id=1, source_target_pairs={{0,256},{1,257},{2,258},{3,259},{4,260},{5,261},{6,262},{7,263},{8... | collective-permute-start | bytes 589832 | tf_op jit(solution)/shard_map/ppermute | solution.py:43
  23.0 17.5 %collective-permute-start.2 = (bf16[6,32,512]{2,0,1:T(8,128)(2,1)}, bf16[6,32,512]{2,0,1:T(8,128)(2,1)}, u32[]{:S(2)}, u32[]{:S(2)}) collective-permute-start(bf16[6,32,512]{2,0,1:T(8,128)(2,1)} %get-tuple-element.22), channel_id=1, source_target_pairs={{0,128},{1,129},{2,130},{3,131},{4,132},{5,133},{6,134},{7,135},{8... | collective-permute-start | bytes 589832 | tf_op jit(solution)/shard_map/ppermute | solution.py:43
  33.7 20.1 %all-to-all-start.1 = ((bf16[4,512,256]{2,1,0:T(8,128)(2,1)}), bf16[4,512,256]{2,1,0:T(8,128)(2,1)S(1)}, u32[]{:S(2)}, u32[]{:S(2)}) async-start(bf16[4,512,256]{2,1,0:T(8,128)(2,1)} %broadcast_in_dim.6), calls=%async_computation.1 | async-start | bytes 2097152 | tf_op jit(solution)/shard_map/all_to_all | solution.py:64
  38.5 56.5 %collective-permute-start.1 = (bf16[128,32,256]{2,1,0:T(8,128)(2,1)}, bf16[128,32,256]{2,1,0:T(8,128)(2,1)S(1)}, u32[]{:S(2)}, u32[]{:S(2)}) collective-permute-start(bf16[128,32,256]{2,1,0:T(8,128)(2,1)} %constant_dynamic-slice_fusion.1), channel_id=1, source_target_pairs={{0,1},{1,0},{2,3},{3,2},{4,5},{5,4},{6,7},{7,6},{8,9},{9,8},{10,11... | collective-permute-start | bytes 6291464 | tf_op jit(solution)/shard_map/ppermute | solution.py:32
  42.5 11.1 %collective-permute-start = (bf16[6,16]{1,0:T(8,128)(2,1)S(1)}, bf16[6,16]{1,0:T(8,128)(2,1)S(1)}, u32[]{:S(2)}, u32[]{:S(2)}) collective-permute-start(bf16[6,16]{1,0:T(8,128)(2,1)S(1)} %constant_dynamic-slice_fusion), channel_id=1, source_target_pairs={{0,1},{1,0},{2,3},{3,2},{4,5},{5,4},{6,7},{7,6},{8,9},{9,8},{10,11... | collective-permute-start | bytes 584 | tf_op jit(solution)/shard_map/ppermute | solution.py:32
  44.9 11.1 %collective-permute-start.7 = (bf16[6,32,512]{2,0,1:T(8,128)(2,1)}, bf16[6,32,512]{2,0,1:T(8,128)(2,1)S(1)}, u32[]{:S(2)}, u32[]{:S(2)}) collective-permute-start(bf16[6,32,512]{2,0,1:T(8,128)(2,1)} %fusion.2), channel_id=1, source_target_pairs={{0,96},{128,224},{256,352},{384,480},{1,97},{129,225},{257,353},{3... | collective-permute-start | bytes 589832 | tf_op jit(solution)/shard_map/ppermute | solution.py:50
  47.8 13.4 %collective-permute-start.6 = (bf16[6,32,512]{2,0,1:T(8,128)(2,1)}, bf16[6,32,512]{2,0,1:T(8,128)(2,1)}, u32[]{:S(2)}, u32[]{:S(2)}) collective-permute-start(bf16[6,32,512]{2,0,1:T(8,128)(2,1)} %fusion.2), channel_id=1, source_target_pairs={{0,64},{128,192},{256,320},{384,448},{1,65},{129,193},{257,321},{3... | collective-permute-start | bytes 589832 | tf_op jit(solution)/shard_map/ppermute | solution.py:50
  51.7 14.4 %collective-permute-start.5 = (bf16[6,32,512]{2,0,1:T(8,128)(2,1)}, bf16[6,32,512]{2,0,1:T(8,128)(2,1)}, u32[]{:S(2)}, u32[]{:S(2)}) collective-permute-start(bf16[6,32,512]{2,0,1:T(8,128)(2,1)} %fusion.2), channel_id=1, source_target_pairs={{0,32},{128,160},{256,288},{384,416},{1,33},{129,161},{257,289},{3... | collective-permute-start | bytes 589832 | tf_op jit(solution)/shard_map/ppermute | solution.py:50
  53.7 33.7 %collective-permute-start.9 = (bf16[4,512,256]{2,1,0:T(8,128)(2,1)S(1)}, bf16[4,512,256]{2,1,0:T(8,128)(2,1)S(1)}, u32[]{:S(2)}, u32[]{:S(2)}) collective-permute-start(bf16[4,512,256]{2,1,0:T(8,128)(2,1)S(1)} %all-to-all-done.1.refs_0_), channel_id=1, source_target_pairs={{0,32},{32,64},{64,96},{96,16},{16,48},{48,80},{80,112},{112,0},{1... | collective-permute-start | bytes 3145736 | tf_op jit(solution)/shard_map/ppermute | solution.py:28
  56.0 35.8 %collective-permute-start.11 = (bf16[4,512,256]{2,1,0:T(8,128)(2,1)S(1)}, bf16[4,512,256]{2,1,0:T(8,128)(2,1)S(1)}, u32[]{:S(2)}, u32[]{:S(2)}) collective-permute-start(bf16[4,512,256]{2,1,0:T(8,128)(2,1)S(1)} %all-to-all-done.1.refs_0_), channel_id=1, source_target_pairs={{0,112},{32,0},{64,32},{96,64},{16,96},{48,16},{80,48},{112,80},{1... | collective-permute-start | bytes 3145736 | tf_op jit(solution)/shard_map/ppermute | solution.py:28
  80.6 14.5 %collective-permute-start.8 = (bf16[4,6,32,512]{3,2,1,0:T(8,128)(2,1)S(1)}, bf16[4,6,32,512]{3,2,1,0:T(8,128)(2,1)S(1)}, u32[]{:S(2)}, u32[]{:S(2)}) collective-permute-start(bf16[4,6,32,512]{3,2,1,0:T(8,128)(2,1)S(1)} %all_to_all.20.w_own.refs_3_), channel_id=1, source_target_pairs={{0,1},{1,0},{2,3},{3,2},{4,5},{5,4},{6,7},{7,6},{8,9},{9,8},{10,11... | collective-permute-start | bytes 2359304 | tf_op jit(solution)/shard_map/ppermute | solution.py:32
  87.5 19.5 %collective-permute-start.10 = (bf16[2,512,256]{2,1,0:T(8,128)(2,1)S(1)}, bf16[2,512,256]{2,1,0:T(8,128)(2,1)S(1)}, u32[]{:S(2)}, u32[]{:S(2)}) collective-permute-start(bf16[2,512,256]{2,1,0:T(8,128)(2,1)S(1)} %slice.55), channel_id=1, source_target_pairs={{0,32},{32,64},{64,96},{96,16},{16,48},{48,80},{80,112},{112,0},{1... | collective-permute-start | bytes 1572872 | tf_op jit(solution)/shard_map/ppermute | solution.py:28
  91.9 15.1 %copy-start = (bf16[128,32,512]{2,1,0:T(8,128)(2,1)S(1)}, bf16[128,32,512]{2,1,0:T(8,128)(2,1)}, u32[]{:S(2)}) copy-start(bf16[128,32,512]{2,1,0:T(8,128)(2,1)} %refs_1_.1) | copy-start | bytes 12582916
  91.9 15.1 %copy-start.1 = (f32[16,16]{1,0:T(8,128)S(1)}, f32[16,16]{1,0:T(8,128)}, u32[]{:S(2)}) copy-start(f32[16,16]{1,0:T(8,128)} %refs_5_.1) | copy-start | bytes 3076
  91.9 15.0 %collective-permute-start.12 = (bf16[2,512,256]{2,1,0:T(8,128)(2,1)S(1)}, bf16[2,512,256]{2,1,0:T(8,128)(2,1)S(1)}, u32[]{:S(2)}, u32[]{:S(2)}) collective-permute-start(bf16[2,512,256]{2,1,0:T(8,128)(2,1)S(1)} %slice.56), channel_id=1, source_target_pairs={{0,112},{32,0},{64,32},{96,64},{16,96},{48,16},{80,48},{112,80},{1... | collective-permute-start | bytes 1572872 | tf_op jit(solution)/shard_map/ppermute | solution.py:28
  107.0 30.5 %copy-start.4 = (f32[512]{0:T(512)S(1)}, f32[512]{0:T(512)}, u32[]{:S(2)}) copy-start(f32[512]{0:T(512)} %param.10) | copy-start | bytes 6148
  107.0 44.0 %copy-start.3 = (f32[1,6,16]{2,0,1:T(1,128)S(1)}, f32[1,6,16]{2,0,1:T(1,128)}, u32[]{:S(2)}) copy-start(f32[1,6,16]{2,0,1:T(1,128)} %param.9) | copy-start | bytes 1156
  107.0 44.0 %slice-start = ((f32[512]{0:T(512)}), f32[6]{0:T(128)S(1)}, s32[]{:S(2)}) async-start(f32[512]{0:T(512)} %param.10), calls=%async_computation.4 | async-start | bytes 1024 | tf_op jit(solution)/shard_map/slice | solution.py:279
  134.7 16.2 %collective-permute-start.13 = (f32[1,128]{1,0:T(1,128)S(1)}, f32[1,128]{1,0:T(1,128)S(1)}, u32[]{:S(2)}, u32[]{:S(2)}) collective-permute-start(f32[1,128]{1,0:T(1,128)S(1)} %bitcast.36), channel_id=1, source_target_pairs={{0,0},{1,1},{2,32},{3,33},{4,64},{5,65},{6,96},{7,97},{8,128},{9,1... | collective-permute-start | bytes 1544 | tf_op jit(solution)/shard_map/ppermute | solution.py:273

commit v8 on v7

--- a/solution.py
+++ b/solution.py
@@ -46,16 +46,16 @@
 
 def window_spread(mine):
     parts, lows = lax.axis_size("x"), lax.axis_size("ylo")
-    return [
-        lax.ppermute(mine, PAIR, [(i * lows, i * lows + k) for i in range(parts)])
-        for k in range(1, lows)
-    ]
-
-
-def window_quarter(mine, spread):
     quarter = jnp.where(lax.axis_index("ylo") == 0, mine, jnp.zeros_like(mine))
-    for piece in spread:
-        quarter = quarter + piece
+    stride = lows // 2
+    while stride:
+        moves = [
+            (i * lows + k, i * lows + k + stride)
+            for i in range(parts)
+            for k in range(0, lows, 2 * stride)
+        ]
+        quarter = quarter + lax.ppermute(quarter, PAIR, moves)
+        stride //= 2
     return quarter
 
 
@@ -205,7 +205,7 @@
     chunk = collected(amp)
     chunk, amp_cols, scalars = lax.optimization_barrier((chunk, amp_cols, scalars))
     behind, ahead = shifted(chunk, "y", 1), shifted(chunk, "y", -1)
-    window = collected(window_quarter(scattered, spread))
+    window = collected(spread)
     window_other = swapped(window)
 
     head_rows = 8

time: 153 us -> 149 us (0.974)
  waiting for transfers between devices: 28.4 us -> 25.9 us
    all_to_all x1, blocking collectives: 22.5 us -> 20.2 us  [per_device(): summed = jnp.sum(lax.all_to_all(tiles, AUX, 0, 0, tiled=True), axis=0)]
    select_n x0 -> x1, other arithmetic: none -> 1.95 us  [window_spread(): quarter = jnp.where(lax.axis_index('ylo') == 0, mine, jnp.zeros_like(mine))]
    ppermute x3 -> x2, waiting for transfers between devices: 4.88 us -> 3.51 us  [window_spread(): quarter = quarter + lax.ppermute(quarter, PAIR, moves)]
    ppermute x3 -> x2, starting transfers between devices: 8.73 us -> 8.01 us  [window_spread(): quarter = quarter + lax.ppermute(quarter, PAIR, moves)]
  transfers between devices with their start and end apart: 16 -> 15, of which waited for: 4 -> 4; matrix products, arithmetic and copies ran while one was open for 7% -> 7% of each run, Pallas kernels for 8% -> 8%
where the time goes in v8:
time: 149 us; the launch traced here: 148 us
  starting transfers between devices  55.2 us (37%)
  blocking collectives  34.3 us (23%)
  waiting for transfers between devices  25.9 us (17%)
  Pallas kernels  17 us (11%)
  local copies, waits for them, and re-layouts  9.65 us (6%)
  other arithmetic  4.27 us (3%)
  between operations  1.57 us (1%)
    all_to_all x1, blocking collectives, per_device(): summed = jnp.sum(lax.all_to_all(tiles, AUX, 0, 0, tiled=True), axis=0)  20.2 us
    all_to_all x1, starting transfers between devices, per_device(): lax.all_to_all(sent.reshape(-1, *split.shape[1:]), AUX, 0, 0, tiled=True)  16 us
    ppermute x4, starting transfers between devices, shifted(): lax.ppermute(array, Y, [(index(y), index((y + by) % full)) for y in range...  14.5 us
    all_to_all x1, blocking collectives, collected(): lax.all_to_all(jnp.broadcast_to(array[None], (parts, *array.shape)), 'x',...  14.1 us
    ppermute x1, waiting for transfers between devices, per_device(): summed = lax.ppermute(summed, AXES, moves)  13.6 us
    pallas_call x1, Pallas kernels, early(): pl.pallas_call(early_kernel, grid_spec=pltpu.PrefetchScalarGridSpec(num_s...  11.9 us
    ppermute x2, starting transfers between devices, window_spread(): quarter = quarter + lax.ppermute(quarter, PAIR, moves)  8.01 us
    ppermute x3, starting transfers between devices, swapped(): return lax.ppermute(array, 'core', [(0, 1), (1, 0)])  5.93 us
  transfers between devices with their start and end apart: 15, of which 4 were waited for; matrix products, arithmetic and copies ran while one was open for 7% of the time, Pallas kernels for 8%

profile of v8, /device:TPU:6, one launch (start us, length us, event | category | flops | bytes accessed | tf_op | source)
XLA Modules:
  0.0 147.8 jit_solution(16958067848378369252)
XLA Ops:
  0.6 0.7 slice_bitcast_fusion.2
  1.4 0.7 tile.7
  2.1 16.0 %all-to-all-start = ((bf16[32,16,256]{2,1,0:T(8,128)(2,1)}), bf16[32,16,256]{2,1,0:T(8,128)(2,1)S(1)}, u32[]{:S(2)}, u32[]{:S(2)}) async-start(bf16[32,16,256]{2,1,0:T(8,128)(2,1)} %bitcast.3), calls=%async_computation | async-start | bytes 524288 | tf_op jit(solution)/shard_map/all_to_all | solution.py:182
  18.1 1.3 slice_bitcast_fusion
  19.4 1.0 fusion.4
  20.4 1.3 collective-permute-start.4
  21.7 1.4 collective-permute-start.3
  23.0 1.4 collective-permute-start.2
  24.4 3.1 %constant_dynamic-slice_fusion.1 = bf16[128,32,256]{2,1,0:T(8,128)(2,1)} fusion(bf16[128,32,512]{2,1,0:T(8,128)(2,1)} %refs_1_.1, s32[]{:T(128)S(6)} %select_n.89), kind=kLoop, calls=%fused_computation.13 | loop fusion | bytes 4194308 | tf_op jit(solution)/shard_map/dynamic_slice | solution.py:186
  27.5 5.1 %all-to-all-done = bf16[32,16,256]{2,1,0:T(8,128)(2,1)S(1)} async-done(((bf16[32,16,256]{2,1,0:T(8,128)(2,1)}), bf16[32,16,256]{2,1,0:T(8,128)(2,1)S(1)}, u32[]{:S(2)}, u32[]{:S(2)}) %all-to-all-start) | async-done | bytes 262176 | tf_op jit(solution)/shard_map/all_to_all | solution.py:182
  32.6 1.1 broadcast_in_dim.6
  33.7 4.8 %all-to-all-start.1 = ((bf16[4,512,256]{2,1,0:T(8,128)(2,1)}), bf16[4,512,256]{2,1,0:T(8,128)(2,1)S(1)}, u32[]{:S(2)}, u32[]{:S(2)}) async-start(bf16[4,512,256]{2,1,0:T(8,128)(2,1)} %broadcast_in_dim.6), calls=%async_computation.1 | async-start | bytes 2097152 | tf_op jit(solution)/shard_map/all_to_all | solution.py:64
  38.5 1.9 %collective-permute-start.1 = (bf16[128,32,256]{2,1,0:T(8,128)(2,1)}, bf16[128,32,256]{2,1,0:T(8,128)(2,1)S(1)}, u32[]{:S(2)}, u32[]{:S(2)}) collective-permute-start(bf16[128,32,256]{2,1,0:T(8,128)(2,1)} %constant_dynamic-slice_fusion.1), channel_id=1, source_target_pairs={{0,1},{1,0},{2,3},{3,2},{4,5},{5,4},{6,7},{7,6},{8,9},{9,8},{10,11... | collective-permute-start | bytes 6291464 | tf_op jit(solution)/shard_map/ppermute | solution.py:32
  40.4 2.0 %fusion.3 = bf16[6,32,512]{2,0,1:T(8,128)(2,1)} fusion(bf16[6,32,512]{2,0,1:T(8,128)(2,1)} %collective-permute-done.4, bf16[6,32,512]{2,0,1:T(8,128)(2,1)} %collective-permute-done.3, bf16[6,32,512]{2,0,1:T(8,128)(2,1)} %collective-permute-done.2, bf16[6,128,512]{2,0,1:T(8,128)(2,1)} %copy-done.2, pred[]{:T(512)S(6)} %and.65, pred[]{:T(512)S(6)} %eq.42), kind=kLoop, calls=%fused_computation.5 | loop fusion | flops 491520 | bytes 983042 | tf_op jit(solution)/shard_map/jit(_where)/select_n | solution.py:49
  42.4 6.0 %collective-permute-start.5 = (bf16[6,32,512]{2,0,1:T(8,128)(2,1)}, bf16[6,32,512]{2,0,1:T(8,128)(2,1)}, u32[]{:S(2)}, u32[]{:S(2)}) collective-permute-start(bf16[6,32,512]{2,0,1:T(8,128)(2,1)} %fusion.3), channel_id=1, source_target_pairs={{0,64},{128,192},{256,320},{384,448},{1,65},{129,193},{257,321},{3... | collective-permute-start | bytes 589832 | tf_op jit(solution)/shard_map/ppermute | solution.py:57
  48.6 2.1 %collective-permute-start = (bf16[6,16]{1,0:T(8,128)(2,1)S(1)}, bf16[6,16]{1,0:T(8,128)(2,1)S(1)}, u32[]{:S(2)}, u32[]{:S(2)}) collective-permute-start(bf16[6,16]{1,0:T(8,128)(2,1)S(1)} %constant_dynamic-slice_fusion), channel_id=1, source_target_pairs={{0,1},{1,0},{2,3},{3,2},{4,5},{5,4},{6,7},{7,6},{8,9},{9,8},{10,11... | collective-permute-start | bytes 584 | tf_op jit(solution)/shard_map/ppermute | solution.py:32
  50.7 3.5 %collective-permute-done.5 = bf16[6,32,512]{2,0,1:T(8,128)(2,1)} collective-permute-done((bf16[6,32,512]{2,0,1:T(8,128)(2,1)}, bf16[6,32,512]{2,0,1:T(8,128)(2,1)}, u32[]{:S(2)}, u32[]{:S(2)}) %collective-permute-start.5) | collective-permute-done | bytes 196640 | tf_op jit(solution)/shard_map/ppermute | solution.py:57
  54.2 1.1 add.162
  55.3 2.0 %collective-permute-start.6 = (bf16[6,32,512]{2,0,1:T(8,128)(2,1)S(1)}, bf16[6,32,512]{2,0,1:T(8,128)(2,1)}, u32[]{:S(2)}, u32[]{:S(2)}) collective-permute-start(bf16[6,32,512]{2,0,1:T(8,128)(2,1)S(1)} %add.162), channel_id=1, source_target_pairs={{0,32},{64,96},{128,160},{192,224},{256,288},{320,352},{384,416},{... | collective-permute-start | bytes 589832 | tf_op jit(solution)/shard_map/ppermute | solution.py:57
  57.4 1.9 %collective-permute-start.8 = (bf16[4,512,256]{2,1,0:T(8,128)(2,1)S(1)}, bf16[4,512,256]{2,1,0:T(8,128)(2,1)S(1)}, u32[]{:S(2)}, u32[]{:S(2)}) collective-permute-start(bf16[4,512,256]{2,1,0:T(8,128)(2,1)S(1)} %all-to-all-done.1.refs_0_), channel_id=1, source_target_pairs={{0,32},{32,64},{64,96},{96,16},{16,48},{48,80},{80,112},{112,0},{1... | collective-permute-start | bytes 3145736 | tf_op jit(solution)/shard_map/ppermute | solution.py:28
  59.3 5.1 %collective-permute-start.10 = (bf16[4,512,256]{2,1,0:T(8,128)(2,1)S(1)}, bf16[4,512,256]{2,1,0:T(8,128)(2,1)S(1)}, u32[]{:S(2)}, u32[]{:S(2)}) collective-permute-start(bf16[4,512,256]{2,1,0:T(8,128)(2,1)S(1)} %all-to-all-done.1.refs_0_), channel_id=1, source_target_pairs={{0,112},{32,0},{64,32},{96,64},{16,96},{48,16},{80,48},{112,80},{1... | collective-permute-start | bytes 3145736 | tf_op jit(solution)/shard_map/ppermute | solution.py:28
  64.5 1.0 add.163
  65.6 14.1 %all_to_all.20.w_own.refs_3_ = bf16[4,6,32,512]{3,2,1,0:T(8,128)(2,1)S(1)} all-to-all(bf16[4,6,32,512]{3,2,1,0:T(8,128)(2,1)S(1)} %broadcast_in_dim.7), channel_id=1, replica_groups=mesh['x'=4,'ylo'=4,'yhi'=2,'z'=8,'core'=2] {'x'}, dimensions={0} | all-to-all | bytes 1572864 | tf_op jit(solution)/shard_map/all_to_all | solution.py:64
  79.8 1.9 %collective-permute-start.7 = (bf16[4,6,32,512]{3,2,1,0:T(8,128)(2,1)S(1)}, bf16[4,6,32,512]{3,2,1,0:T(8,128)(2,1)S(1)}, u32[]{:S(2)}, u32[]{:S(2)}) collective-permute-start(bf16[4,6,32,512]{3,2,1,0:T(8,128)(2,1)S(1)} %all_to_all.20.w_own.refs_3_), channel_id=1, source_target_pairs={{0,1},{1,0},{2,3},{3,2},{4,5},{5,4},{6,7},{7,6},{8,9},{9,8},{10,11... | collective-permute-start | bytes 2359304 | tf_op jit(solution)/shard_map/ppermute | solution.py:32
  81.7 3.6 %collective-permute-done.8.refs_1_ = bf16[4,512,256]{2,1,0:T(8,128)(2,1)S(1)} collective-permute-done((bf16[4,512,256]{2,1,0:T(8,128)(2,1)S(1)}, bf16[4,512,256]{2,1,0:T(8,128)(2,1)S(1)}, u32[]{:S(2)}, u32[]{:S(2)}) %collective-permute-start.8) | collective-permute-done | bytes 1048608 | tf_op jit(solution)/shard_map/ppermute | solution.py:28
  85.3 3.9 %collective-permute-start.9 = (bf16[2,512,256]{2,1,0:T(8,128)(2,1)S(1)}, bf16[2,512,256]{2,1,0:T(8,128)(2,1)S(1)}, u32[]{:S(2)}, u32[]{:S(2)}) collective-permute-start(bf16[2,512,256]{2,1,0:T(8,128)(2,1)S(1)} %slice.55), channel_id=1, source_target_pairs={{0,32},{32,64},{64,96},{96,16},{16,48},{48,80},{80,112},{112,0},{1... | collective-permute-start | bytes 1572872 | tf_op jit(solution)/shard_map/ppermute | solution.py:28
  89.3 3.6 %collective-permute-start.11 = (bf16[2,512,256]{2,1,0:T(8,128)(2,1)S(1)}, bf16[2,512,256]{2,1,0:T(8,128)(2,1)S(1)}, u32[]{:S(2)}, u32[]{:S(2)}) collective-permute-start(bf16[2,512,256]{2,1,0:T(8,128)(2,1)S(1)} %slice.56), channel_id=1, source_target_pairs={{0,112},{32,0},{64,32},{96,64},{16,96},{48,16},{80,48},{112,80},{1... | collective-permute-start | bytes 1572872 | tf_op jit(solution)/shard_map/ppermute | solution.py:28
  92.9 11.9 %shard_map.77 = (f32[72,256]{1,0:T(8,128)S(1)}, f32[12,8,256]{2,1,0:T(8,128)S(1)}) custom-call(s32[19]{0:T(128)S(1)} %concatenate.3.scalars.refs_0_, bf16[128,32,512]{2,1,0:T(8,128)(2,1)} %refs_1_.1, bf16[128,32,256]{2,1,0:T(8,128)(2,1)S(1)} %collective-permute-done.1.f_other.refs_2_, bf16[4,6,32,512]{3,2,1,0:T(8,128)(2,1)S(1)} %all_to_all.20.w_own.refs_3_, ...), custom_call_target="tpu_custom_call" | custom-call | flops 12000000 | bytes 100000 | tf_op jit(solution)/shard_map/pallas_call | solution.py:228
  104.9 5.1 %shard_map.78 = f32[32,1,128]{2,1,0:T(1,128)S(1)} custom-call(s32[19]{0:T(128)S(1)} %concatenate.3.scalars.refs_0_, bf16[128,32,512]{2,1,0:T(8,128)(2,1)S(1)} %copy-done, bf16[128,32,256]{2,1,0:T(8,128)(2,1)S(1)} %collective-permute-done.1.f_other.refs_2_, bf16[4,6,32,512]{3,2,1,0:T(8,128)(2,1)S(1)} %all_to_all.20.w_own.refs_3_, ...), custom_call_target="tpu_custom_call" | custom-call | flops 4000000 | bytes 100000 | tf_op jit(solution)/shard_map/pallas_call | solution.py:248
  110.0 20.2 %all_to_all.21 = f32[32,1,128]{2,1,0:T(1,128)S(1)} all-to-all(f32[32,1,128]{2,1,0:T(1,128)S(1)} %shard_map.78), channel_id=1, replica_groups=mesh['x'=4,'ylo'=4,'yhi'=2,'z'=8,'core'=2] {'yhi','z','core'}, dimensions={0} | all-to-all | bytes 32768 | tf_op jit(solution)/shard_map/all_to_all | solution.py:266
  130.2 1.9 %collective-permute-start.12 = (f32[1,128]{1,0:T(1,128)S(1)}, f32[1,128]{1,0:T(1,128)S(1)}, u32[]{:S(2)}, u32[]{:S(2)}) collective-permute-start(f32[1,128]{1,0:T(1,128)S(1)} %bitcast.36), channel_id=1, source_target_pairs={{0,0},{1,1},{2,32},{3,33},{4,64},{5,65},{6,96},{7,97},{8,128},{9,1... | collective-permute-start | bytes 1544 | tf_op jit(solution)/shard_map/ppermute | solution.py:273
  132.9 13.6 %collective-permute-done.12 = f32[1,128]{1,0:T(1,128)S(1)} collective-permute-done((f32[1,128]{1,0:T(1,128)S(1)}, f32[1,128]{1,0:T(1,128)S(1)}, u32[]{:S(2)}, u32[]{:S(2)}) %collective-permute-start.12) | collective-permute-done | bytes 544 | tf_op jit(solution)/shard_map/ppermute | solution.py:273
  (39 shorter events, 2.0 us)
Async XLA Ops:
  2.1 30.6 %all-to-all-start = ((bf16[32,16,256]{2,1,0:T(8,128)(2,1)}), bf16[32,16,256]{2,1,0:T(8,128)(2,1)S(1)}, u32[]{:S(2)}, u32[]{:S(2)}) async-start(bf16[32,16,256]{2,1,0:T(8,128)(2,1)} %bitcast.3), calls=%async_computation | async-start | bytes 524288 | tf_op jit(solution)/shard_map/all_to_all | solution.py:182
  19.4 14.3 %copy-start.2 = (bf16[6,128,512]{2,0,1:T(8,128)(2,1)}, bf16[6,128,512]{2,0,1:T(8,128)(2,1)S(1)}, u32[]{:S(2)}) copy-start(bf16[6,128,512]{2,0,1:T(8,128)(2,1)S(1)} %slice_bitcast_fusion) | copy-start | bytes 2359300
  20.4 20.0 %collective-permute-start.4 = (bf16[6,32,512]{2,0,1:T(8,128)(2,1)}, bf16[6,32,512]{2,0,1:T(8,128)(2,1)}, u32[]{:S(2)}, u32[]{:S(2)}) collective-permute-start(bf16[6,32,512]{2,0,1:T(8,128)(2,1)} %get-tuple-element.23), channel_id=1, source_target_pairs={{0,384},{1,385},{2,386},{3,387},{4,388},{5,389},{6,390},{7,391},{8... | collective-permute-start | bytes 589832 | tf_op jit(solution)/shard_map/ppermute | solution.py:43
  21.7 18.7 %collective-permute-start.3 = (bf16[6,32,512]{2,0,1:T(8,128)(2,1)}, bf16[6,32,512]{2,0,1:T(8,128)(2,1)}, u32[]{:S(2)}, u32[]{:S(2)}) collective-permute-start(bf16[6,32,512]{2,0,1:T(8,128)(2,1)} %get-tuple-element.24), channel_id=1, source_target_pairs={{0,256},{1,257},{2,258},{3,259},{4,260},{5,261},{6,262},{7,263},{8... | collective-permute-start | bytes 589832 | tf_op jit(solution)/shard_map/ppermute | solution.py:43
  23.0 17.4 %collective-permute-start.2 = (bf16[6,32,512]{2,0,1:T(8,128)(2,1)}, bf16[6,32,512]{2,0,1:T(8,128)(2,1)}, u32[]{:S(2)}, u32[]{:S(2)}) collective-permute-start(bf16[6,32,512]{2,0,1:T(8,128)(2,1)} %get-tuple-element.22), channel_id=1, source_target_pairs={{0,128},{1,129},{2,130},{3,131},{4,132},{5,133},{6,134},{7,135},{8... | collective-permute-start | bytes 589832 | tf_op jit(solution)/shard_map/ppermute | solution.py:43
  33.7 23.7 %all-to-all-start.1 = ((bf16[4,512,256]{2,1,0:T(8,128)(2,1)}), bf16[4,512,256]{2,1,0:T(8,128)(2,1)S(1)}, u32[]{:S(2)}, u32[]{:S(2)}) async-start(bf16[4,512,256]{2,1,0:T(8,128)(2,1)} %broadcast_in_dim.6), calls=%async_computation.1 | async-start | bytes 2097152 | tf_op jit(solution)/shard_map/all_to_all | solution.py:64
  38.5 54.4 %collective-permute-start.1 = (bf16[128,32,256]{2,1,0:T(8,128)(2,1)}, bf16[128,32,256]{2,1,0:T(8,128)(2,1)S(1)}, u32[]{:S(2)}, u32[]{:S(2)}) collective-permute-start(bf16[128,32,256]{2,1,0:T(8,128)(2,1)} %constant_dynamic-slice_fusion.1), channel_id=1, source_target_pairs={{0,1},{1,0},{2,3},{3,2},{4,5},{5,4},{6,7},{7,6},{8,9},{9,8},{10,11... | collective-permute-start | bytes 6291464 | tf_op jit(solution)/shard_map/ppermute | solution.py:32
  42.4 11.8 %collective-permute-start.5 = (bf16[6,32,512]{2,0,1:T(8,128)(2,1)}, bf16[6,32,512]{2,0,1:T(8,128)(2,1)}, u32[]{:S(2)}, u32[]{:S(2)}) collective-permute-start(bf16[6,32,512]{2,0,1:T(8,128)(2,1)} %fusion.3), channel_id=1, source_target_pairs={{0,64},{128,192},{256,320},{384,448},{1,65},{129,193},{257,321},{3... | collective-permute-start | bytes 589832 | tf_op jit(solution)/shard_map/ppermute | solution.py:57
  48.6 8.7 %collective-permute-start = (bf16[6,16]{1,0:T(8,128)(2,1)S(1)}, bf16[6,16]{1,0:T(8,128)(2,1)S(1)}, u32[]{:S(2)}, u32[]{:S(2)}) collective-permute-start(bf16[6,16]{1,0:T(8,128)(2,1)S(1)} %constant_dynamic-slice_fusion), channel_id=1, source_target_pairs={{0,1},{1,0},{2,3},{3,2},{4,5},{5,4},{6,7},{7,6},{8,9},{9,8},{10,11... | collective-permute-start | bytes 584 | tf_op jit(solution)/shard_map/ppermute | solution.py:32
  55.3 9.1 %collective-permute-start.6 = (bf16[6,32,512]{2,0,1:T(8,128)(2,1)S(1)}, bf16[6,32,512]{2,0,1:T(8,128)(2,1)}, u32[]{:S(2)}, u32[]{:S(2)}) collective-permute-start(bf16[6,32,512]{2,0,1:T(8,128)(2,1)S(1)} %add.162), channel_id=1, source_target_pairs={{0,32},{64,96},{128,160},{192,224},{256,288},{320,352},{384,416},{... | collective-permute-start | bytes 589832 | tf_op jit(solution)/shard_map/ppermute | solution.py:57
  57.4 27.9 %collective-permute-start.8 = (bf16[4,512,256]{2,1,0:T(8,128)(2,1)S(1)}, bf16[4,512,256]{2,1,0:T(8,128)(2,1)S(1)}, u32[]{:S(2)}, u32[]{:S(2)}) collective-permute-start(bf16[4,512,256]{2,1,0:T(8,128)(2,1)S(1)} %all-to-all-done.1.refs_0_), channel_id=1, source_target_pairs={{0,32},{32,64},{64,96},{96,16},{16,48},{48,80},{80,112},{112,0},{1... | collective-permute-start | bytes 3145736 | tf_op jit(solution)/shard_map/ppermute | solution.py:28
  59.3 29.9 %collective-permute-start.10 = (bf16[4,512,256]{2,1,0:T(8,128)(2,1)S(1)}, bf16[4,512,256]{2,1,0:T(8,128)(2,1)S(1)}, u32[]{:S(2)}, u32[]{:S(2)}) collective-permute-start(bf16[4,512,256]{2,1,0:T(8,128)(2,1)S(1)} %all-to-all-done.1.refs_0_), channel_id=1, source_target_pairs={{0,112},{32,0},{64,32},{96,64},{16,96},{48,16},{80,48},{112,80},{1... | collective-permute-start | bytes 3145736 | tf_op jit(solution)/shard_map/ppermute | solution.py:28
  79.8 13.1 %collective-permute-start.7 = (bf16[4,6,32,512]{3,2,1,0:T(8,128)(2,1)S(1)}, bf16[4,6,32,512]{3,2,1,0:T(8,128)(2,1)S(1)}, u32[]{:S(2)}, u32[]{:S(2)}) collective-permute-start(bf16[4,6,32,512]{3,2,1,0:T(8,128)(2,1)S(1)} %all_to_all.20.w_own.refs_3_), channel_id=1, source_target_pairs={{0,1},{1,0},{2,3},{3,2},{4,5},{5,4},{6,7},{7,6},{8,9},{9,8},{10,11... | collective-permute-start | bytes 2359304 | tf_op jit(solution)/shard_map/ppermute | solution.py:32
  85.3 19.5 %collective-permute-start.9 = (bf16[2,512,256]{2,1,0:T(8,128)(2,1)S(1)}, bf16[2,512,256]{2,1,0:T(8,128)(2,1)S(1)}, u32[]{:S(2)}, u32[]{:S(2)}) collective-permute-start(bf16[2,512,256]{2,1,0:T(8,128)(2,1)S(1)} %slice.55), channel_id=1, source_target_pairs={{0,32},{32,64},{64,96},{96,16},{16,48},{48,80},{80,112},{112,0},{1... | collective-permute-start | bytes 1572872 | tf_op jit(solution)/shard_map/ppermute | solution.py:28
  89.3 15.5 %copy-start = (bf16[128,32,512]{2,1,0:T(8,128)(2,1)S(1)}, bf16[128,32,512]{2,1,0:T(8,128)(2,1)}, u32[]{:S(2)}) copy-start(bf16[128,32,512]{2,1,0:T(8,128)(2,1)} %refs_1_.1) | copy-start | bytes 12582916
  89.3 15.5 %copy-start.1 = (f32[16,16]{1,0:T(8,128)S(1)}, f32[16,16]{1,0:T(8,128)}, u32[]{:S(2)}) copy-start(f32[16,16]{1,0:T(8,128)} %refs_5_.1) | copy-start | bytes 3076
  89.3 15.5 %collective-permute-start.11 = (bf16[2,512,256]{2,1,0:T(8,128)(2,1)S(1)}, bf16[2,512,256]{2,1,0:T(8,128)(2,1)S(1)}, u32[]{:S(2)}, u32[]{:S(2)}) collective-permute-start(bf16[2,512,256]{2,1,0:T(8,128)(2,1)S(1)} %slice.56), channel_id=1, source_target_pairs={{0,112},{32,0},{64,32},{96,64},{16,96},{48,16},{80,48},{112,80},{1... | collective-permute-start | bytes 1572872 | tf_op jit(solution)/shard_map/ppermute | solution.py:28
  104.8 28.0 %copy-start.4 = (f32[512]{0:T(512)S(1)}, f32[512]{0:T(512)}, u32[]{:S(2)}) copy-start(f32[512]{0:T(512)} %param.10) | copy-start | bytes 6148
  104.9 41.7 %copy-start.3 = (f32[1,6,16]{2,0,1:T(1,128)S(1)}, f32[1,6,16]{2,0,1:T(1,128)}, u32[]{:S(2)}) copy-start(f32[1,6,16]{2,0,1:T(1,128)} %param.9) | copy-start | bytes 1156
  104.9 41.7 %slice-start = ((f32[512]{0:T(512)}), f32[6]{0:T(128)S(1)}, s32[]{:S(2)}) async-start(f32[512]{0:T(512)} %param.10), calls=%async_computation.4 | async-start | bytes 1024 | tf_op jit(solution)/shard_map/slice | solution.py:279
  130.2 16.2 %collective-permute-start.12 = (f32[1,128]{1,0:T(1,128)S(1)}, f32[1,128]{1,0:T(1,128)S(1)}, u32[]{:S(2)}, u32[]{:S(2)}) collective-permute-start(f32[1,128]{1,0:T(1,128)S(1)} %bitcast.36), channel_id=1, source_target_pairs={{0,0},{1,1},{2,32},{3,33},{4,64},{5,65},{6,96},{7,97},{8,128},{9,1... | collective-permute-start | bytes 1544 | tf_op jit(solution)/shard_map/ppermute | solution.py:273
